TPU v7x, 32 devices: a whole 2x2x4 slice. The times are simulated.
32 devices in a mesh: dp: 8 (over z, x), tensor: 4 (over y, core).
Axes of the slice: x: 2, y: 2, z: 4, core: 2. Of those that a mesh axis runs over, the one named last changes fastest.
Arguments:
- layer_input: bfloat16 [1536, 2560], P('dp')
- segment_ids: int32 [1536], P('dp'), may hold values from 0 to 31, as said below
- valid_mask: int32 [1536], P('dp'), may hold values from 0 to 1, as said below
- cotangent: bfloat16 [1536, 2560], P('dp'), may hold values from -8 to 8
- attn_gain: bfloat16 [2560], P('dp'), may hold values from 0.25 to 1.75
- q_down: bfloat16 [2560, 768], P('dp'), may hold values from -0.125 to 0.125
- q_gain: bfloat16 [768], P('dp'), may hold values from 0.25 to 1.75
- q_up: bfloat16 [768, 3840], P('dp', 'tensor'), may hold values from -0.21875 to 0.21875
- kv_down: bfloat16 [2560, 288], P('dp'), may hold values from -0.125 to 0.125
- kv_gain: bfloat16 [256], P('dp'), may hold values from 0.25 to 1.75
- kv_up: bfloat16 [256, 5120], P('dp', 'tensor'), may hold values from -0.375 to 0.375
- o_proj: bfloat16 [2560, 2560], P('tensor', 'dp'), may hold values from -4 to 4
- mlp_gain: bfloat16 [2560], P('dp'), may hold values from 0.25 to 1.75
- w_gate: bfloat16 [2560, 6400], P('dp', 'tensor'), may hold values from -0.125 to 0.125
- w_up: bfloat16 [2560, 6400], P('dp', 'tensor'), may hold values from -0.125 to 0.125
- w_down: bfloat16 [6400, 2560], P('tensor', 'dp'), may hold values from -1.5 to 1.5
Outputs:
- block_out: float32 [1536, 2560], P('dp')
- grad_input: float32 [1536, 2560], P('dp')
- grad_attn_gain: float32 [2560], P('dp')
- grad_q_down: float32 [2560, 768], P('dp')
- grad_q_gain: float32 [768], P('dp')
- grad_q_up: float32 [768, 3840], P('dp', 'tensor')
- grad_kv_down: float32 [2560, 288], P('dp')
- grad_kv_gain: float32 [256], P('dp')
- grad_kv_up: float32 [256, 5120], P('dp', 'tensor')
- grad_o_proj: float32 [2560, 2560], P('tensor', 'dp')
- grad_mlp_gain: float32 [2560], P('dp')
- grad_w_gate: float32 [2560, 6400], P('dp', 'tensor')
- grad_w_up: float32 [2560, 6400], P('dp', 'tensor')
- grad_w_down: float32 [6400, 2560], P('tensor', 'dp')
- rms_stats: float32 [3], replicated
Inputs may be any that keep to these rules, and one draw needn't show every extreme that they name: `segment_ids`: within each sequence of 192 tokens the ids start at 0 and never fall; a document is a run of equal ids, and padding tokens carry the id of their sequence's last document. `valid_mask`: within each sequence the valid tokens are a leading run, followed by padding; the last sequence has no padding.
All inputs are finite; a program needn't handle non-finite values.
Results may differ from a plain program's by a relative error of at most 0.024.
Values may be sent and summed in bfloat16 or wider, within the bound.
A program may use at most 192 MiB of HBM per device.

v0:
```python
import math

import jax
import jax.numpy as jnp
from jax import lax
from jax.sharding import PartitionSpec as P

D = 2560
KR = 256
NOPE = 64
ROPE = 32
VD = 64


NORM_EPS = 1e-05
RESIDUAL_SCALE = 1.4 / math.sqrt(62.0)
ROPE_BASE = 10000.0
NEGATIVE = -1e30


def rope_tables(length, rot_dim):
    half_dim = rot_dim // 2
    position = jnp.arange(length, dtype=jnp.float32)
    frequency = jnp.exp(
        -math.log(ROPE_BASE) * 2.0 * jnp.arange(half_dim, dtype=jnp.float32) / rot_dim
    )
    phases = position[:, None] * frequency[None, :]
    return (jnp.cos(phases), jnp.sin(phases))


def rotate(values, cosine, sine_table):
    half_dim = values.shape[-1] // 2
    first_half = values[..., :half_dim]
    second_half = values[..., half_dim:]
    return jnp.concatenate(
        [
            first_half * cosine - second_half * sine_table,
            second_half * cosine + first_half * sine_table,
        ],
        axis=-1,
    )


def unrotate(grads, cosine, sine_table):
    half_dim = grads.shape[-1] // 2
    first_half = grads[..., :half_dim]
    second_half = grads[..., half_dim:]
    return jnp.concatenate(
        [
            first_half * cosine + second_half * sine_table,
            second_half * cosine - first_half * sine_table,
        ],
        axis=-1,
    )


def inverse_rms(values):
    return lax.rsqrt(jnp.mean(values * values, axis=-1, keepdims=True) + NORM_EPS)


def norm_back(grad_unit, unit, inv_rms):
    return inv_rms * (grad_unit - unit * jnp.mean(grad_unit * unit, axis=-1, keepdims=True))


def attend_forward(query_major, key_major, value_major, allowed):
    inv_root = 1.0 / math.sqrt(query_major.shape[-1])

    def one_head(operands):
        query_head, key_head, value_head = operands
        scores = (
            jnp.einsum("qd,kd->qk", query_head, key_head, preferred_element_type=jnp.float32)
            * inv_root
        )
        scores = jnp.where(allowed, scores, NEGATIVE)
        row_max = jnp.max(scores, axis=-1, keepdims=True)
        weights = jnp.exp(scores - row_max)
        totals = jnp.sum(weights, axis=-1, keepdims=True)
        probs_low = (weights / totals).astype(jnp.bfloat16)
        mixed_head = jnp.dot(probs_low, value_head, preferred_element_type=jnp.float32)
        return (mixed_head, row_max[:, 0] + jnp.log(totals[:, 0]))

    return lax.map(one_head, (query_major, key_major, value_major))


def attend_backward(query_major, key_major, value_major, grad_major, log_norm, allowed):
    inv_root = 1.0 / math.sqrt(query_major.shape[-1])

    def one_head(operands):
        query_head, key_head, value_head, grad_head, norm_head = operands
        scores = (
            jnp.einsum("qd,kd->qk", query_head, key_head, preferred_element_type=jnp.float32)
            * inv_root
        )
        scores = jnp.where(allowed, scores, NEGATIVE)
        probs = jnp.exp(scores - norm_head[:, None])
        probs_low = probs.astype(jnp.bfloat16)
        grad_value = jnp.einsum(
            "qk,qd->kd", probs_low, grad_head, preferred_element_type=jnp.float32
        )
        grad_probs = jnp.einsum(
            "qd,kd->qk", grad_head, value_head, preferred_element_type=jnp.float32
        )
        inner = jnp.sum(probs * grad_probs, axis=-1, keepdims=True)
        grad_scores = (probs * (grad_probs - inner)).astype(jnp.bfloat16)
        grad_query = jnp.dot(grad_scores, key_head, preferred_element_type=jnp.float32) * inv_root
        grad_key = (
            jnp.einsum("qk,qd->kd", grad_scores, query_head, preferred_element_type=jnp.float32)
            * inv_root
        )
        return (grad_query, grad_key, grad_value)

    return lax.map(one_head, (query_major, key_major, value_major, grad_major, log_norm))


def per_device(
    layer_input,
    segment_ids,
    valid_mask,
    cotangent,
    attn_gain,
    q_down,
    q_gain,
    q_up,
    kv_down,
    kv_gain,
    kv_up,
    o_proj,
    mlp_gain,
    w_gate,
    w_up,
    w_down,
):
    length = layer_input.shape[0]
    heads_local = q_up.shape[1] // (NOPE + ROPE)
    share = length // lax.axis_size("tensor")
    begin = lax.axis_index("tensor") * share

    def rows_of(values):
        return lax.dynamic_slice_in_dim(values, begin, share, 0)

    gathered = (
        lax.all_gather(attn_gain, "dp", axis=0, tiled=True),
        lax.all_gather(q_down, "dp", axis=0, tiled=True),
        lax.all_gather(q_gain, "dp", axis=0, tiled=True),
        lax.all_gather(q_up, "dp", axis=0, tiled=True),
        lax.all_gather(kv_down, "dp", axis=0, tiled=True),
        lax.all_gather(kv_gain, "dp", axis=0, tiled=True),
        lax.all_gather(kv_up, "dp", axis=0, tiled=True),
        lax.all_gather(o_proj, "dp", axis=1, tiled=True),
    )
    gain_attn = gathered[0].astype(jnp.float32)
    gain_q = gathered[2].astype(jnp.float32)
    gain_kv = gathered[5].astype(jnp.float32)
    full_q_down, full_q_up, full_kv_down, full_kv_up, full_o_proj = (
        gathered[1],
        gathered[3],
        gathered[4],
        gathered[6],
        gathered[7],
    )
    stream = layer_input.astype(jnp.float32)
    cosine, sine_table = rope_tables(length, ROPE)
    head_cos = cosine[:, None, :]
    head_sin = sine_table[:, None, :]
    inv_one = inverse_rms(stream)
    unit_one = stream * inv_one
    normed = (unit_one * gain_attn).astype(jnp.bfloat16)
    q_latent = jnp.dot(normed, full_q_down, preferred_element_type=jnp.float32)
    inv_q = inverse_rms(q_latent)
    unit_q = q_latent * inv_q
    q_normed = (unit_q * gain_q).astype(jnp.bfloat16)
    q_heads = jnp.dot(q_normed, full_q_up, preferred_element_type=jnp.float32).reshape(
        length, heads_local, NOPE + ROPE
    )
    kv_joint = jnp.dot(normed, full_kv_down, preferred_element_type=jnp.float32)
    kv_latent = kv_joint[:, :KR]
    inv_kv = inverse_rms(kv_latent)
    unit_kv = kv_latent * inv_kv
    kv_normed = (unit_kv * gain_kv).astype(jnp.bfloat16)
    kv_heads = jnp.dot(kv_normed, full_kv_up, preferred_element_type=jnp.float32).reshape(
        length, heads_local, NOPE + VD
    )
    queries = jnp.concatenate(
        [q_heads[..., :NOPE], rotate(q_heads[..., NOPE:], head_cos, head_sin)], axis=-1
    ).astype(jnp.bfloat16)
    key_rot = rotate(kv_joint[:, KR:], cosine, sine_table)
    key_rows = jnp.concatenate(
        [kv_heads[..., :NOPE], jnp.broadcast_to(key_rot[:, None, :], (length, heads_local, ROPE))],
        axis=-1,
    ).astype(jnp.bfloat16)
    value_rows = kv_heads[..., NOPE:].astype(jnp.bfloat16)
    position = jnp.arange(length)
    allowed = (
        (segment_ids[:, None] == segment_ids[None, :])
        & (position[None, :] <= position[:, None])
        & ((valid_mask[None, :] == 1) | (position[None, :] == position[:, None]))
    )
    query_major = queries.transpose(1, 0, 2)
    key_major = key_rows.transpose(1, 0, 2)
    value_major = value_rows.transpose(1, 0, 2)
    mixed_heads, log_norm = attend_forward(query_major, key_major, value_major, allowed)
    mixed = mixed_heads.transpose(1, 0, 2).reshape(length, heads_local * VD).astype(jnp.bfloat16)
    attn_part = jnp.dot(mixed, full_o_proj, preferred_element_type=jnp.float32)
    mlp_pack = (
        lax.all_gather(mlp_gain, "dp", axis=0, tiled=True),
        lax.all_gather(w_gate, "dp", axis=0, tiled=True),
        lax.all_gather(w_up, "dp", axis=0, tiled=True),
        lax.all_gather(w_down, "dp", axis=1, tiled=True),
    )
    gain_mlp = mlp_pack[0].astype(jnp.float32)
    attn_out = lax.psum(attn_part, "tensor")
    resid = stream + RESIDUAL_SCALE * attn_out
    inv_two = inverse_rms(resid)
    unit_two = resid * inv_two
    normed_two = (unit_two * gain_mlp).astype(jnp.bfloat16)
    attn_rows = rows_of(RESIDUAL_SCALE * attn_out)
    resid_rows = rows_of(resid)
    gate = jnp.dot(normed_two, mlp_pack[1], preferred_element_type=jnp.float32)
    upper = jnp.dot(normed_two, mlp_pack[2], preferred_element_type=jnp.float32)
    sigma = jax.nn.sigmoid(gate)
    swish = gate * sigma
    hidden = (swish * upper).astype(jnp.bfloat16)
    mlp_part = jnp.dot(hidden, mlp_pack[3], preferred_element_type=jnp.float32)
    mlp_out = lax.psum(mlp_part.astype(jnp.bfloat16), "tensor").astype(jnp.float32)
    block_full = resid + RESIDUAL_SCALE * mlp_out
    mlp_rows = rows_of(RESIDUAL_SCALE * mlp_out)
    weight_rows = rows_of(valid_mask.astype(jnp.float32)[:, None])
    stat_sums = lax.psum(
        (
            jnp.sum(weight_rows * resid_rows * resid_rows),
            jnp.sum(weight_rows * attn_rows * attn_rows),
            jnp.sum(weight_rows * mlp_rows * mlp_rows),
            jnp.sum(weight_rows),
        ),
        ("dp", "tensor"),
    )
    total_cells = stat_sums[3] * D
    rms_stats = jnp.sqrt(jnp.stack([stat_sums[0], stat_sums[1], stat_sums[2]]) / total_cells)
    back_all = (
        lax.all_gather(q_down, "dp", axis=0, tiled=True),
        lax.all_gather(q_up, "dp", axis=0, tiled=True),
        lax.all_gather(kv_down, "dp", axis=0, tiled=True),
        lax.all_gather(kv_up, "dp", axis=0, tiled=True),
        lax.all_gather(o_proj, "dp", axis=1, tiled=True),
        lax.all_gather(w_gate, "dp", axis=0, tiled=True),
        lax.all_gather(w_up, "dp", axis=0, tiled=True),
        lax.all_gather(w_down, "dp", axis=1, tiled=True),
    )
    back_attn = back_all[:5]
    back_mlp = back_all[5:]
    grad_out = cotangent.astype(jnp.float32)
    grad_mlp = (RESIDUAL_SCALE * grad_out).astype(jnp.bfloat16)
    grad_w_down = jnp.einsum("tf,td->fd", hidden, grad_mlp, preferred_element_type=jnp.float32)
    grad_hidden = jnp.einsum("td,fd->tf", grad_mlp, back_mlp[2], preferred_element_type=jnp.float32)
    grad_gate = (grad_hidden * upper * (sigma * (1.0 + gate * (1.0 - sigma)))).astype(jnp.bfloat16)
    grad_upper = (grad_hidden * swish).astype(jnp.bfloat16)
    grad_w_gate = jnp.einsum("td,tf->df", normed_two, grad_gate, preferred_element_type=jnp.float32)
    grad_w_up = jnp.einsum("td,tf->df", normed_two, grad_upper, preferred_element_type=jnp.float32)
    normed_two_part = jnp.einsum(
        "tf,df->td", grad_gate, back_mlp[0], preferred_element_type=jnp.float32
    ) + jnp.einsum("tf,df->td", grad_upper, back_mlp[1], preferred_element_type=jnp.float32)
    grad_normed_two = lax.psum(normed_two_part, "tensor")
    grad_mlp_gain = jnp.sum(grad_normed_two * unit_two, axis=0)
    grad_resid = grad_out + norm_back(grad_normed_two * gain_mlp, unit_two, inv_two)
    grad_attn = (RESIDUAL_SCALE * grad_resid).astype(jnp.bfloat16)
    grad_o_proj = jnp.einsum("tv,td->vd", mixed, grad_attn, preferred_element_type=jnp.float32)
    grad_mixed = jnp.einsum(
        "td,vd->tv", grad_attn, back_attn[4], preferred_element_type=jnp.float32
    ).astype(jnp.bfloat16)
    grad_major = grad_mixed.reshape(length, heads_local, VD).transpose(1, 0, 2)
    grad_q_major, grad_k_major, grad_v_major = attend_backward(
        query_major, key_major, value_major, grad_major, log_norm, allowed
    )
    grad_queries = grad_q_major.transpose(1, 0, 2)
    grad_keys = grad_k_major.transpose(1, 0, 2)
    grad_values = grad_v_major.transpose(1, 0, 2)
    grad_q_heads = (
        jnp.concatenate(
            [grad_queries[..., :NOPE], unrotate(grad_queries[..., NOPE:], head_cos, head_sin)],
            axis=-1,
        )
        .reshape(length, heads_local * (NOPE + ROPE))
        .astype(jnp.bfloat16)
    )
    grad_kv_heads = (
        jnp.concatenate([grad_keys[..., :NOPE], grad_values], axis=-1)
        .reshape(length, heads_local * (NOPE + VD))
        .astype(jnp.bfloat16)
    )
    grad_key_rot = unrotate(jnp.sum(grad_keys[..., NOPE:], axis=1), cosine, sine_table)
    grad_q_up = jnp.einsum("tr,tc->rc", q_normed, grad_q_heads, preferred_element_type=jnp.float32)
    grad_kv_up = jnp.einsum(
        "tr,tc->rc", kv_normed, grad_kv_heads, preferred_element_type=jnp.float32
    )
    grad_q_normed, grad_kv_normed, grad_kv_rot = (
        lax.psum(
            jnp.einsum(
                "tc,rc->tr", grad_q_heads, back_attn[1], preferred_element_type=jnp.float32
            ).astype(jnp.bfloat16),
            "tensor",
        ).astype(jnp.float32),
        lax.psum(
            jnp.einsum(
                "tc,rc->tr", grad_kv_heads, back_attn[3], preferred_element_type=jnp.float32
            ).astype(jnp.bfloat16),
            "tensor",
        ).astype(jnp.float32),
        lax.psum(grad_key_rot.astype(jnp.bfloat16), "tensor").astype(jnp.float32),
    )
    grad_q_gain = jnp.sum(grad_q_normed * unit_q, axis=0)
    grad_kv_gain = jnp.sum(grad_kv_normed * unit_kv, axis=0)
    grad_q_latent = norm_back(grad_q_normed * gain_q, unit_q, inv_q).astype(jnp.bfloat16)
    grad_kv_joint = jnp.concatenate(
        [norm_back(grad_kv_normed * gain_kv, unit_kv, inv_kv), grad_kv_rot], axis=-1
    ).astype(jnp.bfloat16)
    grad_q_down = jnp.einsum("td,tr->dr", normed, grad_q_latent, preferred_element_type=jnp.float32)
    grad_kv_down = jnp.einsum(
        "td,tr->dr", normed, grad_kv_joint, preferred_element_type=jnp.float32
    )
    grad_normed = jnp.einsum(
        "tr,dr->td", grad_q_latent, back_attn[0], preferred_element_type=jnp.float32
    ) + jnp.einsum("tr,dr->td", grad_kv_joint, back_attn[2], preferred_element_type=jnp.float32)
    grad_attn_gain = jnp.sum(grad_normed * unit_one, axis=0)
    grad_input = grad_resid + norm_back(grad_normed * gain_attn, unit_one, inv_one)
    all_shards = (
        lax.psum_scatter(
            grad_attn_gain.astype(jnp.bfloat16), "dp", scatter_dimension=0, tiled=True
        ).astype(jnp.float32),
        lax.psum_scatter(
            grad_q_down.astype(jnp.bfloat16), "dp", scatter_dimension=0, tiled=True
        ).astype(jnp.float32),
        lax.psum_scatter(
            grad_q_gain.astype(jnp.bfloat16), "dp", scatter_dimension=0, tiled=True
        ).astype(jnp.float32),
        lax.psum_scatter(
            grad_q_up.astype(jnp.bfloat16), "dp", scatter_dimension=0, tiled=True
        ).astype(jnp.float32),
        lax.psum_scatter(
            grad_kv_down.astype(jnp.bfloat16), "dp", scatter_dimension=0, tiled=True
        ).astype(jnp.float32),
        lax.psum_scatter(
            grad_kv_gain.astype(jnp.bfloat16), "dp", scatter_dimension=0, tiled=True
        ).astype(jnp.float32),
        lax.psum_scatter(
            grad_kv_up.astype(jnp.bfloat16), "dp", scatter_dimension=0, tiled=True
        ).astype(jnp.float32),
        lax.psum_scatter(
            grad_o_proj.astype(jnp.bfloat16), "dp", scatter_dimension=1, tiled=True
        ).astype(jnp.float32),
        lax.psum_scatter(
            grad_mlp_gain.astype(jnp.bfloat16), "dp", scatter_dimension=0, tiled=True
        ).astype(jnp.float32),
        lax.psum_scatter(
            grad_w_gate.astype(jnp.bfloat16), "dp", scatter_dimension=0, tiled=True
        ).astype(jnp.float32),
        lax.psum_scatter(
            grad_w_up.astype(jnp.bfloat16), "dp", scatter_dimension=0, tiled=True
        ).astype(jnp.float32),
        lax.psum_scatter(
            grad_w_down.astype(jnp.bfloat16), "dp", scatter_dimension=1, tiled=True
        ).astype(jnp.float32),
    )
    return (
        block_full,
        grad_input,
        all_shards[0],
        all_shards[1],
        all_shards[2],
        all_shards[3],
        all_shards[4],
        all_shards[5],
        all_shards[6],
        all_shards[7],
        all_shards[8],
        all_shards[9],
        all_shards[10],
        all_shards[11],
        rms_stats,
    )


def solution(mesh):
    placed = (
        P("dp", None),
        P("dp"),
        P("dp"),
        P("dp", None),
        P("dp"),
        P("dp", None),
        P("dp"),
        P("dp", "tensor"),
        P("dp", None),
        P("dp"),
        P("dp", "tensor"),
        P("tensor", "dp"),
        P("dp"),
        P("dp", "tensor"),
        P("dp", "tensor"),
        P("tensor", "dp"),
    )
    return jax.shard_map(
        per_device,
        mesh=mesh,
        in_specs=placed,
        out_specs=(
            P("dp", None),
            P("dp", None),
            P("dp"),
            P("dp", None),
            P("dp"),
            P("dp", "tensor"),
            P("dp", None),
            P("dp"),
            P("dp", "tensor"),
            P("tensor", "dp"),
            P("dp"),
            P("dp", "tensor"),
            P("dp", "tensor"),
            P("tensor", "dp"),
            P(),
        ),
        check_vma=False,
    )
```

profile of v0, /device:TPU:1, one launch (start us, length us, event | category | flops | bytes accessed | tf_op | source)
XLA Modules:
  0.0 1712.7 jit_solution(12870119952922842517)
XLA Ops:
  16.8 31.5 %all-reduce.10 = (bf16[2560]{0:T(1024)(128)(2,1)S(1)}, bf16[768]{0:T(1024)(128)(2,1)S(1)}, bf16[256]{0:T(256)(128)(2,1)S(1)}, bf16[2560]{0:T(1024)(128)(2,1)S(1)}) all-reduce(bf16[2560]{0:T(1024)(128)(2,1)S(1)} %dynamic-update-slice, bf16[768]{0:T(1024)(128)(2,1)S(1)} %dynamic-update-slice.1, ...), channel_id=1, replica_groups=mesh['dp'=8,'tensor'=4] {'dp'}, use_global_device_ids=true, to_apply=%add | all-reduce | flops 6144 | bytes 24576
  48.8 25.9 %all_gather.50 = bf16[256,1280]{1,0:T(8,128)(2,1)S(1)} all-gather(bf16[32,1280]{1,0:T(8,128)(2,1)S(1)} %copy-done.27), channel_id=1, replica_groups=mesh['dp'=8,'tensor'=4] {'dp'}, dimensions={0}, use_global_device_ids=true | all-gather | bytes 737280 | tf_op jit(solution)/shard_map/all_gather | solution.py:148
  84.3 47.5 %all-gather.9.cloned.1.call-done = bf16[2560,768]{1,0:T(8,128)(2,1)} async-done(((bf16[320,768]{1,0:T(8,128)(2,1)}), bf16[2560,768]{1,0:T(8,128)(2,1)}) %all-gather.9.cloned.1.call-update) | async-done | bytes 3932176 | tf_op jit(solution)/shard_map/all_gather | solution.py:143
  135.1 42.0 %all-gather.11.cloned.1.call-done = bf16[768,960]{1,0:T(8,128)(2,1)} async-done(((bf16[96,960]{1,0:T(8,128)(2,1)}), bf16[768,960]{1,0:T(8,128)(2,1)}) %all-gather.11.cloned.1.call-update) | async-done | bytes 1474576 | tf_op jit(solution)/shard_map/all_gather | solution.py:145
  179.9 26.3 %while.28 = (s32[]{:T(128)}, bf16[10,192,64]{1,2,0:T(8,128)(2,1)S(1)}, f32[10,192]{1,0:T(8,128)}, bf16[10,192,96]{2,1,0:T(8,128)(2,1)S(1)}, bf16[10,192,96]{2,1,...) while((s32[]{:T(128)}, ...), condition=%wide.region_6.7_spmd.clone, body=%wide.region_3.6_spmd.clone.sunk | while | flops 12312386 | bytes 717417 | solution.py:82
  206.2 33.4 %all-gather.13.cloned.1.call-done = bf16[640,2560]{0,1:T(8,128)(2,1)} async-done(((bf16[640,320]{0,1:T(8,128)(2,1)}), bf16[640,2560]{0,1:T(8,128)(2,1)}) %all-gather.13.cloned.1.call-update) | async-done | bytes 3276816 | tf_op jit(solution)/shard_map/all_gather | solution.py:149
  246.5 46.5 %all-reduce.16.cloned.1.call-done = f32[192,2560]{1,0:T(8,128)} async-done(((f32[192,2560]{1,0:T(8,128)}), f32[192,2560]{1,0:T(8,128)}) %all-reduce.16.cloned.1.call-update) | async-done | bytes 1966096 | tf_op jit(solution)/shard_map/psum | solution.py:211
  297.3 124.1 %all-gather.15.cloned.1.call-done = bf16[2560,1600]{1,0:T(8,128)(2,1)} async-done(((bf16[320,1600]{1,0:T(8,128)(2,1)}), bf16[2560,1600]{1,0:T(8,128)(2,1)}) %all-gather.15.cloned.1.call-update) | async-done | bytes 8192016 | tf_op jit(solution)/shard_map/all_gather | solution.py:206
  428.1 120.3 %all-gather.17.cloned.1.call-done = bf16[2560,1600]{1,0:T(8,128)(2,1)} async-done(((bf16[320,1600]{1,0:T(8,128)(2,1)}), bf16[2560,1600]{1,0:T(8,128)(2,1)}) %all-gather.17.cloned.1.call-update) | async-done | bytes 8192016 | tf_op jit(solution)/shard_map/all_gather | solution.py:207
  555.2 120.3 %all-gather.19.cloned.1.call-done = bf16[1600,2560]{0,1:T(8,128)(2,1)} async-done(((bf16[1600,320]{0,1:T(8,128)(2,1)}), bf16[1600,2560]{0,1:T(8,128)(2,1)}) %all-gather.19.cloned.1.call-update) | async-done | bytes 8192016 | tf_op jit(solution)/shard_map/all_gather | solution.py:208
  694.2 7.5 convolution_convert_fusion.6
  701.8 40.1 %all-reduce.18.cloned.1.call-done = f32[192,2560]{1,0:T(8,128)} async-done(((f32[192,2560]{1,0:T(8,128)}), f32[192,2560]{1,0:T(8,128)}) %all-reduce.18.cloned.1.call-update) | async-done | bytes 1966096 | tf_op jit(solution)/shard_map/psum | solution.py:262
  750.0 71.9 %while.29 = (s32[]{:T(128)}, f32[10,192,96]{1,2,0:T(8,128)}, f32[10,192,96]{1,2,0:T(8,128)}, bf16[10,192,64]{1,2,0:T(8,128)(2,1)}, bf16[10,192,96]{2,1,0:T(8,128...) while((s32[]{:T(128)}, f32[10,192,96]{1,2,0:T(8,128)}, ...), condition=%wide.region_14.15_spmd.clone, body=%wide.region_12.14_spmd.clone.sunk | while | flops 31260480 | bytes 2329721 | solution.py:112
  838.3 12.9 psum.75
  851.2 18.6 %all-reduce.20.cloned.1.call-done = (bf16[192,2560]{1,0:T(8,128)(2,1)}, bf16[192,768]{1,0:T(8,128)(2,1)}, bf16[192,256]{1,0:T(8,128)(2,1)}) async-done(((bf16[192,2560]{1,0:T(8,128)(2,1)}, bf16[192,768]{1,0:T(8,128)(2,1)}, bf16[192,256]{1,0:T(8,128)(2,1)}), (bf16[192,2560]{1,0:T(8,128)(2,1)}, bf16[192,768]{1,0:T(8,128)(2,1)}, bf16[192,256]{1,0:T(8,128)(2,1)})) %all-reduce.20.cloned.1.call-update) | async-done | bytes 1376272 | tf_op jit(solution)/shard_map/psum | solution.py:224
  906.3 7.3 convolution_convert_fusion
  921.6 40.1 %all-reduce.8 = (f32[1]{0:T(128)}, f32[1]{0:T(128)}, f32[1]{0:T(128)}, f32[]{:T(128)}) all-reduce(f32[1]{0:T(128)} %bitcast.21, f32[1]{0:T(128)} %bitcast.20, f32[1]{0:T(128)} %bitcast.19, f32[]{:T(128)} %get-tuple-element.279), channel_id=1, replica_groups=mesh['dp'=8,'tensor'=4] {'dp','tensor'}, use_global_device_ids=true, to_apply=%region_43.44 | all-reduce | flops 4 | bytes 32 | tf_op jit(solution)/shard_map/psum | solution.py:228
  968.3 29.0 %all-reduce.9 = (bf16[2560]{0:T(1024)(128)(2,1)S(1)}, bf16[768]{0:T(1024)(128)(2,1)S(1)}, bf16[256]{0:T(256)(128)(2,1)S(1)}, bf16[2560]{0:T(1024)(128)(2,1)S(1)}) all-reduce(bf16[2560]{0:T(1024)(128)(2,1)S(1)} %get-tuple-element.217, bf16[768]{0:T(1024)(128)(2,1)S(1)} %copy-done.35, ...), channel_id=2, replica_groups=mesh['dp'=8,'tensor'=4] {'dp'}, use_global_device_ids=true, to_apply=%region_23.24.clone | all-reduce | flops 6144 | bytes 24576
  1008.2 64.3 %reduce-scatter.25.cloned.1.call-done = bf16[320,288]{1,0:T(8,128)(2,1)} async-done(((bf16[2560,288]{1,0:T(8,128)(2,1)}), bf16[320,288]{1,0:T(8,128)(2,1)}) %reduce-scatter.25.cloned.1.call-update) | async-done | bytes 184336
  1074.4 77.9 %reduce-scatter.17.cloned.1.call-done = bf16[640,320]{0,1:T(8,128)(2,1)} async-done(((bf16[640,2560]{0,1:T(8,128)(2,1)}), bf16[640,320]{0,1:T(8,128)(2,1)}) %reduce-scatter.17.cloned.1.call-update) | async-done | bytes 409616 | tf_op jit(solution)/shard_map/reduce_scatter | solution.py:347
  1154.3 85.7 %reduce-scatter.11.cloned.1.call-done = bf16[320,768]{1,0:T(8,128)(2,1)} async-done(((bf16[2560,768]{1,0:T(8,128)(2,1)}), bf16[320,768]{1,0:T(8,128)(2,1)}) %reduce-scatter.11.cloned.1.call-update) | async-done | bytes 491536 | tf_op jit(solution)/shard_map/reduce_scatter | solution.py:329
  1242.0 152.7 %reduce-scatter.19.cloned.1.call-done = bf16[320,1600]{1,0:T(8,128)(2,1)} async-done(((bf16[2560,1600]{1,0:T(8,128)(2,1)}), bf16[320,1600]{1,0:T(8,128)(2,1)}) %reduce-scatter.19.cloned.1.call-update) | async-done | bytes 1024016 | tf_op jit(solution)/shard_map/reduce_scatter | solution.py:353
  1397.4 151.5 %reduce-scatter.21.cloned.1.call-done = bf16[320,1600]{1,0:T(8,128)(2,1)} async-done(((bf16[2560,1600]{1,0:T(8,128)(2,1)}), bf16[320,1600]{1,0:T(8,128)(2,1)}) %reduce-scatter.21.cloned.1.call-update) | async-done | bytes 1024016 | tf_op jit(solution)/shard_map/reduce_scatter | solution.py:356
  1551.6 151.1 %reduce-scatter.23.cloned.1.call-done = bf16[1600,320]{0,1:T(8,128)(2,1)} async-done(((bf16[1600,2560]{0,1:T(8,128)(2,1)}), bf16[1600,320]{0,1:T(8,128)(2,1)}) %reduce-scatter.23.cloned.1.call-update) | async-done | bytes 1024016 | tf_op jit(solution)/shard_map/reduce_scatter | solution.py:359
  (378 shorter events, 261.8 us)
Async XLA Ops:
  7.2 67.6 %copy-start.38 = (s32[192]{0:T(256)S(1)}, s32[192]{0:T(256)}, u32[]{:S(2)}) copy-start(s32[192]{0:T(256)} %param.22) | copy-start | bytes 2308
  7.2 67.6 %all-gather.21.cloned.1.call-start = ((), (), s32[]{:S(2)}) async-start(), calls=%async_computation.23 | async-start | bytes 1990656 | tf_op jit(solution)/shard_map/all_gather | solution.py:146
  7.9 123.9 %all-gather.9.cloned.1.call-start = ((), (), s32[]{:S(2)}) async-start(), calls=%async_computation.8 | async-start | bytes 4423680 | tf_op jit(solution)/shard_map/all_gather | solution.py:143
  8.7 168.4 %all-gather.11.cloned.1.call-start = ((), (), s32[]{:S(2)}) async-start(), calls=%async_computation.9 | async-start | bytes 1769472 | tf_op jit(solution)/shard_map/all_gather | solution.py:145
  9.4 230.2 %all-gather.13.cloned.1.call-start = ((), (), s32[]{:S(2)}) async-start(), calls=%async_computation.10 | async-start | bytes 3686400 | tf_op jit(solution)/shard_map/all_gather | solution.py:149
  10.0 282.9 %all-reduce.16.cloned.1.call-start = ((), (), s32[]{:S(2)}) async-start(), calls=%async_computation.11 | async-start | bytes 3932160 | tf_op jit(solution)/shard_map/psum | solution.py:211
  10.1 72.7 %copy-start.36 = (f32[16]{0:T(128)}, f32[16]{0:T(128)S(1)}, u32[]{:S(2)}) copy-start(f32[16]{0:T(128)S(1)} %multiply_exponential_fusion) | copy-start | bytes 196
  48.6 83.2 %copy-start.32 = (f32[192]{0:T(256)}, f32[192]{0:T(256)S(1)}, u32[]{:S(2)}) copy-start(f32[192]{0:T(256)S(1)} %add_rsqrt_fusion.3) | copy-start | bytes 2308
  135.0 44.3 %copy-start.4 = (f32[192,768]{1,0:T(8,128)}, f32[192,768]{1,0:T(8,128)S(1)}, u32[]{:S(2)}) copy-start(f32[192,768]{1,0:T(8,128)S(1)} %get-tuple-element.312) | copy-start | bytes 1769476
  135.1 44.3 %copy-start.28 = (f32[192]{0:T(256)}, f32[192]{0:T(256)S(1)}, u32[]{:S(2)}) copy-start(f32[192]{0:T(256)S(1)} %add_rsqrt_fusion.2) | copy-start | bytes 2308
  244.2 177.2 %all-gather.15.cloned.1.call-start = ((), (), s32[]{:S(2)}) async-start(), calls=%async_computation.12 | async-start | bytes 9584640 | tf_op jit(solution)/shard_map/all_gather | solution.py:206
  244.8 303.7 %all-gather.17.cloned.1.call-start = ((), (), s32[]{:S(2)}) async-start(), calls=%async_computation.13 | async-start | bytes 9584640 | tf_op jit(solution)/shard_map/all_gather | solution.py:207
  245.5 429.9 %all-gather.19.cloned.1.call-start = ((), (), s32[]{:S(2)}) async-start(), calls=%async_computation.14 | async-start | bytes 9584640 | tf_op jit(solution)/shard_map/all_gather | solution.py:208
  246.3 495.6 %all-reduce.18.cloned.1.call-start = ((), (), s32[]{:S(2)}) async-start(), calls=%async_computation.15 | async-start | bytes 3932160 | tf_op jit(solution)/shard_map/psum | solution.py:262
  694.0 175.8 %all-reduce.20.cloned.1.call-start = ((), (), s32[]{:S(2)}) async-start(), calls=%async_computation.25 | async-start | bytes 2752512 | tf_op jit(solution)/shard_map/psum | solution.py:224
  828.8 176.1 %reduce-scatter.15.cloned.1.call-start = ((), (), s32[]{:S(2)}) async-start(), calls=%async_computation.18 | async-start | bytes 737280 | tf_op jit(solution)/shard_map/reduce_scatter | solution.py:344
  831.4 175.1 %reduce-scatter.13.cloned.1.call-start = ((), (), s32[]{:S(2)}) async-start(), calls=%async_computation.17 | async-start | bytes 1769472 | tf_op jit(solution)/shard_map/reduce_scatter | solution.py:335
  834.4 238.1 %reduce-scatter.25.cloned.1.call-start = ((), (), s32[]{:S(2)}) async-start(), calls=%async_computation.24 | async-start | bytes 2211840
  879.6 272.7 %reduce-scatter.17.cloned.1.call-start = ((), (), s32[]{:S(2)}) async-start(), calls=%async_computation.19 | async-start | bytes 3686400 | tf_op jit(solution)/shard_map/reduce_scatter | solution.py:347
  884.3 355.7 %reduce-scatter.11.cloned.1.call-start = ((), (), s32[]{:S(2)}) async-start(), calls=%async_computation.16 | async-start | bytes 4423680 | tf_op jit(solution)/shard_map/reduce_scatter | solution.py:329
  891.3 503.4 %reduce-scatter.19.cloned.1.call-start = ((), (), s32[]{:S(2)}) async-start(), calls=%async_computation.20 | async-start | bytes 9584640 | tf_op jit(solution)/shard_map/reduce_scatter | solution.py:353
  898.9 650.0 %reduce-scatter.21.cloned.1.call-start = ((), (), s32[]{:S(2)}) async-start(), calls=%async_computation.21 | async-start | bytes 9584640 | tf_op jit(solution)/shard_map/reduce_scatter | solution.py:356
  906.3 796.4 %reduce-scatter.23.cloned.1.call-start = ((), (), s32[]{:S(2)}) async-start(), calls=%async_computation.22 | async-start | bytes 9584640 | tf_op jit(solution)/shard_map/reduce_scatter | solution.py:359
  916.9 45.4 %copy-start.19 = (bf16[192,768]{1,0:T(8,128)(2,1)S(1)}, bf16[192,768]{1,0:T(8,128)(2,1)}, u32[]{:S(2)}) copy-start(bf16[192,768]{1,0:T(8,128)(2,1)} %copy-done.18) | copy-start | bytes 884740
  (35 other events, 346.4 us)
Sparse Core Ops, SparseCore 0:
  10.2 50.0 all-gather.20
  62.5 69.2 all-gather.8
  134.0 43.0 all-gather.10
  179.1 60.4 all-gather.12
  244.3 48.6 all-reduce.15
  295.0 126.3 all-gather.14
  423.6 124.8 all-gather.16
  550.6 124.8 all-gather.18
  694.1 47.7 all-reduce.17
  828.9 40.8 all-reduce.19
  874.0 60.2 reduce-scatter.14
  938.2 64.7 reduce-scatter.12
  1007.4 65.1 reduce-scatter.24
  1076.0 76.3 reduce-scatter.16
  1156.3 83.6 reduce-scatter.10
  1243.4 151.2 reduce-scatter.18
  1398.6 150.2 reduce-scatter.20
  1552.3 150.2 reduce-scatter.22
where the time goes:
time: 1730 us; the launch traced here: 1710 us
  waiting for transfers between devices  1280 us (74%)
  matrix products  166 us (10%)
  blocking collectives  139 us (8%)
  local copies, waits for them, and re-layouts  56 us (3%)
  other arithmetic  48.4 us (3%)
  between operations  20 us (1%)
    reduce_scatter x1, waiting for transfers between devices, per_device(): lax.psum_scatter(grad_w_gate.astype(jnp.bfloat16), 'dp', scatter_dimensio...  153 us
    reduce_scatter x1, waiting for transfers between devices, per_device(): lax.psum_scatter(grad_w_up.astype(jnp.bfloat16), 'dp', scatter_dimension=...  151 us
    reduce_scatter x1, waiting for transfers between devices, per_device(): lax.psum_scatter(grad_w_down.astype(jnp.bfloat16), 'dp', scatter_dimensio...  151 us
    all_gather x1, waiting for transfers between devices, per_device(): lax.all_gather(w_gate, 'dp', axis=0, tiled=True)  124 us
    all_gather x1, waiting for transfers between devices, per_device(): lax.all_gather(w_up, 'dp', axis=0, tiled=True)  120 us
    all_gather x1, waiting for transfers between devices, per_device(): lax.all_gather(w_down, 'dp', axis=1, tiled=True)  120 us
    reduce_scatter x1, waiting for transfers between devices, per_device(): lax.psum_scatter(grad_q_down.astype(jnp.bfloat16), 'dp', scatter_dimensio...  85.7 us
    reduce_scatter x1, waiting for transfers between devices, per_device(): lax.psum_scatter(grad_o_proj.astype(jnp.bfloat16), 'dp', scatter_dimensio...  77.9 us
  transfers between devices with their start and end apart: 18, of which 15 were waited for; matrix products, arithmetic and copies ran while one was open for 9% of the time, Pallas kernels for 0%

commit v1 on v0

v1 whole, which is shorter than its diff:
```python
import math

import jax
import jax.numpy as jnp
from jax import lax
from jax.sharding import PartitionSpec as P

D = 2560
KR = 256
NOPE = 64
ROPE = 32
VD = 64


NORM_EPS = 1e-05
RESIDUAL_SCALE = 1.4 / math.sqrt(62.0)
ROPE_BASE = 10000.0
NEGATIVE = -1e30


def rope_tables(length, rot_dim):
    half_dim = rot_dim // 2
    position = jnp.arange(length, dtype=jnp.float32)
    frequency = jnp.exp(
        -math.log(ROPE_BASE) * 2.0 * jnp.arange(half_dim, dtype=jnp.float32) / rot_dim
    )
    phases = position[:, None] * frequency[None, :]
    return (jnp.cos(phases), jnp.sin(phases))


def rotate(values, cosine, sine_table):
    half_dim = values.shape[-1] // 2
    first_half = values[..., :half_dim]
    second_half = values[..., half_dim:]
    return jnp.concatenate(
        [
            first_half * cosine - second_half * sine_table,
            second_half * cosine + first_half * sine_table,
        ],
        axis=-1,
    )


def unrotate(grads, cosine, sine_table):
    half_dim = grads.shape[-1] // 2
    first_half = grads[..., :half_dim]
    second_half = grads[..., half_dim:]
    return jnp.concatenate(
        [
            first_half * cosine + second_half * sine_table,
            second_half * cosine - first_half * sine_table,
        ],
        axis=-1,
    )


def inverse_rms(values):
    return lax.rsqrt(jnp.mean(values * values, axis=-1, keepdims=True) + NORM_EPS)


def norm_back(grad_unit, unit, inv_rms):
    return inv_rms * (grad_unit - unit * jnp.mean(grad_unit * unit, axis=-1, keepdims=True))


def attend_forward(query_major, key_major, value_major, allowed):
    inv_root = 1.0 / math.sqrt(query_major.shape[-1])

    def one_head(operands):
        query_head, key_head, value_head = operands
        scores = (
            jnp.einsum("qd,kd->qk", query_head, key_head, preferred_element_type=jnp.float32)
            * inv_root
        )
        scores = jnp.where(allowed, scores, NEGATIVE)
        row_max = jnp.max(scores, axis=-1, keepdims=True)
        weights = jnp.exp(scores - row_max)
        totals = jnp.sum(weights, axis=-1, keepdims=True)
        probs_low = (weights / totals).astype(jnp.bfloat16)
        mixed_head = jnp.dot(probs_low, value_head, preferred_element_type=jnp.float32)
        return (mixed_head, row_max[:, 0] + jnp.log(totals[:, 0]))

    return lax.map(one_head, (query_major, key_major, value_major))


def attend_backward(query_major, key_major, value_major, grad_major, log_norm, allowed):
    inv_root = 1.0 / math.sqrt(query_major.shape[-1])

    def one_head(operands):
        query_head, key_head, value_head, grad_head, norm_head = operands
        scores = (
            jnp.einsum("qd,kd->qk", query_head, key_head, preferred_element_type=jnp.float32)
            * inv_root
        )
        scores = jnp.where(allowed, scores, NEGATIVE)
        probs = jnp.exp(scores - norm_head[:, None])
        probs_low = probs.astype(jnp.bfloat16)
        grad_value = jnp.einsum(
            "qk,qd->kd", probs_low, grad_head, preferred_element_type=jnp.float32
        )
        grad_probs = jnp.einsum(
            "qd,kd->qk", grad_head, value_head, preferred_element_type=jnp.float32
        )
        inner = jnp.sum(probs * grad_probs, axis=-1, keepdims=True)
        grad_scores = (probs * (grad_probs - inner)).astype(jnp.bfloat16)
        grad_query = jnp.dot(grad_scores, key_head, preferred_element_type=jnp.float32) * inv_root
        grad_key = (
            jnp.einsum("qk,qd->kd", grad_scores, query_head, preferred_element_type=jnp.float32)
            * inv_root
        )
        return (grad_query, grad_key, grad_value)

    return lax.map(one_head, (query_major, key_major, value_major, grad_major, log_norm))


BF = jnp.bfloat16
F32 = jnp.float32
EVERY = ("dp", "tensor")


def dot(left, right):
    return jnp.dot(left, right, preferred_element_type=F32)


def dot_nt(left, right):
    return jnp.einsum("ac,bc->ab", left, right, preferred_element_type=F32)


def dot_tn(left, right):
    return jnp.einsum("ca,cb->ab", left, right, preferred_element_type=F32)


def gather_dp(block):
    return lax.all_gather(block, "dp", axis=0, tiled=True)


def gather_tensor(block):
    return lax.all_gather(block, "tensor", axis=0, tiled=True)


def gather_every(block):
    return lax.all_gather(block, EVERY, axis=0, tiled=True)


def scatter_dp(part):
    return lax.psum_scatter(part, "dp", scatter_dimension=0, tiled=True).astype(F32)


def scatter_tensor(part):
    return lax.psum_scatter(part, "tensor", scatter_dimension=0, tiled=True).astype(F32)


def scatter_every(part):
    return lax.psum_scatter(part, EVERY, scatter_dimension=0, tiled=True).astype(F32)


def swap_dp(blocks):
    return lax.all_to_all(blocks, "dp", 0, 0, tiled=True)


def per_device(
    layer_input,
    segment_ids,
    valid_mask,
    cotangent,
    attn_gain,
    q_down,
    q_gain,
    q_up,
    kv_down,
    kv_gain,
    kv_up,
    o_proj,
    mlp_gain,
    w_gate,
    w_up,
    w_down,
):
    length = layer_input.shape[0]
    heads_local = q_up.shape[1] // (NOPE + ROPE)
    n_dp = lax.axis_size("dp")
    n_tensor = lax.axis_size("tensor")
    share = length // n_tensor
    me = lax.axis_index("tensor")
    width = w_gate.shape[0]
    slice_ff = w_gate.shape[1] // n_dp
    rows_down = width // n_tensor

    def rows_of(values, count):
        return lax.dynamic_slice_in_dim(values, me * count, count, 0)

    full_q_down = gather_every(rows_of(q_down, rows_down))
    full_kv_down = gather_every(rows_of(kv_down, rows_down))
    full_q_up = gather_dp(q_up)
    full_kv_up = gather_dp(kv_up)
    gain_attn = gather_dp(attn_gain).astype(F32)
    gain_q = gather_dp(q_gain).astype(F32)
    gain_kv = gather_dp(kv_gain).astype(F32)
    gain_mlp = gather_dp(mlp_gain).astype(F32)
    full_o = gather_dp(o_proj.T)

    packed = jnp.concatenate(
        [
            w_gate.reshape(width, n_dp, slice_ff),
            w_up.reshape(width, n_dp, slice_ff),
            w_down.T.reshape(width, n_dp, slice_ff),
        ],
        axis=2,
    ).transpose(1, 0, 2)
    mine = swap_dp(packed).reshape(n_dp * width, 3 * slice_ff)
    w_in = mine[:, : 2 * slice_ff]
    w_out = mine[:, 2 * slice_ff :]

    stream = layer_input.astype(F32)
    cosine, sine_table = rope_tables(length, ROPE)
    head_cos = cosine[:, None, :]
    head_sin = sine_table[:, None, :]
    inv_one = inverse_rms(stream)
    unit_one = stream * inv_one
    normed = (unit_one * gain_attn).astype(BF)
    q_latent = dot(normed, full_q_down)
    inv_q = inverse_rms(q_latent)
    unit_q = q_latent * inv_q
    q_normed = (unit_q * gain_q).astype(BF)
    q_heads = dot(q_normed, full_q_up).reshape(length, heads_local, NOPE + ROPE)
    kv_joint = dot(normed, full_kv_down)
    kv_latent = kv_joint[:, :KR]
    inv_kv = inverse_rms(kv_latent)
    unit_kv = kv_latent * inv_kv
    kv_normed = (unit_kv * gain_kv).astype(BF)
    kv_heads = dot(kv_normed, full_kv_up).reshape(length, heads_local, NOPE + VD)
    queries = jnp.concatenate(
        [q_heads[..., :NOPE], rotate(q_heads[..., NOPE:], head_cos, head_sin)], axis=-1
    ).astype(BF)
    key_rot = rotate(kv_joint[:, KR:], cosine, sine_table)
    key_rows = jnp.concatenate(
        [kv_heads[..., :NOPE], jnp.broadcast_to(key_rot[:, None, :], (length, heads_local, ROPE))],
        axis=-1,
    ).astype(BF)
    value_rows = kv_heads[..., NOPE:].astype(BF)
    position = jnp.arange(length)
    allowed = (
        (segment_ids[:, None] == segment_ids[None, :])
        & (position[None, :] <= position[:, None])
        & ((valid_mask[None, :] == 1) | (position[None, :] == position[:, None]))
    )
    query_major = queries.transpose(1, 0, 2)
    key_major = key_rows.transpose(1, 0, 2)
    value_major = value_rows.transpose(1, 0, 2)
    mixed_heads, log_norm = attend_forward(query_major, key_major, value_major, allowed)
    mixed = mixed_heads.transpose(1, 0, 2).reshape(length, heads_local * VD).astype(BF)
    attn_part = dot_nt(mixed, full_o)

    attn_rows = RESIDUAL_SCALE * scatter_tensor(attn_part.astype(BF))
    resid_rows = rows_of(layer_input, share).astype(F32) + attn_rows
    inv_two = inverse_rms(resid_rows)
    unit_two = resid_rows * inv_two
    normed_two = gather_every((unit_two * gain_mlp).astype(BF))
    cot_rows = rows_of(cotangent, share)
    grad_mlp = (RESIDUAL_SCALE * gather_every(cot_rows).astype(F32)).astype(BF)

    gate_upper = dot(normed_two, w_in)
    gate = gate_upper[:, :slice_ff]
    upper = gate_upper[:, slice_ff:]
    sigma = jax.nn.sigmoid(gate)
    swish = gate * sigma
    hidden = (swish * upper).astype(BF)
    mlp_rows = RESIDUAL_SCALE * scatter_every(dot_nt(hidden, w_out).astype(BF))
    grad_hidden = dot(grad_mlp, w_out)
    grad_both = jnp.concatenate(
        [
            grad_hidden * upper * (sigma * (1.0 + gate * (1.0 - sigma))),
            grad_hidden * swish,
        ],
        axis=1,
    ).astype(BF)
    grad_normed_two = scatter_every(dot_nt(grad_both, w_in).astype(BF))
    grad_packed = jnp.concatenate(
        [dot_tn(normed_two, grad_both), dot_tn(grad_mlp, hidden)], axis=1
    ).astype(BF)
    swapped = swap_dp(grad_packed.reshape(n_dp, width, 3 * slice_ff))

    def unpack(part):
        return part.transpose(1, 0, 2).reshape(width, n_dp * slice_ff).astype(F32)

    grad_w_gate = unpack(swapped[:, :, :slice_ff])
    grad_w_up = unpack(swapped[:, :, slice_ff : 2 * slice_ff])
    grad_w_down = unpack(swapped[:, :, 2 * slice_ff :]).T

    block_rows = resid_rows + mlp_rows
    block_full = gather_tensor(block_rows)
    weight_rows = rows_of(valid_mask.astype(F32)[:, None], share)
    grad_mlp_gain = jnp.sum(grad_normed_two * unit_two, axis=0)
    grad_resid_rows = cot_rows.astype(F32) + norm_back(
        grad_normed_two * gain_mlp, unit_two, inv_two
    )
    grad_attn = gather_tensor((RESIDUAL_SCALE * grad_resid_rows).astype(BF))

    grad_o = dot_tn(grad_attn, mixed)
    grad_mixed = dot(grad_attn, full_o).astype(BF)
    grad_major = grad_mixed.reshape(length, heads_local, VD).transpose(1, 0, 2)
    grad_q_major, grad_k_major, grad_v_major = attend_backward(
        query_major, key_major, value_major, grad_major, log_norm, allowed
    )
    grad_queries = grad_q_major.transpose(1, 0, 2)
    grad_keys = grad_k_major.transpose(1, 0, 2)
    grad_values = grad_v_major.transpose(1, 0, 2)
    grad_q_heads = (
        jnp.concatenate(
            [grad_queries[..., :NOPE], unrotate(grad_queries[..., NOPE:], head_cos, head_sin)],
            axis=-1,
        )
        .reshape(length, heads_local * (NOPE + ROPE))
        .astype(BF)
    )
    grad_kv_heads = (
        jnp.concatenate([grad_keys[..., :NOPE], grad_values], axis=-1)
        .reshape(length, heads_local * (NOPE + VD))
        .astype(BF)
    )
    grad_key_rot = unrotate(jnp.sum(grad_keys[..., NOPE:], axis=1), cosine, sine_table)
    grad_q_up = dot_tn(q_normed, grad_q_heads)
    grad_kv_up = dot_tn(kv_normed, grad_kv_heads)
    grad_latents = lax.psum(
        jnp.concatenate(
            [
                dot_nt(grad_q_heads, full_q_up),
                dot_nt(grad_kv_heads, full_kv_up),
                grad_key_rot,
            ],
            axis=1,
        ).astype(BF),
        "tensor",
    ).astype(F32)
    rank_q = q_latent.shape[1]
    grad_q_normed = grad_latents[:, :rank_q]
    grad_kv_normed = grad_latents[:, rank_q : rank_q + KR]
    grad_kv_rot = grad_latents[:, rank_q + KR :]
    grad_q_gain = jnp.sum(grad_q_normed * unit_q, axis=0)
    grad_kv_gain = jnp.sum(grad_kv_normed * unit_kv, axis=0)
    grad_q_latent = norm_back(grad_q_normed * gain_q, unit_q, inv_q).astype(BF)
    grad_kv_joint = jnp.concatenate(
        [norm_back(grad_kv_normed * gain_kv, unit_kv, inv_kv), grad_kv_rot], axis=-1
    ).astype(BF)
    grad_normed = dot_nt(grad_q_latent, full_q_down) + dot_nt(grad_kv_joint, full_kv_down)
    grad_attn_gain = jnp.sum(grad_normed * unit_one, axis=0)
    grad_input = grad_attn.astype(F32) * (1.0 / RESIDUAL_SCALE) + norm_back(
        grad_normed * gain_attn, unit_one, inv_one
    )

    quarter = lax.dynamic_index_in_dim(
        normed.reshape(length, n_dp, n_tensor, rows_down), me, 2, keepdims=False
    ).reshape(length, n_dp * rows_down)
    grad_q_down = gather_tensor(scatter_dp(dot_tn(quarter, grad_q_latent).astype(BF)).astype(BF))
    grad_kv_down = gather_tensor(scatter_dp(dot_tn(quarter, grad_kv_joint).astype(BF)).astype(BF))

    stat_sums = lax.psum(
        (
            jnp.sum(weight_rows * resid_rows * resid_rows),
            jnp.sum(weight_rows * attn_rows * attn_rows),
            jnp.sum(weight_rows * mlp_rows * mlp_rows),
            jnp.sum(weight_rows),
        ),
        EVERY,
    )
    rms_stats = jnp.sqrt(jnp.stack(stat_sums[:3]) / (stat_sums[3] * D))
    return (
        block_full,
        grad_input,
        scatter_dp(grad_attn_gain),
        grad_q_down.astype(F32),
        scatter_dp(grad_q_gain),
        scatter_dp(grad_q_up.astype(BF)),
        grad_kv_down.astype(F32),
        scatter_dp(grad_kv_gain),
        scatter_dp(grad_kv_up.astype(BF)),
        scatter_dp(grad_o.astype(BF)).T,
        scatter_dp(lax.psum(grad_mlp_gain, "tensor")),
        grad_w_gate,
        grad_w_up,
        grad_w_down,
        rms_stats,
    )


def solution(mesh):
    placed = (
        P("dp", None),
        P("dp"),
        P("dp"),
        P("dp", None),
        P("dp"),
        P("dp", None),
        P("dp"),
        P("dp", "tensor"),
        P("dp", None),
        P("dp"),
        P("dp", "tensor"),
        P("tensor", "dp"),
        P("dp"),
        P("dp", "tensor"),
        P("dp", "tensor"),
        P("tensor", "dp"),
    )
    return jax.shard_map(
        per_device,
        mesh=mesh,
        in_specs=placed,
        out_specs=(
            P("dp", None),
            P("dp", None),
            P("dp"),
            P("dp", None),
            P("dp"),
            P("dp", "tensor"),
            P("dp", None),
            P("dp"),
            P("dp", "tensor"),
            P("tensor", "dp"),
            P("dp"),
            P("dp", "tensor"),
            P("dp", "tensor"),
            P("tensor", "dp"),
            P(),
        ),
        check_vma=False,
    )
```

time: 1730 us -> 1280 us (0.74)
  waiting for transfers between devices: 1280 us -> 640 us
  blocking collectives: 139 us -> 278 us
  local copies, waits for them, and re-layouts: 56 us -> 105 us
    all_gather x7, waiting for transfers between devices: 488 us -> 156 us  [the longest x4 96.8 us: gather_every(): return lax.all_gather(block, EVERY, axis=0, tiled=True)]
    reduce_scatter x7 -> x8, waiting for transfers between devices: 619 us -> 382 us  [the longest x2 236 us: scatter_every(): lax.psum_scatter(part, EVERY, scatter_dimension=0, tiled=True).astype(F32)]
    all_to_all x0 -> x1, blocking collectives: none -> 109 us  [swap_dp(): return lax.all_to_all(blocks, 'dp', 0, 0, tiled=True)]
    psum x3 -> x1, waiting for transfers between devices: 105 us -> 27 us  [per_device(): lax.psum(jnp.concatenate([dot_nt(grad_q_heads, full_q_up), dot_nt(grad_kv...]
    all_to_all x0 -> x1, waiting for transfers between devices: none -> 73.6 us  [swap_dp(): return lax.all_to_all(blocks, 'dp', 0, 0, tiled=True)]
    unnamed x19 -> x16, waiting for transfers between devices: 69 us -> 1.94 us
    all_gather x1 -> x4, blocking collectives: 25.9 us -> 53.8 us  [the longest x1 27.9 us: gather_dp(): return lax.all_gather(block, 'dp', axis=0, tiled=True)]
    convert_element_type x1 -> x6, local copies, waits for them, and re-layouts: 0.91 us -> 19.6 us  [the longest x4 17.2 us: unpack(): return part.transpose(1, 0, 2).reshape(width, n_dp * slice_ff).astype(F32)]
  transfers between devices with their start and end apart: 18 -> 17, of which waited for: 15 -> 11; matrix products, arithmetic and copies ran while one was open for 9% -> 15% of each run, Pallas kernels for 0% -> 0%
where the time goes in v1:
time: 1280 us; the launch traced here: 1270 us
  waiting for transfers between devices  640 us (50%)
  blocking collectives  278 us (22%)
  matrix products  163 us (13%)
  local copies, waits for them, and re-layouts  105 us (8%)
  other arithmetic  45.6 us (4%)
  between operations  19.4 us (2%)
  starting transfers between devices  18.2 us (1%)
    reduce_scatter x2, waiting for transfers between devices, scatter_every(): lax.psum_scatter(part, EVERY, scatter_dimension=0, tiled=True).astype(F32)  236 us
    reduce_scatter x5, waiting for transfers between devices, scatter_dp(): lax.psum_scatter(part, 'dp', scatter_dimension=0, tiled=True).astype(F32)  123 us
    all_to_all x1, blocking collectives, swap_dp(): return lax.all_to_all(blocks, 'dp', 0, 0, tiled=True)  109 us
    all_gather x4, waiting for transfers between devices, gather_every(): return lax.all_gather(block, EVERY, axis=0, tiled=True)  96.8 us
    all_to_all x1, waiting for transfers between devices, swap_dp(): return lax.all_to_all(blocks, 'dp', 0, 0, tiled=True)  73.6 us
    unnamed x2, blocking collectives  59.9 us
    all_gather x2, waiting for transfers between devices, gather_dp(): return lax.all_gather(block, 'dp', axis=0, tiled=True)  58.8 us
    psum x1, blocking collectives, per_device(): lax.psum((jnp.sum(weight_rows * resid_rows * resid_rows), jnp.sum(weight_...  40.5 us
  transfers between devices with their start and end apart: 17, of which 11 were waited for; matrix products, arithmetic and copies ran while one was open for 15% of the time, Pallas kernels for 0%

profile of v1, /device:TPU:1, one launch (start us, length us, event | category | flops | bytes accessed | tf_op | source)
XLA Modules:
  0.0 1270.0 jit_solution(2189441297101710147)
XLA Ops:
  17.1 31.1 %all-reduce.10 = (bf16[2560]{0:T(1024)(128)(2,1)S(1)}, bf16[768]{0:T(1024)(128)(2,1)S(1)}, bf16[256]{0:T(256)(128)(2,1)S(1)}, bf16[2560]{0:T(1024)(128)(2,1)S(1)}) all-reduce(bf16[2560]{0:T(1024)(128)(2,1)S(1)} %dynamic-update-slice, bf16[768]{0:T(1024)(128)(2,1)S(1)} %dynamic-update-slice.1, ...), channel_id=1, replica_groups=mesh['dp'=8,'tensor'=4] {'dp'}, use_global_device_ids=true, to_apply=%add | all-reduce | flops 6144 | bytes 24576
  48.4 27.9 %all_gather.51 = bf16[256,1280]{1,0:T(8,128)(2,1)} all-gather(bf16[32,1280]{1,0:T(8,128)(2,1)S(1)} %copy-done.22), channel_id=1, replica_groups=mesh['dp'=8,'tensor'=4] {'dp'}, dimensions={0}, use_global_device_ids=true | all-gather | bytes 737280 | tf_op jit(solution)/shard_map/all_gather | solution.py:133
  85.2 51.4 %all-gather.8.cloned.1.call-done = bf16[2560,768]{1,0:T(8,128)(2,1)} async-done(((bf16[80,768]{1,0:T(8,128)(2,1)}), bf16[2560,768]{1,0:T(8,128)(2,1)}) %all-gather.8.cloned.1.call-update) | async-done | bytes 3932176 | tf_op jit(solution)/shard_map/all_gather | solution.py:141
  139.8 40.9 %all-gather.10.cloned.1.call-done = bf16[768,960]{1,0:T(8,128)(2,1)} async-done(((bf16[96,960]{1,0:T(8,128)(2,1)}), bf16[768,960]{1,0:T(8,128)(2,1)}) %all-gather.10.cloned.1.call-update) | async-done | bytes 1474576 | tf_op jit(solution)/shard_map/all_gather | solution.py:133
  184.8 40.5 %while.28 = (s32[]{:T(128)}, bf16[10,192,64]{1,2,0:T(8,128)(2,1)}, f32[10,192]{1,0:T(8,128)}, bf16[10,192,96]{2,1,0:T(8,128)(2,1)}, bf16[10,192,96]{2,1,0:T(8,12...) while((s32[]{:T(128)}, bf16[10,192,64]{1,2,0:T(8,128)(2,1)}, ...), condition=%wide.region_6.7_spmd.clone, body=%wide.region_3.6_spmd.clone.sunk | while | flops 12312386 | bytes 667761 | solution.py:82
  225.3 17.9 %all-gather.14.cloned.1.call-done = bf16[2560,640]{1,0:T(8,128)(2,1)} async-done(((bf16[320,640]{1,0:T(8,128)(2,1)}), bf16[2560,640]{1,0:T(8,128)(2,1)}) %all-gather.14.cloned.1.call-update) | async-done | bytes 3276816 | tf_op jit(solution)/shard_map/all_gather | solution.py:133
  247.7 24.0 %reduce-scatter.9.cloned.1.call-done = bf16[48,2560]{1,0:T(8,128)(2,1)} async-done(((bf16[192,2560]{1,0:T(8,128)(2,1)}), bf16[48,2560]{1,0:T(8,128)(2,1)}) %reduce-scatter.9.cloned.1.call-update) | async-done | bytes 245776 | tf_op jit(solution)/shard_map/reduce_scatter | solution.py:149
  276.4 11.5 reduce-scatter.13.cloned.1.call-start
  303.9 109.3 %all_to_all.10 = bf16[8,320,600]{2,1,0:T(8,128)(2,1)} all-to-all(bf16[8,320,600]{2,1,0:T(8,128)(2,1)S(1)} %copy.97), channel_id=1, replica_groups=mesh['dp'=8,'tensor'=4] {'dp'}, dimensions={0} | all-to-all | bytes 6144000 | tf_op jit(solution)/shard_map/all_to_all | solution.py:157
  413.2 8.8 fusion.58
  422.0 45.3 %all-gather.20.cloned.1.call-done = bf16[1536,2560]{1,0:T(8,128)(2,1)} async-done(((bf16[48,2560]{1,0:T(8,128)(2,1)}), bf16[1536,2560]{1,0:T(8,128)(2,1)}) %all-gather.20.cloned.1.call-update) | async-done | bytes 7864336 | tf_op jit(solution)/shard_map/all_gather | solution.py:141
  467.3 8.4 multiply_convert_fusion.7
  492.3 110.2 %reduce-scatter.13.cloned.1.call-done = bf16[48,2560]{1,0:T(8,128)(2,1)} async-done(((bf16[1536,2560]{1,0:T(8,128)(2,1)}), bf16[48,2560]{1,0:T(8,128)(2,1)}) %reduce-scatter.13.cloned.1.call-update) | async-done | bytes 245776 | tf_op jit(solution)/shard_map/reduce_scatter | solution.py:153
  604.4 125.4 %reduce-scatter.11.cloned.1.call-done = bf16[48,2560]{1,0:T(8,128)(2,1)} async-done(((bf16[1536,2560]{1,0:T(8,128)(2,1)}), bf16[48,2560]{1,0:T(8,128)(2,1)}) %reduce-scatter.11.cloned.1.call-update) | async-done | bytes 245776 | tf_op jit(solution)/shard_map/reduce_scatter | solution.py:153
  732.6 12.2 all_gather.57
  750.3 71.8 %while.29 = (s32[]{:T(128)}, f32[10,192,96]{1,2,0:T(8,128)}, f32[10,192,96]{1,2,0:T(8,128)}, bf16[10,192,64]{1,2,0:T(8,128)(2,1)}, bf16[10,192,96]{2,1,0:T(8,128...) while((s32[]{:T(128)}, f32[10,192,96]{1,2,0:T(8,128)}, ...), condition=%wide.region_14.15_spmd.clone, body=%wide.region_12.14_spmd.clone.sunk | while | flops 31260480 | bytes 2328205 | solution.py:112
  839.5 27.0 %all-reduce.13.cloned.1.call-done = bf16[192,1056]{1,0:T(8,128)(2,1)} async-done(((bf16[192,1056]{1,0:T(8,128)(2,1)}), bf16[192,1056]{1,0:T(8,128)(2,1)}) %all-reduce.13.cloned.1.call-update) | async-done | bytes 405520 | tf_op jit(solution)/shard_map/psum | solution.py:323
  887.0 8.3 convolution_convert_fusion.3
  914.9 73.6 %all-to-all-done.1 = bf16[8,320,600]{2,1,0:T(8,128)(2,1)} async-done(((bf16[8,320,600]{2,1,0:T(8,128)(2,1)}), bf16[8,320,600]{2,1,0:T(8,128)(2,1)}, u32[]{:S(2)}, u32[]{:S(2)}) %all-to-all-start.1) | async-done | bytes 3072032 | tf_op jit(solution)/shard_map/all_to_all | solution.py:157
  1018.2 40.5 %all-reduce.8 = (f32[1]{0:T(128)}, f32[1]{0:T(128)}, f32[1]{0:T(128)}, f32[]{:T(128)}) all-reduce(f32[1]{0:T(128)} %bitcast.33, f32[1]{0:T(128)} %bitcast.32, f32[1]{0:T(128)} %bitcast.31, f32[]{:T(128)} %get-tuple-element.335), channel_id=1, replica_groups=mesh['dp'=8,'tensor'=4] {'dp','tensor'}, use_global_device_ids=true, to_apply=%region_39.40 | all-reduce | flops 4 | bytes 32 | tf_op jit(solution)/shard_map/psum | solution.py:356
  1068.0 28.8 %all-reduce.9 = (f32[2560]{0:T(1024)S(1)}, f32[768]{0:T(1024)S(1)}, f32[256]{0:T(256)S(1)}, f32[2560]{0:T(1024)S(1)}) all-reduce(f32[2560]{0:T(1024)S(1)} %get-tuple-element.275, f32[768]{0:T(1024)S(1)} %get-tuple-element.277, f32[256]{0:T(256)S(1)} %copy-done.34, ...), channel_id=5, replica_groups=mesh['dp'=8,'tensor'=4] {'dp'}, use_global_device_ids=true, to_apply=%region_21.22.clone | all-reduce | flops 6144 | bytes 49152
  1098.7 14.6 %psum.48 = f32[320]{0:T(512)} all-reduce(f32[320]{0:T(512)S(1)} %dynamic-slice.12), channel_id=1, replica_groups=mesh['dp'=8,'tensor'=4] {'tensor'}, use_global_device_ids=true, to_apply=%region_32.33 | all-reduce | flops 320 | bytes 2560 | tf_op jit(solution)/shard_map/psum | solution.py:377
  1134.0 44.7 %reduce-scatter.17.cloned.1.call-done = bf16[96,960]{1,0:T(8,128)(2,1)} async-done(((bf16[768,960]{1,0:T(8,128)(2,1)}), bf16[96,960]{1,0:T(8,128)(2,1)}) %reduce-scatter.17.cloned.1.call-update) | async-done | bytes 184336 | tf_op jit(solution)/shard_map/reduce_scatter | solution.py:145
  1180.4 78.0 %reduce-scatter.23.cloned.1.call-done = bf16[320,640]{1,0:T(8,128)(2,1)} async-done(((bf16[2560,640]{1,0:T(8,128)(2,1)}), bf16[320,640]{1,0:T(8,128)(2,1)}) %reduce-scatter.23.cloned.1.call-update) | async-done | bytes 409616 | tf_op jit(solution)/shard_map/reduce_scatter | solution.py:145
  (400 shorter events, 310.3 us)
Async XLA Ops:
  7.2 41.2 %copy-start.22 = (bf16[32,1280]{1,0:T(8,128)(2,1)S(1)}, bf16[32,1280]{1,0:T(8,128)(2,1)}, u32[]{:S(2)}) copy-start(bf16[32,1280]{1,0:T(8,128)(2,1)} %param.30) | copy-start | bytes 245764
  7.3 69.4 %all-gather.12.cloned.1.call-start = ((), (), s32[]{:S(2)}) async-start(), calls=%async_computation.12 | async-start | bytes 2027520 | tf_op jit(solution)/shard_map/all_gather | solution.py:141
  9.2 127.5 %all-gather.8.cloned.1.call-start = ((), (), s32[]{:S(2)}) async-start(), calls=%async_computation.10 | async-start | bytes 4055040 | tf_op jit(solution)/shard_map/all_gather | solution.py:141
  9.9 170.8 %all-gather.10.cloned.1.call-start = ((), (), s32[]{:S(2)}) async-start(), calls=%async_computation.11 | async-start | bytes 1769472 | tf_op jit(solution)/shard_map/all_gather | solution.py:133
  10.7 232.6 %all-gather.14.cloned.1.call-start = ((), (), s32[]{:S(2)}) async-start(), calls=%async_computation.13 | async-start | bytes 3686400 | tf_op jit(solution)/shard_map/all_gather | solution.py:133
  11.2 260.5 %reduce-scatter.9.cloned.1.call-start = ((), (), s32[]{:S(2)}) async-start(), calls=%async_computation.14 | async-start | bytes 1228800 | tf_op jit(solution)/shard_map/reduce_scatter | solution.py:149
  11.3 72.6 %copy-start.32 = (f32[16]{0:T(128)}, f32[16]{0:T(128)S(1)}, u32[]{:S(2)}) copy-start(f32[16]{0:T(128)S(1)} %multiply_exponential_fusion) | copy-start | bytes 196
  16.1 62.8 %copy-start.28 = (f32[192]{0:T(256)}, f32[192]{0:T(256)S(1)}, u32[]{:S(2)}) copy-start(f32[192]{0:T(256)S(1)} %add_rsqrt_fusion.2) | copy-start | bytes 2308
  48.4 134.5 %copy-start.21 = (f32[192,16]{0,1:T(8,128)}, f32[192,16]{0,1:T(8,128)S(1)}, u32[]{:S(2)}) copy-start(f32[192,16]{0,1:T(8,128)S(1)} %get-tuple-element.367) | copy-start | bytes 36868
  139.8 43.2 %copy-start.24 = (f32[192]{0:T(256)}, f32[192]{0:T(256)S(1)}, u32[]{:S(2)}) copy-start(f32[192]{0:T(256)S(1)} %add_rsqrt_fusion.1) | copy-start | bytes 2308
  247.6 165.6 %all-gather.16.cloned.1.call-start = ((), (), s32[]{:S(2)}) async-start(), calls=%async_computation.15 | async-start | bytes 8110080 | tf_op jit(solution)/shard_map/all_gather | solution.py:141
  274.6 192.7 %all-gather.20.cloned.1.call-start = ((), (), s32[]{:S(2)}) async-start(), calls=%async_computation.18 | async-start | bytes 8110080 | tf_op jit(solution)/shard_map/all_gather | solution.py:141
  276.4 326.1 %reduce-scatter.13.cloned.1.call-start = ((), (), s32[]{:S(2)}) async-start(), calls=%async_computation.19 | async-start | bytes 8110080 | tf_op jit(solution)/shard_map/reduce_scatter | solution.py:153
  483.4 246.3 %reduce-scatter.11.cloned.1.call-start = ((), (), s32[]{:S(2)}) async-start(), calls=%async_computation.16 | async-start | bytes 8110080 | tf_op jit(solution)/shard_map/reduce_scatter | solution.py:153
  490.9 111.5 %copy-start.9 = (bf16[48,2560]{1,0:T(8,128)(2,1)S(1)}, bf16[48,2560]{1,0:T(8,128)(2,1)}, u32[]{:S(2)}) copy-start(bf16[48,2560]{1,0:T(8,128)(2,1)} %reduce-scatter.9.cloned.1.call-done) | copy-start | bytes 737284
  491.0 375.5 %all-reduce.13.cloned.1.call-start = ((), (), s32[]{:S(2)}) async-start(), calls=%async_computation.20 | async-start | bytes 884736 | tf_op jit(solution)/shard_map/psum | solution.py:323
  836.3 280.5 %reduce-scatter.19.cloned.1.call-start = ((), (), s32[]{:S(2)}) async-start(), calls=%async_computation.23 | async-start | bytes 552960 | tf_op jit(solution)/shard_map/reduce_scatter | solution.py:145
  870.3 253.8 %reduce-scatter.21.cloned.1.call-start = ((), (), s32[]{:S(2)}) async-start(), calls=%async_computation.24 | async-start | bytes 737280 | tf_op jit(solution)/shard_map/reduce_scatter | solution.py:145
  872.8 252.8 %reduce-scatter.15.cloned.1.call-start = ((), (), s32[]{:S(2)}) async-start(), calls=%async_computation.21 | async-start | bytes 1105920 | tf_op jit(solution)/shard_map/reduce_scatter | solution.py:145
  876.9 257.1 %all-gather.18.cloned.1.call-start = ((), (), s32[]{:S(2)}) async-start(), calls=%async_computation.17 | async-start | bytes 2457600 | tf_op jit(solution)/shard_map/all_gather | solution.py:137
  877.5 301.2 %reduce-scatter.17.cloned.1.call-start = ((), (), s32[]{:S(2)}) async-start(), calls=%async_computation.22 | async-start | bytes 1769472 | tf_op jit(solution)/shard_map/reduce_scatter | solution.py:145
  903.8 84.6 %all-to-all-start.1 = ((bf16[8,320,600]{2,1,0:T(8,128)(2,1)}), bf16[8,320,600]{2,1,0:T(8,128)(2,1)}, u32[]{:S(2)}, u32[]{:S(2)}) async-start(bf16[8,320,600]{2,1,0:T(8,128)(2,1)} %pad_maximum_fusion), calls=%async_computation.9 | async-start | bytes 6553600 | tf_op jit(solution)/shard_map/all_to_all | solution.py:157
  909.7 348.6 %reduce-scatter.23.cloned.1.call-start = ((), (), s32[]{:S(2)}) async-start(), calls=%async_computation.25 | async-start | bytes 3686400 | tf_op jit(solution)/shard_map/reduce_scatter | solution.py:145
  1014.4 47.6 %copy-start.11 = (bf16[192,768]{1,0:T(8,128)(2,1)S(1)}, bf16[192,768]{1,0:T(8,128)(2,1)}, u32[]{:S(2)}) copy-start(bf16[192,768]{1,0:T(8,128)(2,1)} %copy-done.10) | copy-start | bytes 884740
  (37 other events, 232.2 us)
Sparse Core Ops, SparseCore 0:
  11.6 61.5 all-gather.11
  76.6 59.9 all-gather.7
  138.8 41.8 all-gather.9
  182.7 60.5 all-gather.13
  247.7 23.9 reduce-scatter.8
  275.4 112.9 all-gather.15
  392.3 74.9 all-gather.19
  483.5 118.8 reduce-scatter.12
  608.1 121.5 reduce-scatter.10
  836.4 30.0 all-reduce.12
  870.4 63.6 reduce-scatter.18
  937.3 83.4 reduce-scatter.20
  1024.5 62.7 reduce-scatter.14
  1088.7 22.6 all-gather.17
  1115.2 63.4 reduce-scatter.16
  1182.5 75.7 reduce-scatter.22

commit v2 on v1

--- a/solution.py
+++ b/solution.py
@@ -1,8 +1,11 @@
+import functools
 import math
 
 import jax
 import jax.numpy as jnp
 from jax import lax
+from jax.experimental import pallas as pl
+from jax.experimental.pallas import tpu as pltpu
 from jax.sharding import PartitionSpec as P
 
 D = 2560
@@ -114,7 +117,6 @@
 
 BF = jnp.bfloat16
 F32 = jnp.float32
-EVERY = ("dp", "tensor")
 
 
 def dot(left, right):
@@ -129,32 +131,653 @@
     return jnp.einsum("ca,cb->ab", left, right, preferred_element_type=F32)
 
 
-def gather_dp(block):
-    return lax.all_gather(block, "dp", axis=0, tiled=True)
-
-
-def gather_tensor(block):
-    return lax.all_gather(block, "tensor", axis=0, tiled=True)
-
-
-def gather_every(block):
-    return lax.all_gather(block, EVERY, axis=0, tiled=True)
-
-
-def scatter_dp(part):
-    return lax.psum_scatter(part, "dp", scatter_dimension=0, tiled=True).astype(F32)
-
-
-def scatter_tensor(part):
-    return lax.psum_scatter(part, "tensor", scatter_dimension=0, tiled=True).astype(F32)
-
-
-def scatter_every(part):
-    return lax.psum_scatter(part, EVERY, scatter_dimension=0, tiled=True).astype(F32)
-
-
 def swap_dp(blocks):
     return lax.all_to_all(blocks, "dp", 0, 0, tiled=True)
+
+
+MESH = pl.DeviceIdType.MESH
+ANY = pl.BlockSpec(memory_space=pl.ANY)
+VMEM = pl.BlockSpec(memory_space=pltpu.VMEM)
+VMEM_BYTES = 60 * 1024 * 1024
+
+
+class Links:
+    def __init__(self, n_dp):
+        self.n_high = n_dp // 2
+        dp = lax.axis_index("dp")
+        tensor = lax.axis_index("tensor")
+        self.high, self.low = dp // 2, dp % 2
+        self.side, self.core = tensor // 2, tensor % 2
+
+    def device(self, high=None, low=None, side=None, core=None):
+        high = self.high if high is None else high
+        low = self.low if low is None else low
+        side = self.side if side is None else side
+        core = self.core if core is None else core
+        return {"dp": high * 2 + low, "tensor": side * 2 + core}
+
+    def behind(self, step):
+        return (self.high + self.n_high - step) % self.n_high
+
+    def ahead(self, step):
+        return (self.high + step) % self.n_high
+
+    def over_low(self):
+        return self.device(low=1 - self.low)
+
+    def over_side(self):
+        return self.device(side=1 - self.side)
+
+    def over_core(self):
+        return self.device(core=1 - self.core)
+
+    def meet(self, high=True, low=True, side=True, core=True):
+        barrier = pltpu.get_barrier_semaphore()
+        partners = []
+        if high:
+            partners += [self.device(high=self.ahead(k)) for k in range(1, self.n_high)]
+        if low:
+            partners.append(self.over_low())
+        if side:
+            partners.append(self.over_side())
+        if core:
+            partners.append(self.over_core())
+        for partner in partners:
+            pl.semaphore_signal(barrier, inc=1, device_id=partner, device_id_type=MESH)
+        pl.semaphore_wait(barrier, len(partners))
+
+
+class Copies:
+    def __init__(self, send, recv, local):
+        self.send, self.recv, self.local = send, recv, local
+        self.count = self.local_count = 0
+        self.started = []
+        self.local_started = []
+
+    def go(self, source, target, device):
+        copy = pltpu.make_async_remote_copy(
+            src_ref=source,
+            dst_ref=target,
+            send_sem=self.send.at[self.count],
+            recv_sem=self.recv.at[self.count],
+            device_id=device,
+            device_id_type=MESH,
+        )
+        self.count += 1
+        copy.start()
+        self.started.append(copy)
+        return copy
+
+    def near(self, source, target):
+        copy = pltpu.make_async_copy(source, target, self.local.at[self.local_count])
+        self.local_count += 1
+        copy.start()
+        self.local_started.append(copy)
+        return copy
+
+    def finish(self):
+        for copy in self.started:
+            copy.wait_send()
+
+
+def take_turns(*streams):
+    streams = list(streams)
+    while streams:
+        for stream in list(streams):
+            try:
+                next(stream)
+            except StopIteration:
+                streams.remove(stream)
+
+
+def steps_by_distance(count):
+    order, k = [], 1
+    while len(order) < count - 1:
+        order.append(k)
+        if len(order) < count - 1:
+            order.append(count - k)
+        k += 1
+    return order
+
+
+def every_gather(links, copies, block, out):
+    n_high = links.n_high
+    cut = out.shape[-1] // 256 * 128
+    halves = (pl.ds(0, cut), pl.ds(cut, out.shape[-1] - cut))
+
+    def slot(high, low, side):
+        return out.at[high * 2 + low, side * 2 + links.core]
+
+    mine = slot(links.high, links.low, links.side)
+    own = copies.near(block, mine)
+    arrive = {}
+    for k in steps_by_distance(n_high):
+        arrive[k] = copies.go(block, mine, links.device(high=links.ahead(k)))
+    yield
+    order = [0] + steps_by_distance(n_high)
+    last, over_low, over_side, corner_a, corner_b = [], {}, {}, {}, {}
+
+    def first(k):
+        here = slot(links.behind(k), links.low, links.side)
+        if k:
+            arrive[k].wait_recv()
+        source = here if k else block
+        over_low[k] = copies.go(source, here, links.over_low())
+        over_side[k] = copies.go(source, here, links.over_side())
+        last.append(copies.go(source, here, links.over_core()))
+
+    def second(k):
+        over_low[k].wait_recv()
+        here = slot(links.behind(k), 1 - links.low, links.side)
+        part = here.at[:, halves[0]]
+        corner_a[k] = copies.go(part, part, links.over_side())
+        last.append(copies.go(here, here, links.over_core()))
+        over_side[k].wait_recv()
+        here = slot(links.behind(k), links.low, 1 - links.side)
+        part = here.at[:, halves[1]]
+        corner_b[k] = copies.go(part, part, links.over_low())
+        last.append(copies.go(here, here, links.over_core()))
+
+    def third(k):
+        here = slot(links.behind(k), 1 - links.low, 1 - links.side)
+        for corner, half in ((corner_a, halves[0]), (corner_b, halves[1])):
+            corner[k].wait_recv()
+            part = here.at[:, half]
+            last.append(copies.go(part, part, links.over_core()))
+
+    for i in range(n_high + 2):
+        if i < n_high:
+            first(order[i])
+            yield
+        if 0 <= i - 1 < n_high:
+            second(order[i - 1])
+            yield
+        if 0 <= i - 2:
+            third(order[i - 2])
+            yield
+    for copy in last:
+        copy.wait_recv()
+    own.wait()
+
+
+def dp_gather(links, copies, block, out):
+    mine = out.at[links.high * 2 + links.low]
+    own = copies.near(block, mine)
+    arrive, last = {}, []
+    for k in steps_by_distance(links.n_high):
+        arrive[k] = copies.go(block, mine, links.device(high=links.ahead(k)))
+    last.append(copies.go(block, mine, links.over_low()))
+    yield
+    for k in steps_by_distance(links.n_high):
+        arrive[k].wait_recv()
+        here = out.at[links.behind(k) * 2 + links.low]
+        last.append(copies.go(here, here, links.over_low()))
+        yield
+    for copy in last:
+        copy.wait_recv()
+    own.wait()
+
+
+def tensor_gather(links, copies, block, out):
+    mine = out.at[links.side * 2 + links.core]
+    own = copies.near(block, mine)
+    last = [copies.go(block, mine, links.over_core())]
+    across = copies.go(block, mine, links.over_side())
+    yield
+    across.wait_recv()
+    here = out.at[(1 - links.side) * 2 + links.core]
+    last.append(copies.go(here, here, links.over_core()))
+    yield
+    for copy in last:
+        copy.wait_recv()
+    own.wait()
+
+
+def every_scatter(links, copies, part, bufs, result):
+    own, from_core, low_a, side_b, side_a, low_b, done, from_high = bufs
+    n_high = links.n_high
+    columns = part.shape[-1]
+    cut = columns // 256 * 128
+    half_a, half_b = pl.ds(0, cut), pl.ds(cut, columns - cut)
+    order = steps_by_distance(n_high) + [0]
+    loads, core_in, a_in, b_in, a_last, b_last, high_in = {}, {}, {}, {}, {}, {}, {}
+    for k in order:
+        there = links.ahead(k)
+        core_in[k] = copies.go(
+            part.at[there, :, :, 1 - links.core], from_core.at[k], links.over_core()
+        )
+        loads[k] = copies.near(part.at[there, :, :, links.core], own.at[k])
+    yield
+
+    def first(k):
+        core_in[k].wait_recv()
+        loads[k].wait()
+        for low in range(2):
+            for side in range(2):
+                own[k, low, side] = (
+                    own[k, low, side].astype(F32) + from_core[k, low, side].astype(F32)
+                ).astype(BF)
+        a_in[k] = copies.go(
+            own.at[k, 1 - links.low, :, :, half_a], low_a.at[k], links.over_low()
+        )
+        b_in[k] = copies.go(
+            own.at[k, :, 1 - links.side, :, half_b], side_b.at[k], links.over_side()
+        )
+
+    def second(k):
+        a_in[k].wait_recv()
+        for side in range(2):
+            low_a[k, side] = (
+                low_a[k, side].astype(F32) + own[k, links.low, side, :, half_a].astype(F32)
+            ).astype(BF)
+        a_last[k] = copies.go(low_a.at[k, 1 - links.side], side_a.at[k], links.over_side())
+        b_in[k].wait_recv()
+        for low in range(2):
+            side_b[k, low] = (
+                side_b[k, low].astype(F32) + own[k, low, links.side, :, half_b].astype(F32)
+            ).astype(BF)
+        b_last[k] = copies.go(side_b.at[k, 1 - links.low], low_b.at[k], links.over_low())
+
+    def third(k):
+        a_last[k].wait_recv()
+        done[k, :, half_a] = (
+            side_a[k].astype(F32) + low_a[k, links.side].astype(F32)
+        ).astype(BF)
+        b_last[k].wait_recv()
+        done[k, :, half_b] = (
+            low_b[k].astype(F32) + side_b[k, links.low].astype(F32)
+        ).astype(BF)
+        if k:
+            high_in[k] = copies.go(
+                done.at[k], from_high.at[k - 1], links.device(high=links.ahead(k))
+            )
+
+    for i in range(n_high + 2):
+        if i < n_high:
+            first(order[i])
+            yield
+        if 0 <= i - 1 < n_high:
+            second(order[i - 1])
+            yield
+        if 0 <= i - 2:
+            third(order[i - 2])
+            yield
+    total = done[0].astype(F32)
+    for k in steps_by_distance(n_high):
+        high_in[k].wait_recv()
+        total = total + from_high[k - 1].astype(F32)
+    result[...] = total
+
+
+def every_scatter_scratch(n_high, rows, columns):
+    cut = columns // 256 * 128
+    return [
+        pltpu.VMEM((n_high, 2, 2, rows, columns), BF),
+        pltpu.VMEM((n_high, 2, 2, rows, columns), BF),
+        pltpu.VMEM((n_high, 2, rows, cut), BF),
+        pltpu.VMEM((n_high, 2, rows, columns - cut), BF),
+        pltpu.VMEM((n_high, rows, cut), BF),
+        pltpu.VMEM((n_high, rows, columns - cut), BF),
+        pltpu.VMEM((n_high, rows, columns), BF),
+        pltpu.VMEM((n_high - 1, rows, columns), BF),
+    ]
+
+
+def dp_scatter(links, copies, part, bufs, result):
+    from_low, done, from_high = bufs
+    order = steps_by_distance(links.n_high) + [0]
+    low_in, high_in = {}, {}
+    for k in order:
+        low_in[k] = copies.go(
+            part.at[links.ahead(k), 1 - links.low], from_low.at[k], links.over_low()
+        )
+    yield
+    for k in order:
+        low_in[k].wait_recv()
+        done[k] = (
+            part[links.ahead(k), links.low].astype(F32) + from_low[k].astype(F32)
+        ).astype(BF)
+        if k:
+            high_in[k] = copies.go(
+                done.at[k], from_high.at[k - 1], links.device(high=links.ahead(k))
+            )
+        yield
+    total = done[0].astype(F32)
+    for k in steps_by_distance(links.n_high):
+        high_in[k].wait_recv()
+        total = total + from_high[k - 1].astype(F32)
+    result[...] = total.astype(result.dtype)
+    yield
+
+
+def dp_scatter_scratch(n_high, shape):
+    return [
+        pltpu.VMEM((n_high, *shape), BF),
+        pltpu.VMEM((n_high, *shape), BF),
+        pltpu.VMEM((n_high - 1, *shape), BF),
+    ]
+
+
+def semaphores(count, local):
+    return [
+        pltpu.SemaphoreType.DMA((count,)),
+        pltpu.SemaphoreType.DMA((count,)),
+        pltpu.SemaphoreType.DMA((local,)),
+    ]
+
+
+def params(number):
+    return pltpu.CompilerParams(
+        collective_id=number, has_side_effects=True, vmem_limit_bytes=VMEM_BYTES
+    )
+
+
+def count_every_gather(n_high):
+    return n_high - 1 + 9 * n_high
+
+
+def weights_kernel(n_dp, down, o_t, q_up, kv_up, gains, cot, f_down, f_o, f_q, f_kv, f_g, f_cot, send, recv, local):
+    links = Links(n_dp)
+    copies = Copies(send, recv, local)
+    links.meet()
+    take_turns(
+        every_gather(links, copies, down, f_down),
+        dp_gather(links, copies, gains, f_g),
+        dp_gather(links, copies, q_up, f_q),
+        dp_gather(links, copies, kv_up, f_kv),
+        dp_gather(links, copies, o_t, f_o),
+        every_gather(links, copies, cot, f_cot),
+    )
+    copies.finish()
+
+
+def gather_weights(n_dp, n_tensor, down, o_t, q_up, kv_up, gains, cot):
+    n_high = n_dp // 2
+    count = 2 * count_every_gather(n_high) + 4 * (2 * n_high - 1)
+
+    def over(block, *lead):
+        return jax.ShapeDtypeStruct((*lead, *block.shape), block.dtype)
+
+    return pl.pallas_call(
+        functools.partial(weights_kernel, n_dp),
+        out_shape=(
+            over(down, n_dp, n_tensor),
+            over(o_t, n_dp),
+            over(q_up, n_dp),
+            over(kv_up, n_dp),
+            over(gains, n_dp),
+            over(cot, n_dp, n_tensor),
+        ),
+        in_specs=[ANY] * 6,
+        out_specs=[ANY] * 6,
+        scratch_shapes=semaphores(count, 6),
+        compiler_params=params(1),
+        name="gather_weights",
+    )(down, o_t, q_up, kv_up, gains, cot)
+
+
+def resid_kernel(n_dp, part, x_rows, gain, full, resid, branch, from_core, out_side, from_side, block, send, recv, local):
+    links = Links(n_dp)
+    copies = Copies(send, recv, local)
+    links.meet()
+    arrive = copies.go(part.at[:, 1 - links.core], from_core, links.over_core())
+    arrive.wait_recv()
+    out_side[...] = (
+        part[1 - links.side, links.core].astype(F32) + from_core[1 - links.side].astype(F32)
+    ).astype(BF)
+    arrive = copies.go(out_side, from_side, links.over_side())
+    mine = part[links.side, links.core].astype(F32) + from_core[links.side].astype(F32)
+    arrive.wait_recv()
+    attn = RESIDUAL_SCALE * (mine + from_side[...].astype(F32))
+    stream = x_rows[...].astype(F32) + attn
+    branch[...] = attn
+    resid[...] = stream
+    block[...] = (stream * inverse_rms(stream) * gain[...]).astype(BF)
+    take_turns(every_gather(links, copies, block, full))
+    copies.finish()
+
+
+def attention_residual(n_dp, part, x_rows, gain):
+    n_tensor = 4
+    rows, columns = x_rows.shape
+    block = (rows, columns)
+    return pl.pallas_call(
+        functools.partial(resid_kernel, n_dp),
+        out_shape=(
+            jax.ShapeDtypeStruct((n_dp, n_tensor, rows, columns), BF),
+            jax.ShapeDtypeStruct(block, F32),
+            jax.ShapeDtypeStruct(block, F32),
+        ),
+        in_specs=[VMEM] * 3,
+        out_specs=[ANY, VMEM, VMEM],
+        scratch_shapes=[
+            pltpu.VMEM((2, *block), BF),
+            pltpu.VMEM(block, BF),
+            pltpu.VMEM(block, BF),
+            pltpu.VMEM(block, BF),
+            *semaphores(2 + count_every_gather(n_dp // 2), 1),
+        ],
+        compiler_params=params(2),
+        name="attention_residual",
+    )(part.reshape(2, 2, rows, columns), x_rows, gain)
+
+
+def grad_rows_kernel(n_dp, both, *refs):
+    links = Links(n_dp)
+    copies = Copies(*refs[-3:])
+    g_part, resid, cot, gain = refs[:4]
+    if both:
+        m_part, attn_full, g_rows, block_full, m_rows = refs[4:9]
+        scratch = refs[9:-3]
+    else:
+        attn_full, g_rows = refs[4:6]
+        scratch = refs[6:-3]
+    links.meet()
+
+    def grad_stream():
+        grad_rows = scratch[0]
+        yield from every_scatter(links, copies, g_part, scratch[1:9], g_rows)
+        stream = resid[...]
+        inv = inverse_rms(stream)
+        grad = cot[...].astype(F32) + norm_back(g_rows[...] * gain[...], stream * inv, inv)
+        grad_rows[...] = (RESIDUAL_SCALE * grad).astype(BF)
+        yield from tensor_gather(links, copies, grad_rows, attn_full)
+
+    if both:
+        block = block_stream(links, copies, m_part, resid, block_full, m_rows, scratch[9:])
+        take_turns(grad_stream(), block)
+    else:
+        take_turns(grad_stream())
+    copies.finish()
+
+
+def block_stream(links, copies, m_part, resid, block_full, m_rows, scratch):
+    block_rows = scratch[0]
+    yield from every_scatter(links, copies, m_part, scratch[1:9], m_rows)
+    m_rows[...] = RESIDUAL_SCALE * m_rows[...]
+    block_rows[...] = resid[...] + m_rows[...]
+    yield from tensor_gather(links, copies, block_rows, block_full)
+
+
+def block_rows_kernel(n_dp, m_part, resid, block_full, m_rows, *rest):
+    links = Links(n_dp)
+    copies = Copies(*rest[-3:])
+    links.meet()
+    take_turns(block_stream(links, copies, m_part, resid, block_full, m_rows, rest[:-3]))
+    copies.finish()
+
+
+def residual_grads(n_dp, g_part, m_part, resid, cot, gain):
+    n_high = n_dp // 2
+    rows, columns = resid.shape
+    shape = (n_high, 2, 2, 2, rows, columns)
+    g_part, m_part = g_part.reshape(shape), m_part.reshape(shape)
+    both = n_high <= 4
+    one = jax.ShapeDtypeStruct((rows, columns), F32)
+    grad_out = (jax.ShapeDtypeStruct((4, rows, columns), BF), one)
+    block_out = (jax.ShapeDtypeStruct((4, rows, columns), F32), one)
+    grad_scratch = [
+        pltpu.VMEM((rows, columns), BF),
+        *every_scatter_scratch(n_high, rows, columns),
+    ]
+    block_scratch = [
+        pltpu.VMEM((rows, columns), F32),
+        *every_scatter_scratch(n_high, rows, columns),
+    ]
+    count, local = 6 * n_high - 1 + 3, n_high + 1
+    if both:
+        return pl.pallas_call(
+            functools.partial(grad_rows_kernel, n_dp, True),
+            out_shape=grad_out + block_out,
+            in_specs=[ANY, VMEM, VMEM, VMEM, ANY],
+            out_specs=[ANY, VMEM, ANY, VMEM],
+            scratch_shapes=[*grad_scratch, *block_scratch, *semaphores(2 * count, 2 * local)],
+            compiler_params=params(3),
+            name="residual_grads",
+        )(g_part, resid, cot, gain, m_part)
+    grads = pl.pallas_call(
+        functools.partial(grad_rows_kernel, n_dp, False),
+        out_shape=grad_out,
+        in_specs=[ANY, VMEM, VMEM, VMEM],
+        out_specs=[ANY, VMEM],
+        scratch_shapes=[*grad_scratch, *semaphores(count, local)],
+        compiler_params=params(3),
+        name="residual_grads",
+    )(g_part, resid, cot, gain)
+    block = pl.pallas_call(
+        functools.partial(block_rows_kernel, n_dp),
+        out_shape=block_out,
+        in_specs=[ANY, VMEM],
+        out_specs=[ANY, VMEM],
+        scratch_shapes=[*block_scratch, *semaphores(count, local)],
+        compiler_params=params(6),
+        name="block_rows",
+    )(m_part, resid)
+    return (*grads, *block)
+
+
+def latent_kernel(n_dp, part, full, from_core, half, from_side, send, recv, local):
+    links = Links(n_dp)
+    copies = Copies(send, recv, local)
+    links.meet(high=False, low=False)
+    arrive = copies.go(part.at[1 - links.core], from_core, links.over_core())
+    arrive.wait_recv()
+    half[...] = (part[links.core].astype(F32) + from_core[...].astype(F32)).astype(BF)
+    arrive = copies.go(half, from_side, links.over_side())
+    arrive.wait_recv()
+    full[links.core] = (half[...].astype(F32) + from_side[...].astype(F32)).astype(BF)
+    arrive = copies.go(full.at[links.core], full.at[links.core], links.over_core())
+    arrive.wait_recv()
+    copies.finish()
+
+
+def sum_latents(n_dp, part):
+    rows, columns = part.shape
+    half = (rows // 2, columns)
+    return pl.pallas_call(
+        functools.partial(latent_kernel, n_dp),
+        out_shape=jax.ShapeDtypeStruct((2, *half), BF),
+        in_specs=[VMEM],
+        out_specs=VMEM,
+        scratch_shapes=[pltpu.VMEM(half, BF)] * 3 + semaphores(3, 1),
+        compiler_params=params(4),
+        name="sum_latents",
+    )(part.reshape(2, *half)).reshape(rows, columns)
+
+
+def weight_grads_kernel(n_dp, d_part, o_part, q_part, kv_part, small, stats, d_full, o_sum, q_sum, kv_sum, small_full, *rest):
+    d_block, small_block, stats_block = rest[:3]
+    bufs = rest[3:15]
+    small_in, stats_in = rest[15:17]
+    send, recv, local = rest[17:]
+    links = Links(n_dp)
+    copies = Copies(send, recv, local)
+    links.meet()
+
+    def small_stream():
+        n_high = links.n_high
+        low_in = copies.go(
+            small.at[:, 1 - links.low], small_in.at[pl.ds(0, n_high)], links.over_low()
+        )
+        stats_low = copies.go(stats, stats_in.at[0], links.over_low())
+        yield
+        low_in.wait_recv()
+        stats_low.wait_recv()
+        for k in range(n_high):
+            small_in[k] = small_in[k] + small[k, links.low]
+        stats_block[...] = stats[...] + stats_in[0]
+        waits = []
+        for k in range(1, n_high):
+            there = links.ahead(k)
+            waits.append(
+                copies.go(
+                    small_in.at[there], small_in.at[n_high + k - 1], links.device(high=there)
+                )
+            )
+            waits.append(copies.go(stats_block, stats_in.at[k], links.device(high=there)))
+        yield
+        for wait in waits:
+            wait.wait_recv()
+        total = small_in[links.high]
+        everything = stats_block[...]
+        for k in range(1, n_high):
+            total = total + small_in[n_high + k - 1]
+            everything = everything + stats_in[k]
+        small_block[0] = total
+        small_block[1] = everything
+        yield from tensor_gather(links, copies, small_block, small_full)
+
+    def down_stream():
+        yield from dp_scatter(links, copies, d_part, bufs[:3], d_block)
+        yield from tensor_gather(links, copies, d_block, d_full)
+
+    take_turns(
+        down_stream(),
+        dp_scatter(links, copies, q_part, bufs[6:9], q_sum),
+        dp_scatter(links, copies, kv_part, bufs[9:12], kv_sum),
+        dp_scatter(links, copies, o_part, bufs[3:6], o_sum),
+        small_stream(),
+    )
+    copies.finish()
+
+
+def sum_weight_grads(n_dp, down, o_t, q_up, kv_up, small, stats):
+    n_high = n_dp // 2
+
+    def parts(array):
+        return array.reshape(n_high, 2, array.shape[0] // n_dp, *array.shape[1:])
+
+    down, o_t, q_up, kv_up = parts(down), parts(o_t), parts(q_up), parts(kv_up)
+    small = small.reshape(n_high, 2, *small.shape[1:])
+    count = 4 * (2 * n_high - 1) + 2 * n_high + 6
+    d_shape, o_shape, q_shape, kv_shape = (a.shape[2:] for a in (down, o_t, q_up, kv_up))
+    one = stats.shape
+    return pl.pallas_call(
+        functools.partial(weight_grads_kernel, n_dp),
+        out_shape=(
+            jax.ShapeDtypeStruct((4, *d_shape), BF),
+            jax.ShapeDtypeStruct(o_shape, F32),
+            jax.ShapeDtypeStruct(q_shape, F32),
+            jax.ShapeDtypeStruct(kv_shape, F32),
+            jax.ShapeDtypeStruct((4, 2, *one), F32),
+        ),
+        in_specs=[VMEM] * 6,
+        out_specs=[VMEM] * 5,
+        scratch_shapes=[
+            pltpu.VMEM(d_shape, BF),
+            pltpu.VMEM((2, *one), F32),
+            pltpu.VMEM(one, F32),
+            *dp_scatter_scratch(n_high, d_shape),
+            *dp_scatter_scratch(n_high, o_shape),
+            *dp_scatter_scratch(n_high, q_shape),
+            *dp_scatter_scratch(n_high, kv_shape),
+            pltpu.VMEM((2 * n_high - 1, *one), F32),
+            pltpu.VMEM((n_high, *one), F32),
+            *semaphores(count, 2),
+        ],
+        compiler_params=params(5),
+        name="sum_weight_grads",
+    )(down, o_t, q_up, kv_up, small, stats)
 
 
 def per_device(
@@ -188,15 +811,45 @@
     def rows_of(values, count):
         return lax.dynamic_slice_in_dim(values, me * count, count, 0)
 
-    full_q_down = gather_every(rows_of(q_down, rows_down))
-    full_kv_down = gather_every(rows_of(kv_down, rows_down))
-    full_q_up = gather_dp(q_up)
-    full_kv_up = gather_dp(kv_up)
-    gain_attn = gather_dp(attn_gain).astype(F32)
-    gain_q = gather_dp(q_gain).astype(F32)
-    gain_kv = gather_dp(kv_gain).astype(F32)
-    gain_mlp = gather_dp(mlp_gain).astype(F32)
-    full_o = gather_dp(o_proj.T)
+    rank_q = q_down.shape[1]
+    columns_down = rank_q + kv_down.shape[1]
+    pad_down = -columns_down % 128
+    down_rows = jnp.concatenate(
+        [
+            rows_of(q_down, rows_down),
+            rows_of(kv_down, rows_down),
+            jnp.zeros((rows_down, pad_down), BF),
+        ],
+        axis=1,
+    )
+    lanes = -(-width // 128) * 128
+
+    def lane_rows(rows, count, kind):
+        padded = [jnp.pad(row.astype(kind), (0, lanes - row.shape[0])) for row in rows]
+        return jnp.stack(padded + [jnp.zeros((lanes,), kind)] * (count - len(padded)))
+
+    cot_rows = rows_of(cotangent, share)
+    f_down, f_o, f_q, f_kv, f_g, f_cot = gather_weights(
+        n_dp,
+        n_tensor,
+        down_rows,
+        o_proj.T,
+        q_up,
+        kv_up,
+        lane_rows([attn_gain, q_gain, kv_gain, mlp_gain], 16, BF),
+        cot_rows,
+    )
+    full_down = f_down.reshape(n_dp * width, columns_down + pad_down)
+    full_o = f_o.reshape(n_dp * width, -1)
+    full_kv_up = f_kv.reshape(-1, kv_up.shape[1])
+
+    def gain_of(row, gain):
+        return f_g[:, row, : gain.shape[0]].reshape(-1).astype(F32)
+
+    gain_attn = gain_of(0, attn_gain)
+    gain_q = gain_of(1, q_gain)
+    gain_kv = gain_of(2, kv_gain)
+    gain_mlp = gain_of(3, mlp_gain)
 
     packed = jnp.concatenate(
         [
@@ -206,7 +859,9 @@
         ],
         axis=2,
     ).transpose(1, 0, 2)
+    packed, f_q = lax.optimization_barrier((packed, f_q))
     mine = swap_dp(packed).reshape(n_dp * width, 3 * slice_ff)
+    full_q_up = f_q.reshape(-1, q_up.shape[1])
     w_in = mine[:, : 2 * slice_ff]
     w_out = mine[:, 2 * slice_ff :]
 
@@ -217,12 +872,13 @@
     inv_one = inverse_rms(stream)
     unit_one = stream * inv_one
     normed = (unit_one * gain_attn).astype(BF)
-    q_latent = dot(normed, full_q_down)
+    latents = dot(normed, full_down)
+    q_latent = latents[:, :rank_q]
     inv_q = inverse_rms(q_latent)
     unit_q = q_latent * inv_q
     q_normed = (unit_q * gain_q).astype(BF)
     q_heads = dot(q_normed, full_q_up).reshape(length, heads_local, NOPE + ROPE)
-    kv_joint = dot(normed, full_kv_down)
+    kv_joint = latents[:, rank_q:columns_down]
     kv_latent = kv_joint[:, :KR]
     inv_kv = inverse_rms(kv_latent)
     unit_kv = kv_latent * inv_kv
@@ -250,13 +906,14 @@
     mixed = mixed_heads.transpose(1, 0, 2).reshape(length, heads_local * VD).astype(BF)
     attn_part = dot_nt(mixed, full_o)
 
-    attn_rows = RESIDUAL_SCALE * scatter_tensor(attn_part.astype(BF))
-    resid_rows = rows_of(layer_input, share).astype(F32) + attn_rows
+    x_rows = rows_of(layer_input, share)
+    f_normed, resid_rows, attn_rows = attention_residual(
+        n_dp, attn_part.astype(BF), x_rows, gain_mlp[None, :]
+    )
+    normed_two = f_normed.reshape(n_dp * length, -1)
     inv_two = inverse_rms(resid_rows)
     unit_two = resid_rows * inv_two
-    normed_two = gather_every((unit_two * gain_mlp).astype(BF))
-    cot_rows = rows_of(cotangent, share)
-    grad_mlp = (RESIDUAL_SCALE * gather_every(cot_rows).astype(F32)).astype(BF)
+    grad_mlp = (RESIDUAL_SCALE * f_cot.reshape(n_dp * length, -1).astype(F32)).astype(BF)
 
     gate_upper = dot(normed_two, w_in)
     gate = gate_upper[:, :slice_ff]
@@ -264,7 +921,7 @@
     sigma = jax.nn.sigmoid(gate)
     swish = gate * sigma
     hidden = (swish * upper).astype(BF)
-    mlp_rows = RESIDUAL_SCALE * scatter_every(dot_nt(hidden, w_out).astype(BF))
+    mlp_part = dot_nt(hidden, w_out).astype(BF)
     grad_hidden = dot(grad_mlp, w_out)
     grad_both = jnp.concatenate(
         [
@@ -273,27 +930,23 @@
         ],
         axis=1,
     ).astype(BF)
-    grad_normed_two = scatter_every(dot_nt(grad_both, w_in).astype(BF))
+    normed_part = dot_nt(grad_both, w_in).astype(BF)
     grad_packed = jnp.concatenate(
         [dot_tn(normed_two, grad_both), dot_tn(grad_mlp, hidden)], axis=1
     ).astype(BF)
     swapped = swap_dp(grad_packed.reshape(n_dp, width, 3 * slice_ff))
+    normed_part, grad_packed = lax.optimization_barrier((normed_part, grad_packed))
+    f_attn, grad_normed_two, f_block, mlp_rows = residual_grads(
+        n_dp, normed_part, mlp_part, resid_rows, cot_rows, gain_mlp[None, :]
+    )
+    grad_attn = f_attn.reshape(length, -1)
+    block_full = f_block.reshape(length, -1)
 
     def unpack(part):
         return part.transpose(1, 0, 2).reshape(width, n_dp * slice_ff).astype(F32)
 
-    grad_w_gate = unpack(swapped[:, :, :slice_ff])
-    grad_w_up = unpack(swapped[:, :, slice_ff : 2 * slice_ff])
-    grad_w_down = unpack(swapped[:, :, 2 * slice_ff :]).T
-
-    block_rows = resid_rows + mlp_rows
-    block_full = gather_tensor(block_rows)
     weight_rows = rows_of(valid_mask.astype(F32)[:, None], share)
     grad_mlp_gain = jnp.sum(grad_normed_two * unit_two, axis=0)
-    grad_resid_rows = cot_rows.astype(F32) + norm_back(
-        grad_normed_two * gain_mlp, unit_two, inv_two
-    )
-    grad_attn = gather_tensor((RESIDUAL_SCALE * grad_resid_rows).astype(BF))
 
     grad_o = dot_tn(grad_attn, mixed)
     grad_mixed = dot(grad_attn, full_o).astype(BF)
@@ -318,30 +971,36 @@
         .astype(BF)
     )
     grad_key_rot = unrotate(jnp.sum(grad_keys[..., NOPE:], axis=1), cosine, sine_table)
+    grad_q_heads, swapped = lax.optimization_barrier((grad_q_heads, swapped))
     grad_q_up = dot_tn(q_normed, grad_q_heads)
     grad_kv_up = dot_tn(kv_normed, grad_kv_heads)
-    grad_latents = lax.psum(
+    grad_latents = sum_latents(
+        n_dp,
         jnp.concatenate(
             [
                 dot_nt(grad_q_heads, full_q_up),
                 dot_nt(grad_kv_heads, full_kv_up),
                 grad_key_rot,
+                jnp.zeros((length, pad_down), F32),
             ],
             axis=1,
         ).astype(BF),
-        "tensor",
     ).astype(F32)
-    rank_q = q_latent.shape[1]
     grad_q_normed = grad_latents[:, :rank_q]
     grad_kv_normed = grad_latents[:, rank_q : rank_q + KR]
-    grad_kv_rot = grad_latents[:, rank_q + KR :]
+    grad_kv_rot = grad_latents[:, rank_q + KR : columns_down]
     grad_q_gain = jnp.sum(grad_q_normed * unit_q, axis=0)
     grad_kv_gain = jnp.sum(grad_kv_normed * unit_kv, axis=0)
-    grad_q_latent = norm_back(grad_q_normed * gain_q, unit_q, inv_q).astype(BF)
-    grad_kv_joint = jnp.concatenate(
-        [norm_back(grad_kv_normed * gain_kv, unit_kv, inv_kv), grad_kv_rot], axis=-1
+    grad_down = jnp.concatenate(
+        [
+            norm_back(grad_q_normed * gain_q, unit_q, inv_q),
+            norm_back(grad_kv_normed * gain_kv, unit_kv, inv_kv),
+            grad_kv_rot,
+            jnp.zeros((length, pad_down), F32),
+        ],
+        axis=-1,
     ).astype(BF)
-    grad_normed = dot_nt(grad_q_latent, full_q_down) + dot_nt(grad_kv_joint, full_kv_down)
+    grad_normed = dot_nt(grad_down, full_down)
     grad_attn_gain = jnp.sum(grad_normed * unit_one, axis=0)
     grad_input = grad_attn.astype(F32) * (1.0 / RESIDUAL_SCALE) + norm_back(
         grad_normed * gain_attn, unit_one, inv_one
@@ -350,31 +1009,53 @@
     quarter = lax.dynamic_index_in_dim(
         normed.reshape(length, n_dp, n_tensor, rows_down), me, 2, keepdims=False
     ).reshape(length, n_dp * rows_down)
-    grad_q_down = gather_tensor(scatter_dp(dot_tn(quarter, grad_q_latent).astype(BF)).astype(BF))
-    grad_kv_down = gather_tensor(scatter_dp(dot_tn(quarter, grad_kv_joint).astype(BF)).astype(BF))
-
-    stat_sums = lax.psum(
-        (
+    def by_dp(vector):
+        return vector.reshape(n_dp, -1)
+
+    def small_rows(vectors):
+        return jnp.stack(
+            [jnp.pad(by_dp(v), ((0, 0), (0, lanes - v.shape[0] // n_dp))) for v in vectors]
+            + [jnp.zeros((n_dp, lanes), F32)] * (8 - len(vectors)),
+            axis=1,
+        )
+
+    stats = jnp.stack(
+        [
             jnp.sum(weight_rows * resid_rows * resid_rows),
             jnp.sum(weight_rows * attn_rows * attn_rows),
             jnp.sum(weight_rows * mlp_rows * mlp_rows),
             jnp.sum(weight_rows),
-        ),
-        EVERY,
-    )
-    rms_stats = jnp.sqrt(jnp.stack(stat_sums[:3]) / (stat_sums[3] * D))
+        ]
+    )
+    s_down, s_o, s_q, s_kv, s_small = sum_weight_grads(
+        n_dp,
+        dot_tn(quarter, grad_down).astype(BF),
+        grad_o.astype(BF),
+        grad_q_up.astype(BF),
+        grad_kv_up.astype(BF),
+        small_rows([grad_attn_gain, grad_q_gain, grad_kv_gain, grad_mlp_gain]),
+        lane_rows([stats], 8, F32),
+    )
+    grad_w_gate = unpack(swapped[:, :, :slice_ff])
+    grad_w_up = unpack(swapped[:, :, slice_ff : 2 * slice_ff])
+    grad_w_down = unpack(swapped[:, :, 2 * slice_ff :]).T
+
+    d_down = s_down.reshape(width, -1).astype(F32)
+    gains = s_small[me, 0]
+    stat_sums = jnp.sum(s_small[:, 1, 0, :4], axis=0)
+    rms_stats = jnp.sqrt(stat_sums[:3] / (stat_sums[3] * D))
     return (
         block_full,
         grad_input,
-        scatter_dp(grad_attn_gain),
-        grad_q_down.astype(F32),
-        scatter_dp(grad_q_gain),
-        scatter_dp(grad_q_up.astype(BF)),
-        grad_kv_down.astype(F32),
-        scatter_dp(grad_kv_gain),
-        scatter_dp(grad_kv_up.astype(BF)),
-        scatter_dp(grad_o.astype(BF)).T,
-        scatter_dp(lax.psum(grad_mlp_gain, "tensor")),
+        gains[0, : attn_gain.shape[0]],
+        d_down[:, :rank_q],
+        gains[1, : q_gain.shape[0]],
+        s_q,
+        d_down[:, rank_q:columns_down],
+        gains[2, : kv_gain.shape[0]],
+        s_kv,
+        s_o.T,
+        jnp.sum(s_small[:, 0, 3], axis=0)[: mlp_gain.shape[0]],
         grad_w_gate,
         grad_w_up,
         grad_w_down,

time: 1280 us -> 854 us (0.67)
  waiting for transfers between devices: 640 us -> 0.01 us
  Pallas kernels: 0 us -> 465 us
  blocking collectives: 278 us -> 0 us
  starting transfers between devices: 18.2 us -> 44.4 us
  local copies, waits for them, and re-layouts: 105 us -> 128 us
  between operations: 19.4 us -> 2.08 us
    pallas_call x0 -> x5, Pallas kernels: none -> 465 us  [the longest x1 154 us: sum_weight_grads(): pl.pallas_call(functools.partial(weight_grads_kernel, n_dp), out_shape=(j...]
    reduce_scatter x8 -> x0, waiting for transfers between devices: 382 us -> none  [the longest x2 236 us: scatter_every(): lax.psum_scatter(part, EVERY, scatter_dimension=0, tiled=True).astype(F32)]
    all_gather x7 -> x0, waiting for transfers between devices: 156 us -> none  [the longest x4 96.8 us: gather_every(): return lax.all_gather(block, EVERY, axis=0, tiled=True)]
    all_to_all x1 -> x0, blocking collectives: 109 us -> none  [swap_dp(): return lax.all_to_all(blocks, 'dp', 0, 0, tiled=True)]
    all_to_all x1 -> x2, waiting for transfers between devices: 73.6 us -> 0.01 us  [swap_dp(): return lax.all_to_all(blocks, 'dp', 0, 0, tiled=True)]
    unnamed x2 -> x0, blocking collectives: 59.9 us -> none
    psum x2 -> x0, blocking collectives: 55.1 us -> none  [the longest x1 40.5 us: per_device(): lax.psum((jnp.sum(weight_rows * resid_rows * resid_rows), jnp.sum(weight_...]
    all_gather x4 -> x0, blocking collectives: 53.8 us -> none  [the longest x1 27.9 us: gather_dp(): return lax.all_gather(block, 'dp', axis=0, tiled=True)]
  transfers between devices with their start and end apart: 17 -> 2, of which waited for: 11 -> 0; matrix products, arithmetic and copies ran while one was open for 15% -> 23% of each run, Pallas kernels for 0% -> 6%
where the time goes in v2:
time: 854 us; the launch traced here: 843 us
  Pallas kernels  465 us (54%)
  matrix products  151 us (18%)
  local copies, waits for them, and re-layouts  128 us (15%)
  other arithmetic  51.8 us (6%)
  starting transfers between devices  44.4 us (5%)
    pallas_call x1, Pallas kernels, sum_weight_grads(): pl.pallas_call(functools.partial(weight_grads_kernel, n_dp), out_shape=(j...  154 us
    pallas_call x1, Pallas kernels, gather_weights(): pl.pallas_call(functools.partial(weights_kernel, n_dp), out_shape=(over(d...  143 us
    pallas_call x1, Pallas kernels, residual_grads(): pl.pallas_call(functools.partial(grad_rows_kernel, n_dp, True), out_shape...  102 us
    pallas_call x1, Pallas kernels, attention_residual(): pl.pallas_call(functools.partial(resid_kernel, n_dp), out_shape=(jax.Shap...  53.8 us
    all_to_all x2, starting transfers between devices, swap_dp(): return lax.all_to_all(blocks, 'dp', 0, 0, tiled=True)  44.4 us
    dot_general x6, matrix products, dot_nt(): return jnp.einsum('ac,bc->ab', left, right, preferred_element_type=F32)  31.3 us
    dot_general x6, matrix products, dot(): return jnp.dot(left, right, preferred_element_type=F32)  24.4 us
    dot_general x2, local copies, waits for them, and re-layouts, dot_tn(): return jnp.einsum('ca,cb->ab', left, right, preferred_element_type=F32)  21.3 us
  transfers between devices with their start and end apart: 2, of which 0 were waited for; matrix products, arithmetic and copies ran while one was open for 23% of the time, Pallas kernels for 6%

profile of v2, /device:TPU:1, one launch (start us, length us, event | category | flops | bytes accessed | tf_op | source)
XLA Modules:
  0.0 842.7 jit_solution(7564652643212242910)
XLA Ops:
  18.1 4.8 maximum_bitcast_fusion
  24.1 142.8 %gather_weights.1 = (bf16[8,4,80,1152]{3,2,1,0:T(8,128)(2,1)}, bf16[8,320,640]{2,1,0:T(8,128)(2,1)}, bf16[8,96,960]{2,1,0:T(8,128)(2,1)}, bf16[8,32,1280]{2,1,0:...) custom-call(bf16[80,1152]{1,0:T(8,128)(2,1)} %concatenate.49.down, ...), custom_call_target="tpu_custom_call" | custom-call | tf_op jit(solution)/shard_map/gather_weights/pallas_call | solution.py:501
  171.0 39.8 %all-to-all-start = ((bf16[8,320,600]{2,1,0:T(8,128)(2,1)}), bf16[8,320,600]{2,1,0:T(8,128)(2,1)}, u32[]{:S(2)}, u32[]{:S(2)}) async-start(bf16[8,320,600]{2,1,0:T(8,128)(2,1)} %copy.130), calls=%async_computation | async-start | bytes 6553600 | tf_op jit(solution)/shard_map/all_to_all | solution.py:135
  238.2 40.5 %while.28 = (s32[]{:T(128)}, bf16[10,192,64]{1,2,0:T(8,128)(2,1)}, f32[10,192]{1,0:T(8,128)}, bf16[10,192,96]{2,1,0:T(8,128)(2,1)}, bf16[10,192,96]{2,1,0:T(8,12...) while((s32[]{:T(128)}, bf16[10,192,64]{1,2,0:T(8,128)(2,1)}, ...), condition=%wide.region_6.7_spmd.clone, body=%wide.region_3.6_spmd.clone.sunk | while | flops 12312386 | bytes 667753 | solution.py:85
  281.6 4.2 convolution_convert_fusion.3
  285.8 53.8 %attention_residual.1 = (bf16[8,4,48,2560]{3,2,1,0:T(8,128)(2,1)}, f32[48,2560]{1,0:T(8,128)}, f32[48,2560]{1,0:T(8,128)}) custom-call(bf16[2,2,48,2560]{3,2,1,0:T(8,128)(2,1)} %bitcast.230, bf16[48,2560]{1,0:T(8,128)(2,1)} %get-tuple-element.406.x_rows, f32[1,2560]{1,0:T(1,128)} %reshape.344.gain.refs_3_), custom_call_target="tpu_custom_call" | custom-call | tf_op jit(solution)/shard_map/attention_residual/pallas_call | solution.py:544
  339.5 10.6 %copy.141 = bf16[2560,1536]{1,0:T(8,128)(2,1)} copy(bf16[2560,1536]{0,1:T(8,128)(2,1)} %bitcast.218) | data formatting | bytes 15728640 | tf_op jit(solution)/shard_map/ca,cb->ab/dot_general | solution.py:131
  350.1 8.4 %multiply_convert_fusion.1 = bf16[8,4,48,2560]{3,2,1,0:T(8,128)(2,1)} fusion(bf16[8,4,48,2560]{3,2,1,0:T(8,128)(2,1)} %get-tuple-element.129), kind=kLoop, calls=%fused_computation.66 | loop fusion | flops 11796480 | bytes 15728640 | tf_op jit(solution)/shard_map/convert_element_type | solution.py:916
  358.6 10.7 %copy.142 = bf16[2560,1536]{1,0:T(8,128)(2,1)} copy(bf16[2560,1536]{0,1:T(8,128)(2,1)} %bitcast.212) | data formatting | bytes 15728640 | tf_op jit(solution)/shard_map/ca,cb->ab/dot_general | solution.py:131
  371.8 6.8 fusion.55
  378.7 6.7 multiply_convert_fusion.4
  385.5 7.9 convolution_convert_fusion
  393.4 8.7 %convolution_convert_fusion.1 = bf16[1536,2560]{1,0:T(8,128)(2,1)} fusion(bf16[2560,600]{1,0:T(8,128)(2,1)} %bitcast.4, bf16[1536,200]{0,1:T(8,128)(2,1)S(1)} %get-tuple-element.386, bf16[1536,200]{0,1:T(8,128)(2,1)S(1)} %get-tuple-element.385), kind=kOutput, calls=%fused_computation.68 | convolution fusion | flops 3152117760 | bytes 11714560 | tf_op jit(solution)/shard_map/ac,bc->ab/dot_general | solution.py:127
  402.1 102.3 %residual_grads.1 = (bf16[4,48,2560]{2,1,0:T(8,128)(2,1)}, f32[48,2560]{1,0:T(8,128)}, f32[4,48,2560]{2,1,0:T(8,128)}, f32[48,2560]{1,0:T(8,128)}) custom-call(bf16[4,2,2,2,48,2560]{5,4,3,2,1,0:T(8,128)(2,1)} %bitcast.215, f32[48,2560]{1,0:T(8,128)} %get-tuple-element.139.refs_1_, bf16[48,2560]{1,0:T(8,128)(2,1)} %get-tuple-element.407.cot.refs_2_, ...), custom_call_target="tpu_custom_call" | custom-call | tf_op jit(solution)/shard_map/residual_grads/pallas_call | solution.py:629
  507.8 6.8 convolution_convert_fusion.6
  514.5 5.8 convolution_convert_fusion.8
  522.6 5.8 copy.143
  528.4 4.6 all-to-all-start.1
  533.7 64.3 %while.29 = (s32[]{:T(128)}, f32[10,192,96]{1,2,0:T(8,128)}, f32[10,192,96]{1,2,0:T(8,128)}, bf16[10,192,64]{1,2,0:T(8,128)(2,1)}, bf16[10,192,96]{2,1,0:T(8,128...) while((s32[]{:T(128)}, f32[10,192,96]{1,2,0:T(8,128)}, ...), condition=%wide.region_9.10_spmd.clone, body=%wide.region_7.9_spmd.clone.sunk | while | flops 31260480 | bytes 2378873 | solution.py:115
  622.5 12.1 %sum_latents.1 = bf16[2,96,1152]{2,1,0:T(8,128)(2,1)} custom-call(bf16[2,96,1152]{2,1,0:T(8,128)(2,1)} %concatenate.61.part), custom_call_target="tpu_custom_call" | custom-call | tf_op jit(solution)/shard_map/sum_latents/pallas_call | solution.py:677
  639.1 6.1 fusion.62
  650.5 153.8 %sum_weight_grads.1 = (bf16[4,80,1152]{2,1,0:T(8,128)(2,1)}, f32[320,640]{1,0:T(8,128)}, f32[96,960]{1,0:T(8,128)}, f32[32,1280]{1,0:T(8,128)}, f32[4,2,8,384]{3,2,1,0:T(8,128)}) custom-call(bf16[4,2,80,1152]{3,2,1,0:T(8,128)(2,1)} %bitcast.227, bf16[4,2,320,640]{3,2,1,0:T(8,128)(2,1)} %bitcast.214, bf16[4,2,96,960]{3,2,1,0:T(8,128)(2,1)} %bitcast.224, ...), custom_call_target="tpu_custom_call" | custom-call | tf_op jit(solution)/shard_map/sum_weight_grads/pallas_call | solution.py:755
  813.8 5.6 convert_bitcast_fusion
  834.0 4.1 fusion.61
  (356 shorter events, 227.8 us)
Async XLA Ops:
  0.7 8.0 copy-start.14
  8.7 7.7 copy-start.2
  171.0 200.8 %all-to-all-start = ((bf16[8,320,600]{2,1,0:T(8,128)(2,1)}), bf16[8,320,600]{2,1,0:T(8,128)(2,1)}, u32[]{:S(2)}, u32[]{:S(2)}) async-start(bf16[8,320,600]{2,1,0:T(8,128)(2,1)} %copy.130), calls=%async_computation | async-start | bytes 6553600 | tf_op jit(solution)/shard_map/all_to_all | solution.py:135
  213.5 4.4 copy-start.21
  232.0 3.2 copy-start.24
  234.1 4.1 copy-start.26
  238.2 41.9 %copy-start.19 = (f32[8,320]{1,0:T(8,128)S(1)}, f32[8,320]{1,0:T(8,128)}, u32[]{:S(2)}) copy-start(f32[8,320]{1,0:T(8,128)} %get-tuple-element.335) | copy-start | bytes 30724
  358.6 13.1 %copy-start.6 = (f32[48,2560]{1,0:T(8,128)S(1)}, f32[48,2560]{1,0:T(8,128)}, u32[]{:S(2)}) copy-start(f32[48,2560]{1,0:T(8,128)} %get-tuple-element.139.refs_1_) | copy-start | bytes 1474564
  385.4 8.0 copy-start.12
  385.5 8.0 copy-start.27
  385.5 8.0 copy-start.28
  507.7 6.8 copy-start.13
  528.4 90.9 %all-to-all-start.1 = ((bf16[8,320,600]{2,1,0:T(8,128)(2,1)}), bf16[8,320,600]{2,1,0:T(8,128)(2,1)}, u32[]{:S(2)}, u32[]{:S(2)}) async-start(bf16[8,320,600]{2,1,0:T(8,128)(2,1)} %copy.143), calls=%async_computation.1 | async-start | bytes 6553600 | tf_op jit(solution)/shard_map/all_to_all | solution.py:135
  533.7 64.3 %copy-start.7 = (f32[48,2560]{1,0:T(8,128)S(1)}, f32[48,2560]{1,0:T(8,128)}, u32[]{:S(2)}) copy-start(f32[48,2560]{1,0:T(8,128)} %get-tuple-element.139.refs_1_) | copy-start | bytes 1474564
  598.0 6.2 copy-start.10
  600.3 8.1 copy-start.23
  604.2 6.8 copy-start.25
  604.4 3.1 copy-start.4
  604.4 9.7 %copy-start.20 = (f32[256]{0:T(256)S(1)}, f32[256]{0:T(256)}, u32[]{:S(2)}) copy-start(f32[256]{0:T(256)} %reshape.343) | copy-start | bytes 3076
  608.4 6.9 copy-start.3
  608.8 5.2 copy-start.5
  834.0 4.1 copy-start.9
  838.2 4.3 copy-start.1
  838.2 3.4 copy-start.15
  (7 other events, 16.2 us)

commit v3 on v2

--- a/solution.py
+++ b/solution.py
@@ -1,4 +1,5 @@
 import functools
+import itertools
 import math
 
 import jax
@@ -31,88 +32,12 @@
     return (jnp.cos(phases), jnp.sin(phases))
 
 
-def rotate(values, cosine, sine_table):
-    half_dim = values.shape[-1] // 2
-    first_half = values[..., :half_dim]
-    second_half = values[..., half_dim:]
-    return jnp.concatenate(
-        [
-            first_half * cosine - second_half * sine_table,
-            second_half * cosine + first_half * sine_table,
-        ],
-        axis=-1,
-    )
-
-
-def unrotate(grads, cosine, sine_table):
-    half_dim = grads.shape[-1] // 2
-    first_half = grads[..., :half_dim]
-    second_half = grads[..., half_dim:]
-    return jnp.concatenate(
-        [
-            first_half * cosine + second_half * sine_table,
-            second_half * cosine - first_half * sine_table,
-        ],
-        axis=-1,
-    )
-
-
 def inverse_rms(values):
     return lax.rsqrt(jnp.mean(values * values, axis=-1, keepdims=True) + NORM_EPS)
 
 
 def norm_back(grad_unit, unit, inv_rms):
     return inv_rms * (grad_unit - unit * jnp.mean(grad_unit * unit, axis=-1, keepdims=True))
-
-
-def attend_forward(query_major, key_major, value_major, allowed):
-    inv_root = 1.0 / math.sqrt(query_major.shape[-1])
-
-    def one_head(operands):
-        query_head, key_head, value_head = operands
-        scores = (
-            jnp.einsum("qd,kd->qk", query_head, key_head, preferred_element_type=jnp.float32)
-            * inv_root
-        )
-        scores = jnp.where(allowed, scores, NEGATIVE)
-        row_max = jnp.max(scores, axis=-1, keepdims=True)
-        weights = jnp.exp(scores - row_max)
-        totals = jnp.sum(weights, axis=-1, keepdims=True)
-        probs_low = (weights / totals).astype(jnp.bfloat16)
-        mixed_head = jnp.dot(probs_low, value_head, preferred_element_type=jnp.float32)
-        return (mixed_head, row_max[:, 0] + jnp.log(totals[:, 0]))
-
-    return lax.map(one_head, (query_major, key_major, value_major))
-
-
-def attend_backward(query_major, key_major, value_major, grad_major, log_norm, allowed):
-    inv_root = 1.0 / math.sqrt(query_major.shape[-1])
-
-    def one_head(operands):
-        query_head, key_head, value_head, grad_head, norm_head = operands
-        scores = (
-            jnp.einsum("qd,kd->qk", query_head, key_head, preferred_element_type=jnp.float32)
-            * inv_root
-        )
-        scores = jnp.where(allowed, scores, NEGATIVE)
-        probs = jnp.exp(scores - norm_head[:, None])
-        probs_low = probs.astype(jnp.bfloat16)
-        grad_value = jnp.einsum(
-            "qk,qd->kd", probs_low, grad_head, preferred_element_type=jnp.float32
-        )
-        grad_probs = jnp.einsum(
-            "qd,kd->qk", grad_head, value_head, preferred_element_type=jnp.float32
-        )
-        inner = jnp.sum(probs * grad_probs, axis=-1, keepdims=True)
-        grad_scores = (probs * (grad_probs - inner)).astype(jnp.bfloat16)
-        grad_query = jnp.dot(grad_scores, key_head, preferred_element_type=jnp.float32) * inv_root
-        grad_key = (
-            jnp.einsum("qk,qd->kd", grad_scores, query_head, preferred_element_type=jnp.float32)
-            * inv_root
-        )
-        return (grad_query, grad_key, grad_value)
-
-    return lax.map(one_head, (query_major, key_major, value_major, grad_major, log_norm))
 
 
 BF = jnp.bfloat16
@@ -171,9 +96,13 @@
     def over_core(self):
         return self.device(core=1 - self.core)
 
-    def meet(self, high=True, low=True, side=True, core=True):
+    def meet(self, high=True, low=True, side=True, core=True, swap=False):
         barrier = pltpu.get_barrier_semaphore()
         partners = []
+        if swap:
+            partners += [
+                self.device(high=self.ahead(k), low=1 - self.low) for k in range(1, self.n_high)
+            ]
         if high:
             partners += [self.device(high=self.ahead(k)) for k in range(1, self.n_high)]
         if low:
@@ -780,6 +709,422 @@
     )(down, o_t, q_up, kv_up, small, stats)
 
 
+def attention_mask(seg_col, seg_row, valid_row):
+    length = seg_col.shape[0]
+    row = lax.broadcasted_iota(jnp.int32, (length, length), 0)
+    column = lax.broadcasted_iota(jnp.int32, (length, length), 1)
+    allowed = (
+        (seg_col[...] == seg_row[...])
+        & (column <= row)
+        & ((valid_row[...] == 1) | (column == row))
+    )
+    return jnp.where(allowed, 0.0, NEGATIVE)
+
+
+def swap_halves(values):
+    half = values.shape[1] // 2
+    return jnp.concatenate([values[:, half:], values[:, :half]], axis=1)
+
+
+def turn(values, cos_full, sin_full):
+    return values * cos_full + swap_halves(values) * sin_full
+
+
+def head_probs(query, key, bias, inv_root):
+    scores = dot_nt(query, key) * inv_root + bias
+    weights = jnp.exp(scores - jnp.max(scores, axis=-1, keepdims=True))
+    return weights / jnp.sum(weights, axis=-1, keepdims=True)
+
+
+def attend_rows(
+    x, gain_attn, gain_q, gain_kv, down, q_up, kv_up, bias, cos_full, sin_full,
+    normed, latents, q_normed, kv_normed, q_rows, kv_rows, key_rot, mixed,
+):
+    rank_q = gain_q.shape[1]
+    stream = x[...].astype(F32)
+    normed[...] = (stream * inverse_rms(stream) * gain_attn).astype(BF)
+    latents[...] = dot(normed[...], down)
+    q_latent = latents[:, :rank_q]
+    q_normed[...] = (q_latent * inverse_rms(q_latent) * gain_q).astype(BF)
+    kv_latent = latents[:, rank_q : rank_q + KR]
+    kv_normed[...] = (kv_latent * inverse_rms(kv_latent) * gain_kv).astype(BF)
+    turned = turn(latents[:, rank_q + KR : rank_q + KR + ROPE], cos_full[...], sin_full[...])
+    key_rot[...] = turned.astype(BF)
+    kv_rows[...] = dot(kv_normed[...], kv_up).astype(BF)
+    q_heads = dot(q_normed[...], q_up)
+    inv_root = 1.0 / math.sqrt(NOPE + ROPE)
+    for head in range(q_rows.shape[1] // (NOPE + ROPE)):
+        base = head * (NOPE + ROPE)
+        query = jnp.concatenate(
+            [
+                q_heads[:, base : base + NOPE],
+                turn(
+                    q_heads[:, base + NOPE : base + NOPE + ROPE], cos_full[...], sin_full[...]
+                ),
+            ],
+            axis=1,
+        ).astype(BF)
+        q_rows[:, base : base + NOPE + ROPE] = query
+        start = head * (NOPE + VD)
+        key = jnp.concatenate([kv_rows[:, start : start + NOPE], key_rot[...]], axis=1)
+        value = kv_rows[:, start + NOPE : start + NOPE + VD]
+        probs = head_probs(query, key, bias, inv_root).astype(BF)
+        mixed[:, head * VD : head * VD + VD] = dot(probs, value).astype(BF)
+
+
+def attend_kernel(
+    x, gain_attn, gain_q, gain_kv, down, q_up, kv_up, seg_col, seg_row, valid_row, cos_full, sin_full,
+    *outs,
+):
+    attend_rows(
+        x, gain_attn[...], gain_q[...], gain_kv[...], down[...], q_up[...], kv_up[...],
+        attention_mask(seg_col, seg_row, valid_row), cos_full, sin_full, *outs,
+    )
+
+
+def attend(x, gain_attn, gain_q, gain_kv, down, q_up, kv_up, segments, valid, cos_full, sin_full):
+    length = x.shape[0]
+    heads = q_up.shape[1] // (NOPE + ROPE)
+
+    def rows(columns, kind):
+        return jax.ShapeDtypeStruct((length, columns), kind)
+
+    return pl.pallas_call(
+        attend_kernel,
+        out_shape=(
+            rows(x.shape[1], BF),
+            rows(down.shape[1], F32),
+            rows(q_up.shape[0], BF),
+            rows(kv_up.shape[0], BF),
+            rows(q_up.shape[1], BF),
+            rows(kv_up.shape[1], BF),
+            rows(ROPE, BF),
+            rows(heads * VD, BF),
+        ),
+        in_specs=[VMEM] * 12,
+        out_specs=[VMEM] * 8,
+        compiler_params=pltpu.CompilerParams(vmem_limit_bytes=VMEM_BYTES),
+        name="attend",
+    )(
+        x,
+        gain_attn[None, :],
+        gain_q[None, :],
+        gain_kv[None, :],
+        down,
+        q_up,
+        kv_up,
+        segments[:, None],
+        segments[None, :],
+        valid[None, :],
+        cos_full,
+        sin_full,
+    )
+
+
+def later(stream, turns):
+    for _ in range(turns):
+        yield
+    yield from stream
+
+
+def swap_start(links, copies, blocks, out, n_dp):
+    me = links.high * 2 + links.low
+    own = copies.near(blocks.at[me], out.at[me])
+    arrive = []
+    for k in range(1, n_dp):
+        there = (me + k) % n_dp
+        arrive.append(copies.go(blocks.at[there], out.at[me], {"dp": there}))
+    return own, arrive
+
+
+def pack_stream(w_gate, w_up, w_down, packed):
+    n_dp, width, lanes = packed.shape
+    slice_ff = w_gate.shape[1] // n_dp
+    for k in range(n_dp):
+        at = k * slice_ff
+        packed[k] = jnp.concatenate(
+            [
+                w_gate[:, at : at + slice_ff],
+                w_up[:, at : at + slice_ff],
+                w_down[at : at + slice_ff, :].T,
+                jnp.zeros((width, lanes - 3 * slice_ff), BF),
+            ],
+            axis=1,
+        )
+        yield
+
+
+def front_kernel(
+    n_dp, x, x_rows, cot, down, gains, q_up, kv_up, o_t, w_gate, w_up, w_down,
+    seg_col, seg_row, valid_row, cos_full, sin_full,
+    f_down, f_o, f_q, f_kv, f_g, f_cot, f_w, f_normed,
+    normed, latents, q_normed, kv_normed, q_rows, kv_rows, key_rot, mixed, resid, branch, gain_mlp,
+    packed, part, from_core, out_side, from_side, block, send, recv, local,
+):
+    links = Links(n_dp)
+    copies = Copies(send, recv, local)
+    links.meet(swap=True)
+    o_stream = dp_gather(links, copies, o_t, f_o)
+    take_turns(
+        every_gather(links, copies, down, f_down),
+        dp_gather(links, copies, gains, f_g),
+        dp_gather(links, copies, q_up, f_q),
+        dp_gather(links, copies, kv_up, f_kv),
+        pack_stream(w_gate, w_up, w_down, packed),
+        later(itertools.islice(o_stream, 1), 7),
+    )
+
+    def gain_of(row, count):
+        return jnp.concatenate(
+            [f_g[k].astype(F32)[row : row + 1, :count] for k in range(n_dp)], axis=1
+        )
+
+    width = down.shape[0] * 4
+    full_down = f_down[...].reshape(n_dp * width, down.shape[1])
+    full_q = f_q[...].reshape(n_dp * q_up.shape[0], q_up.shape[1])
+    full_kv = f_kv[...].reshape(n_dp * kv_up.shape[0], kv_up.shape[1])
+    attend_rows(
+        x, gain_of(0, width), gain_of(1, q_up.shape[0]), gain_of(2, kv_up.shape[0]),
+        full_down, full_q, full_kv, attention_mask(seg_col, seg_row, valid_row), cos_full, sin_full,
+        normed, latents, q_normed, kv_normed, q_rows, kv_rows, key_rot, mixed,
+    )
+    for _ in range(links.n_high - 1):
+        next(o_stream)
+    own, arrive = swap_start(links, copies, packed, f_w, n_dp)
+    cot_stream = every_gather(links, copies, cot, f_cot)
+    next(cot_stream)
+    next(cot_stream)
+    take_turns(o_stream)
+    gain_mlp[...] = gain_of(3, width)
+    full_o = f_o[...].reshape(n_dp * width, o_t.shape[1])
+    rows = block.shape[0]
+    attn_part = dot_nt(mixed[...], full_o).astype(BF)
+    for side in range(2):
+        for core in range(2):
+            at = (side * 2 + core) * rows
+            part[side, core] = attn_part[at : at + rows]
+
+    def resid_stream():
+        over = copies.go(part.at[:, 1 - links.core], from_core, links.over_core())
+        over.wait_recv()
+        out_side[...] = (
+            part[1 - links.side, links.core].astype(F32) + from_core[1 - links.side].astype(F32)
+        ).astype(BF)
+        over = copies.go(out_side, from_side, links.over_side())
+        mine = part[links.side, links.core].astype(F32) + from_core[links.side].astype(F32)
+        over.wait_recv()
+        attn = RESIDUAL_SCALE * (mine + from_side[...].astype(F32))
+        stream = x_rows[...].astype(F32) + attn
+        branch[...] = attn
+        resid[...] = stream
+        block[...] = (stream * inverse_rms(stream) * gain_mlp[...]).astype(BF)
+        yield from every_gather(links, copies, block, f_normed)
+
+    take_turns(resid_stream(), cot_stream)
+    for copy in arrive:
+        copy.wait_recv()
+    own.wait()
+    copies.finish()
+
+
+def front(n_dp, x, x_rows, cot, down, gains, q_up, kv_up, o_t, w_gate, w_up, w_down, segments, valid, cos_full, sin_full):
+    n_high = n_dp // 2
+    length, columns = x.shape
+    rows = x_rows.shape[0]
+    lanes = -(-3 * (w_gate.shape[1] // n_dp) // 128) * 128
+    heads = q_up.shape[1] // (NOPE + ROPE)
+    count = 3 * count_every_gather(n_high) + 4 * (2 * n_high - 1) + n_dp + 1
+
+    def over(block, *lead, kind=BF):
+        return jax.ShapeDtypeStruct((*lead, *block), kind)
+
+    return pl.pallas_call(
+        functools.partial(front_kernel, n_dp),
+        out_shape=(
+            over(down.shape, n_dp, 4),
+            over(o_t.shape, n_dp),
+            over(q_up.shape, n_dp),
+            over(kv_up.shape, n_dp),
+            over(gains.shape, n_dp),
+            over(cot.shape, n_dp, 4),
+            over((w_gate.shape[0], lanes), n_dp),
+            over(cot.shape, n_dp, 4),
+            over((columns,), length),
+            over((down.shape[1],), length, kind=F32),
+            over((q_up.shape[0] * n_dp,), length),
+            over((kv_up.shape[0] * n_dp,), length),
+            over((q_up.shape[1],), length),
+            over((kv_up.shape[1],), length),
+            over((ROPE,), length),
+            over((heads * VD,), length),
+            over((columns,), rows, kind=F32),
+            over((columns,), rows, kind=F32),
+            over((columns,), 1, kind=F32),
+        ),
+        in_specs=[VMEM] * 16,
+        out_specs=[VMEM] * 5 + [ANY] * 3 + [VMEM] * 11,
+        scratch_shapes=[
+            pltpu.VMEM((n_dp, w_gate.shape[0], lanes), BF),
+            pltpu.VMEM((2, 2, rows, columns), BF),
+            pltpu.VMEM((2, rows, columns), BF),
+            pltpu.VMEM((rows, columns), BF),
+            pltpu.VMEM((rows, columns), BF),
+            pltpu.VMEM((rows, columns), BF),
+            *semaphores(count, 8),
+        ],
+        compiler_params=params(7),
+        name="front",
+    )(
+        x, x_rows, cot, down, gains, q_up, kv_up, o_t, w_gate, w_up, w_down,
+        segments[:, None], segments[None, :], valid[None, :], cos_full, sin_full,
+    )
+
+
+def feed_forward_kernel(slice_ff, normed, cot, weights, m_part, g_part, grads, sum_in, sum_out):
+    step = pl.program_id(0)
+    cut = slice_ff * 2 // 128 * 128
+    pad = slice_ff * 2 - cut
+    w_in, w_out = weights[:, : sum_in.shape[0]], weights[:, cut:]
+    rows = normed.shape[0]
+    both = dot(normed[...], w_in)
+    gate, upper = both[:, :slice_ff], both[:, slice_ff : 2 * slice_ff]
+    sigma = jax.nn.sigmoid(gate)
+    swish = gate * sigma
+
+    def zeros(count):
+        return jnp.zeros((rows, count), F32)
+
+    def placed(hidden):
+        rest = w_out.shape[1] - pad - slice_ff
+        return jnp.concatenate([zeros(pad), hidden, zeros(rest)], axis=1).astype(BF)
+
+    hidden = placed(swish * upper)
+    m_part[...] = dot_nt(hidden, w_out).astype(BF)
+    grad_mlp = (RESIDUAL_SCALE * cot[...].astype(F32)).astype(BF)
+    grad_hidden = dot(grad_mlp, w_out)[:, pad : pad + slice_ff]
+    grad_both = jnp.concatenate(
+        [
+            grad_hidden * upper * (sigma * (1.0 + gate * (1.0 - sigma))),
+            grad_hidden * swish,
+            zeros(w_in.shape[1] - 2 * slice_ff),
+        ],
+        axis=1,
+    ).astype(BF)
+    g_part[...] = dot_nt(grad_both, w_in).astype(BF)
+
+    @pl.when(step == 0)
+    def _():
+        sum_in[...] = dot_tn(grad_both, normed[...])
+        sum_out[...] = dot_tn(hidden, grad_mlp)
+
+    @pl.when(step > 0)
+    def _():
+        sum_in[...] += dot_tn(grad_both, normed[...])
+        sum_out[...] += dot_tn(hidden, grad_mlp)
+
+    @pl.when(step == pl.num_programs(0) - 1)
+    def _():
+        mid = sum_in.shape[0]
+        if cut:
+            grads[:, :cut] = sum_in[:cut].T.astype(BF)
+        grads[:, cut:mid] = (sum_in[cut:] + sum_out[: mid - cut]).T.astype(BF)
+        grads[:, mid:] = sum_out[mid - cut :].T.astype(BF)
+
+
+def feed_forward(normed, cot, weights, slice_ff, rows):
+    tokens, columns = normed.shape
+    lanes = weights.shape[1]
+    cut = slice_ff * 2 // 128 * 128
+    wide = -(-slice_ff * 2 // 128) * 128
+    token_block = pl.BlockSpec((rows, columns), lambda i: (i, 0))
+    whole = pl.BlockSpec((columns, lanes), lambda i: (0, 0))
+    part = jax.ShapeDtypeStruct((tokens, columns), BF)
+    return pl.pallas_call(
+        functools.partial(feed_forward_kernel, slice_ff),
+        grid=(tokens // rows,),
+        out_shape=(part, part, jax.ShapeDtypeStruct((columns, lanes), BF)),
+        in_specs=[token_block, token_block, whole],
+        out_specs=[token_block, token_block, whole],
+        scratch_shapes=[
+            pltpu.VMEM((wide, columns), F32),
+            pltpu.VMEM((lanes - cut, columns), F32),
+        ],
+        compiler_params=pltpu.CompilerParams(vmem_limit_bytes=VMEM_BYTES),
+        name="feed_forward",
+    )(normed, cot, weights)
+
+
+def attend_back_kernel(
+    grad_attn, mixed, o_t, q_rows, kv_rows, key_rot, q_normed, kv_normed, q_up, kv_up,
+    seg_col, seg_row, valid_row, cos_full, sin_full,
+    grad_latents, grad_o, grad_q_up, grad_kv_up, grad_q, grad_kv,
+):
+    rank_q = q_up.shape[0]
+    grad_o[...] = dot_tn(grad_attn[...], mixed[...]).astype(BF)
+    grad_mixed = dot(grad_attn[...], o_t[...]).astype(BF)
+    bias = attention_mask(seg_col, seg_row, valid_row)
+    inv_root = 1.0 / math.sqrt(NOPE + ROPE)
+    grad_rot = jnp.zeros((grad_attn.shape[0], ROPE), F32)
+    for head in range(q_rows.shape[1] // (NOPE + ROPE)):
+        base = head * (NOPE + ROPE)
+        start = head * (NOPE + VD)
+        query = q_rows[:, base : base + NOPE + ROPE]
+        key = jnp.concatenate([kv_rows[:, start : start + NOPE], key_rot[...]], axis=1)
+        value = kv_rows[:, start + NOPE : start + NOPE + VD]
+        grad = grad_mixed[:, head * VD : head * VD + VD]
+        probs = head_probs(query, key, bias, inv_root)
+        grad_value = dot_tn(probs.astype(BF), grad)
+        grad_probs = dot_nt(grad, value)
+        inner = jnp.sum(probs * grad_probs, axis=-1, keepdims=True)
+        grad_scores = (probs * (grad_probs - inner)).astype(BF)
+        grad_query = dot(grad_scores, key) * inv_root
+        grad_key = dot_tn(grad_scores, query) * inv_root
+        grad_q[:, base : base + NOPE + ROPE] = jnp.concatenate(
+            [grad_query[:, :NOPE], turn(grad_query[:, NOPE:], cos_full[...], -sin_full[...])],
+            axis=1,
+        ).astype(BF)
+        grad_kv[:, start : start + NOPE + VD] = jnp.concatenate(
+            [grad_key[:, :NOPE], grad_value], axis=1
+        ).astype(BF)
+        grad_rot = grad_rot + grad_key[:, NOPE:]
+    grad_latents[...] = jnp.zeros_like(grad_latents)
+    grad_latents[:, :rank_q] = dot_nt(grad_q[...], q_up[...]).astype(BF)
+    grad_latents[:, rank_q : rank_q + KR] = dot_nt(grad_kv[...], kv_up[...]).astype(BF)
+    grad_latents[:, rank_q + KR : rank_q + KR + ROPE] = turn(
+        grad_rot, cos_full[...], -sin_full[...]
+    ).astype(BF)
+    grad_q_up[...] = dot_tn(q_normed[...], grad_q[...]).astype(BF)
+    grad_kv_up[...] = dot_tn(kv_normed[...], grad_kv[...]).astype(BF)
+
+
+def attend_back(
+    grad_attn, mixed, o_t, q_rows, kv_rows, key_rot, q_normed, kv_normed, q_up, kv_up,
+    segments, valid, cos_full, sin_full, columns_down,
+):
+    length = grad_attn.shape[0]
+
+    def out(shape):
+        return jax.ShapeDtypeStruct(shape, BF)
+
+    return pl.pallas_call(
+        attend_back_kernel,
+        out_shape=(
+            out((length, columns_down)),
+            out(o_t.shape),
+            out(q_up.shape),
+            out(kv_up.shape),
+        ),
+        in_specs=[VMEM] * 15,
+        out_specs=[VMEM] * 4,
+        scratch_shapes=[pltpu.VMEM(q_rows.shape, BF), pltpu.VMEM(kv_rows.shape, BF)],
+        compiler_params=pltpu.CompilerParams(vmem_limit_bytes=VMEM_BYTES),
+        name="attend_back",
+    )(
+        grad_attn, mixed, o_t, q_rows, kv_rows, key_rot, q_normed, kv_normed, q_up, kv_up,
+        segments[:, None], segments[None, :], valid[None, :], cos_full, sin_full,
+    )
+
+
 def per_device(
     layer_input,
     segment_ids,
@@ -799,7 +1144,6 @@
     w_down,
 ):
     length = layer_input.shape[0]
-    heads_local = q_up.shape[1] // (NOPE + ROPE)
     n_dp = lax.axis_size("dp")
     n_tensor = lax.axis_size("tensor")
     share = length // n_tensor
@@ -829,19 +1173,27 @@
         return jnp.stack(padded + [jnp.zeros((lanes,), kind)] * (count - len(padded)))
 
     cot_rows = rows_of(cotangent, share)
-    f_down, f_o, f_q, f_kv, f_g, f_cot = gather_weights(
-        n_dp,
-        n_tensor,
-        down_rows,
-        o_proj.T,
-        q_up,
-        kv_up,
-        lane_rows([attn_gain, q_gain, kv_gain, mlp_gain], 16, BF),
-        cot_rows,
-    )
+    x_rows = rows_of(layer_input, share)
+    gains_block = lane_rows([attn_gain, q_gain, kv_gain, mlp_gain], 16, BF)
+    cosine, sine_table = rope_tables(length, ROPE)
+    cos_full = jnp.concatenate([cosine, cosine], axis=1)
+    sin_full = jnp.concatenate([-sine_table, sine_table], axis=1)
+    fused = n_dp == 8 and rows_down % 16 == 0 and q_up.shape[0] % 16 == 0
+    if fused:
+        (
+            f_down, f_o, f_q, f_kv, f_g, f_cot, f_w, f_normed,
+            normed, latents, q_normed, kv_normed, q_rows, kv_rows, key_rot, mixed,
+            resid_rows, attn_rows, _,
+        ) = front(
+            n_dp, layer_input, x_rows, cot_rows, down_rows, gains_block, q_up, kv_up, o_proj.T,
+            w_gate, w_up, w_down, segment_ids, valid_mask, cos_full, sin_full,
+        )
+    else:
+        f_down, f_o, f_q, f_kv, f_g, f_cot = gather_weights(
+            n_dp, n_tensor, down_rows, o_proj.T, q_up, kv_up, gains_block, cot_rows
+        )
     full_down = f_down.reshape(n_dp * width, columns_down + pad_down)
     full_o = f_o.reshape(n_dp * width, -1)
-    full_kv_up = f_kv.reshape(-1, kv_up.shape[1])
 
     def gain_of(row, gain):
         return f_g[:, row, : gain.shape[0]].reshape(-1).astype(F32)
@@ -850,142 +1202,68 @@
     gain_q = gain_of(1, q_gain)
     gain_kv = gain_of(2, kv_gain)
     gain_mlp = gain_of(3, mlp_gain)
-
-    packed = jnp.concatenate(
-        [
-            w_gate.reshape(width, n_dp, slice_ff),
-            w_up.reshape(width, n_dp, slice_ff),
-            w_down.T.reshape(width, n_dp, slice_ff),
-        ],
-        axis=2,
-    ).transpose(1, 0, 2)
-    packed, f_q = lax.optimization_barrier((packed, f_q))
-    mine = swap_dp(packed).reshape(n_dp * width, 3 * slice_ff)
+    if not fused:
+        packed = jnp.concatenate(
+            [
+                w_gate.reshape(width, n_dp, slice_ff),
+                w_up.reshape(width, n_dp, slice_ff),
+                w_down.T.reshape(width, n_dp, slice_ff),
+                jnp.zeros((width, n_dp, -3 * slice_ff % 128), BF),
+            ],
+            axis=2,
+        ).transpose(1, 0, 2)
+        packed, f_q = lax.optimization_barrier((packed, f_q))
+        f_w = swap_dp(packed)
     full_q_up = f_q.reshape(-1, q_up.shape[1])
-    w_in = mine[:, : 2 * slice_ff]
-    w_out = mine[:, 2 * slice_ff :]
-
+    full_kv_up = f_kv.reshape(-1, kv_up.shape[1])
+    if not fused:
+        normed, latents, q_normed, kv_normed, q_rows, kv_rows, key_rot, mixed = attend(
+            layer_input, gain_attn, gain_q, gain_kv, full_down, full_q_up, full_kv_up,
+            segment_ids, valid_mask, cos_full, sin_full,
+        )
+        f_normed, resid_rows, attn_rows = attention_residual(
+            n_dp, dot_nt(mixed, full_o).astype(BF), x_rows, gain_mlp[None, :]
+        )
+    inv_two = inverse_rms(resid_rows)
+    unit_two = resid_rows * inv_two
+
+    mlp_part, normed_part, grad_packed = feed_forward(
+        f_normed.reshape(n_dp * length, -1),
+        f_cot.reshape(n_dp * length, -1),
+        f_w.reshape(n_dp * width, -1),
+        slice_ff,
+        length,
+    )
+    swapped = swap_dp(grad_packed.reshape(n_dp, width, -1))
+    normed_part, grad_packed = lax.optimization_barrier((normed_part, grad_packed))
+    f_attn, grad_normed_two, f_block, mlp_rows = residual_grads(
+        n_dp, normed_part, mlp_part, resid_rows, cot_rows, gain_mlp[None, :]
+    )
+    grad_attn = f_attn.reshape(length, -1)
+    block_full = f_block.reshape(length, -1)
+
+    def unpack(part):
+        return part.transpose(1, 0, 2).reshape(width, n_dp * slice_ff).astype(F32)
+
+    weight_rows = rows_of(valid_mask.astype(F32)[:, None], share)
+    grad_mlp_gain = jnp.sum(grad_normed_two * unit_two, axis=0)
+
+    grad_part, grad_o, grad_q_up, grad_kv_up = attend_back(
+        grad_attn, mixed, full_o, q_rows, kv_rows, key_rot, q_normed, kv_normed,
+        full_q_up, full_kv_up, segment_ids, valid_mask, cos_full, sin_full,
+        columns_down + pad_down,
+    )
+    grad_part, swapped = lax.optimization_barrier((grad_part, swapped))
+    grad_latents = sum_latents(n_dp, grad_part).astype(F32)
     stream = layer_input.astype(F32)
-    cosine, sine_table = rope_tables(length, ROPE)
-    head_cos = cosine[:, None, :]
-    head_sin = sine_table[:, None, :]
     inv_one = inverse_rms(stream)
     unit_one = stream * inv_one
-    normed = (unit_one * gain_attn).astype(BF)
-    latents = dot(normed, full_down)
     q_latent = latents[:, :rank_q]
     inv_q = inverse_rms(q_latent)
     unit_q = q_latent * inv_q
-    q_normed = (unit_q * gain_q).astype(BF)
-    q_heads = dot(q_normed, full_q_up).reshape(length, heads_local, NOPE + ROPE)
-    kv_joint = latents[:, rank_q:columns_down]
-    kv_latent = kv_joint[:, :KR]
+    kv_latent = latents[:, rank_q : rank_q + KR]
     inv_kv = inverse_rms(kv_latent)
     unit_kv = kv_latent * inv_kv
-    kv_normed = (unit_kv * gain_kv).astype(BF)
-    kv_heads = dot(kv_normed, full_kv_up).reshape(length, heads_local, NOPE + VD)
-    queries = jnp.concatenate(
-        [q_heads[..., :NOPE], rotate(q_heads[..., NOPE:], head_cos, head_sin)], axis=-1
-    ).astype(BF)
-    key_rot = rotate(kv_joint[:, KR:], cosine, sine_table)
-    key_rows = jnp.concatenate(
-        [kv_heads[..., :NOPE], jnp.broadcast_to(key_rot[:, None, :], (length, heads_local, ROPE))],
-        axis=-1,
-    ).astype(BF)
-    value_rows = kv_heads[..., NOPE:].astype(BF)
-    position = jnp.arange(length)
-    allowed = (
-        (segment_ids[:, None] == segment_ids[None, :])
-        & (position[None, :] <= position[:, None])
-        & ((valid_mask[None, :] == 1) | (position[None, :] == position[:, None]))
-    )
-    query_major = queries.transpose(1, 0, 2)
-    key_major = key_rows.transpose(1, 0, 2)
-    value_major = value_rows.transpose(1, 0, 2)
-    mixed_heads, log_norm = attend_forward(query_major, key_major, value_major, allowed)
-    mixed = mixed_heads.transpose(1, 0, 2).reshape(length, heads_local * VD).astype(BF)
-    attn_part = dot_nt(mixed, full_o)
-
-    x_rows = rows_of(layer_input, share)
-    f_normed, resid_rows, attn_rows = attention_residual(
-        n_dp, attn_part.astype(BF), x_rows, gain_mlp[None, :]
-    )
-    normed_two = f_normed.reshape(n_dp * length, -1)
-    inv_two = inverse_rms(resid_rows)
-    unit_two = resid_rows * inv_two
-    grad_mlp = (RESIDUAL_SCALE * f_cot.reshape(n_dp * length, -1).astype(F32)).astype(BF)
-
-    gate_upper = dot(normed_two, w_in)
-    gate = gate_upper[:, :slice_ff]
-    upper = gate_upper[:, slice_ff:]
-    sigma = jax.nn.sigmoid(gate)
-    swish = gate * sigma
-    hidden = (swish * upper).astype(BF)
-    mlp_part = dot_nt(hidden, w_out).astype(BF)
-    grad_hidden = dot(grad_mlp, w_out)
-    grad_both = jnp.concatenate(
-        [
-            grad_hidden * upper * (sigma * (1.0 + gate * (1.0 - sigma))),
-            grad_hidden * swish,
-        ],
-        axis=1,
-    ).astype(BF)
-    normed_part = dot_nt(grad_both, w_in).astype(BF)
-    grad_packed = jnp.concatenate(
-        [dot_tn(normed_two, grad_both), dot_tn(grad_mlp, hidden)], axis=1
-    ).astype(BF)
-    swapped = swap_dp(grad_packed.reshape(n_dp, width, 3 * slice_ff))
-    normed_part, grad_packed = lax.optimization_barrier((normed_part, grad_packed))
-    f_attn, grad_normed_two, f_block, mlp_rows = residual_grads(
-        n_dp, normed_part, mlp_part, resid_rows, cot_rows, gain_mlp[None, :]
-    )
-    grad_attn = f_attn.reshape(length, -1)
-    block_full = f_block.reshape(length, -1)
-
-    def unpack(part):
-        return part.transpose(1, 0, 2).reshape(width, n_dp * slice_ff).astype(F32)
-
-    weight_rows = rows_of(valid_mask.astype(F32)[:, None], share)
-    grad_mlp_gain = jnp.sum(grad_normed_two * unit_two, axis=0)
-
-    grad_o = dot_tn(grad_attn, mixed)
-    grad_mixed = dot(grad_attn, full_o).astype(BF)
-    grad_major = grad_mixed.reshape(length, heads_local, VD).transpose(1, 0, 2)
-    grad_q_major, grad_k_major, grad_v_major = attend_backward(
-        query_major, key_major, value_major, grad_major, log_norm, allowed
-    )
-    grad_queries = grad_q_major.transpose(1, 0, 2)
-    grad_keys = grad_k_major.transpose(1, 0, 2)
-    grad_values = grad_v_major.transpose(1, 0, 2)
-    grad_q_heads = (
-        jnp.concatenate(
-            [grad_queries[..., :NOPE], unrotate(grad_queries[..., NOPE:], head_cos, head_sin)],
-            axis=-1,
-        )
-        .reshape(length, heads_local * (NOPE + ROPE))
-        .astype(BF)
-    )
-    grad_kv_heads = (
-        jnp.concatenate([grad_keys[..., :NOPE], grad_values], axis=-1)
-        .reshape(length, heads_local * (NOPE + VD))
-        .astype(BF)
-    )
-    grad_key_rot = unrotate(jnp.sum(grad_keys[..., NOPE:], axis=1), cosine, sine_table)
-    grad_q_heads, swapped = lax.optimization_barrier((grad_q_heads, swapped))
-    grad_q_up = dot_tn(q_normed, grad_q_heads)
-    grad_kv_up = dot_tn(kv_normed, grad_kv_heads)
-    grad_latents = sum_latents(
-        n_dp,
-        jnp.concatenate(
-            [
-                dot_nt(grad_q_heads, full_q_up),
-                dot_nt(grad_kv_heads, full_kv_up),
-                grad_key_rot,
-                jnp.zeros((length, pad_down), F32),
-            ],
-            axis=1,
-        ).astype(BF),
-    ).astype(F32)
     grad_q_normed = grad_latents[:, :rank_q]
     grad_kv_normed = grad_latents[:, rank_q : rank_q + KR]
     grad_kv_rot = grad_latents[:, rank_q + KR : columns_down]
@@ -1030,15 +1308,15 @@
     s_down, s_o, s_q, s_kv, s_small = sum_weight_grads(
         n_dp,
         dot_tn(quarter, grad_down).astype(BF),
-        grad_o.astype(BF),
-        grad_q_up.astype(BF),
-        grad_kv_up.astype(BF),
+        grad_o,
+        grad_q_up,
+        grad_kv_up,
         small_rows([grad_attn_gain, grad_q_gain, grad_kv_gain, grad_mlp_gain]),
         lane_rows([stats], 8, F32),
     )
     grad_w_gate = unpack(swapped[:, :, :slice_ff])
     grad_w_up = unpack(swapped[:, :, slice_ff : 2 * slice_ff])
-    grad_w_down = unpack(swapped[:, :, 2 * slice_ff :]).T
+    grad_w_down = unpack(swapped[:, :, 2 * slice_ff : 3 * slice_ff]).T
 
     d_down = s_down.reshape(width, -1).astype(F32)
     gains = s_small[me, 0]

time: 854 us -> 710 us (0.83)
  matrix products: 151 us -> 9.25 us
  Pallas kernels: 465 us -> 589 us
  local copies, waits for them, and re-layouts: 128 us -> 44.7 us
  other arithmetic: 51.8 us -> 27.3 us
  starting transfers between devices: 44.4 us -> 29.3 us
    dot_general x76 -> x0, matrix products: 98.8 us -> none  [the longest x6 24.4 us: dot(): return jnp.dot(left, right, preferred_element_type=F32)]
    pallas_call x2 -> x3, Pallas kernels: 197 us -> 294 us  [the longest x1 239 us: front(): pl.pallas_call(functools.partial(front_kernel, n_dp), out_shape=(over(dow...]
    pallas_call x1, Pallas kernels: 102 us -> 132 us  [residual_grads(): pl.pallas_call(functools.partial(grad_rows_kernel, n_dp, True), out_shape...]
    dot_general x6 -> x1, matrix products: 31.3 us -> 6.44 us  [dot_nt(): return jnp.einsum('ac,bc->ab', left, right, preferred_element_type=F32)]
    dot_general x3 -> x0, local copies, waits for them, and re-layouts: 23.9 us -> none  [the longest x2 21.3 us: dot_tn(): return jnp.einsum('ca,cb->ab', left, right, preferred_element_type=F32)]
    dynamic_update_slice x40 -> x0, local copies, waits for them, and re-layouts: 21.8 us -> none  [the longest x10 13.1 us: attend_forward(): return lax.map(one_head, (query_major, key_major, value_major))]
    dot_general x6 -> x1, matrix products: 21.2 us -> 2.8 us  [dot_tn(): return jnp.einsum('ca,cb->ab', left, right, preferred_element_type=F32)]
    all_to_all x2 -> x1, starting transfers between devices: 44.4 us -> 29.3 us  [swap_dp(): return lax.all_to_all(blocks, 'dp', 0, 0, tiled=True)]
  transfers between devices with their start and end apart: 2 -> 1, of which waited for: 0 -> 0; matrix products, arithmetic and copies ran while one was open for 23% -> 2% of each run, Pallas kernels for 6% -> 21%
where the time goes in v3:
time: 710 us; the launch traced here: 701 us
  Pallas kernels  589 us (83%)
  local copies, waits for them, and re-layouts  44.7 us (6%)
  starting transfers between devices  29.3 us (4%)
  other arithmetic  27.3 us (4%)
  matrix products  9.25 us (1%)
    pallas_call x1, Pallas kernels, front(): pl.pallas_call(functools.partial(front_kernel, n_dp), out_shape=(over(dow...  239 us
    pallas_call x1, Pallas kernels, sum_weight_grads(): pl.pallas_call(functools.partial(weight_grads_kernel, n_dp), out_shape=(j...  150 us
    pallas_call x1, Pallas kernels, residual_grads(): pl.pallas_call(functools.partial(grad_rows_kernel, n_dp, True), out_shape...  132 us
    pallas_call x1, Pallas kernels, feed_forward(): pl.pallas_call(functools.partial(feed_forward_kernel, slice_ff), grid=(to...  40.8 us
    all_to_all x1, starting transfers between devices, swap_dp(): return lax.all_to_all(blocks, 'dp', 0, 0, tiled=True)  29.3 us
  transfers between devices with their start and end apart: 1, of which 0 were waited for; matrix products, arithmetic and copies ran while one was open for 2% of the time, Pallas kernels for 21%

profile of v3, /device:TPU:1, one launch (start us, length us, event | category | flops | bytes accessed | tf_op | source)
XLA Modules:
  0.0 701.1 jit_solution(11090806646851653488)
XLA Ops:
  5.0 2.4 copy.45.w_down
  8.3 1.9 constant_dynamic-slice_fusion.3
  11.4 239.2 %front.1 = (bf16[8,4,80,1152]{3,2,1,0:T(8,128)(2,1)}, bf16[8,320,640]{2,1,0:T(8,128)(2,1)}, bf16[8,96,960]{2,1,0:T(8,128)(2,1)}, bf16[8,32,1280]{2,1,0:T(8,128)(...) custom-call(bf16[192,2560]{1,0:T(8,128)(2,1)} %x.19, ...), custom_call_target="tpu_custom_call" | custom-call | tf_op jit(solution)/shard_map/front/pallas_call | solution.py:941
  250.6 40.8 %feed_forward.1 = (bf16[1536,2560]{1,0:T(8,128)(2,1)}, bf16[1536,2560]{1,0:T(8,128)(2,1)}, bf16[2560,640]{1,0:T(8,128)(2,1)}) custom-call(bf16[1536,2560]{1,0:T(8,128)(2,1)} %bitcast.54, bf16[1536,2560]{1,0:T(8,128)(2,1)} %bitcast.53, bf16[2560,640]{1,0:T(8,128)(2,1)} %bitcast.59), custom_call_target="tpu_custom_call" | custom-call | tf_op jit(solution)/shard_map/feed_forward/pallas_call | solution.py:1042
  291.4 29.3 %all-to-all-start = ((bf16[8,320,640]{2,1,0:T(8,128)(2,1)}), bf16[8,320,640]{2,1,0:T(8,128)(2,1)S(1)}, u32[]{:S(2)}, u32[]{:S(2)}) async-start(bf16[8,320,640]{2,1,0:T(8,128)(2,1)} %bitcast.60), calls=%async_computation | async-start | bytes 6553600 | tf_op jit(solution)/shard_map/all_to_all | solution.py:60
  322.4 132.3 %residual_grads.1 = (bf16[4,48,2560]{2,1,0:T(8,128)(2,1)}, f32[48,2560]{1,0:T(8,128)}, f32[4,48,2560]{2,1,0:T(8,128)}, f32[48,2560]{1,0:T(8,128)}) custom-call(bf16[4,2,2,2,48,2560]{5,4,3,2,1,0:T(8,128)(2,1)} %bitcast.56, f32[48,2560]{1,0:T(8,128)} %get-tuple-element.58.refs_1_, bf16[48,2560]{1,0:T(8,128)(2,1)} %get-tuple-element.110.cot.refs_2_, ...), custom_call_target="tpu_custom_call" | custom-call | tf_op jit(solution)/shard_map/residual_grads/pallas_call | solution.py:558
  455.5 2.2 fusion.9
  457.7 2.7 select_maximum_fusion
  462.4 2.5 copy.52
  465.0 14.1 %attend_back.1 = (bf16[192,1152]{1,0:T(8,128)(2,1)}, bf16[2560,640]{1,0:T(8,128)(2,1)}, bf16[768,960]{1,0:T(8,128)(2,1)}, bf16[256,1280]{1,0:T(8,128)(2,1)}) custom-call(bf16[192,2560]{1,0:T(8,128)(2,1)} %bitcast.58, bf16[192,640]{1,0:T(8,128)(2,1)} %get-tuple-element.64.mixed, bf16[2560,640]{1,0:T(8,128)(2,1)} %bitcast.61, ...), custom_call_target="tpu_custom_call" | custom-call | tf_op jit(solution)/shard_map/attend_back/pallas_call | solution.py:1109
  479.0 1.8 constant_dynamic-slice_fusion
  484.1 12.1 %sum_latents.1 = bf16[2,96,1152]{2,1,0:T(8,128)(2,1)} custom-call(bf16[2,96,1152]{2,1,0:T(8,128)(2,1)} %bitcast.74), custom_call_target="tpu_custom_call" | custom-call | tf_op jit(solution)/shard_map/sum_latents/pallas_call | solution.py:606
  501.5 1.8 concatenate.17
  503.3 6.4 fusion.7
  510.1 2.8 convolution_convert_fusion
  513.6 150.1 %sum_weight_grads.1 = (bf16[4,80,1152]{2,1,0:T(8,128)(2,1)}, f32[320,640]{1,0:T(8,128)}, f32[96,960]{1,0:T(8,128)}, f32[32,1280]{1,0:T(8,128)}, f32[4,2,8,384]{3,2,1,0:T(8,128)}) custom-call(bf16[4,2,80,1152]{3,2,1,0:T(8,128)(2,1)} %bitcast.57, bf16[4,2,320,640]{3,2,1,0:T(8,128)(2,1)} %bitcast.62, bf16[4,2,96,960]{3,2,1,0:T(8,128)(2,1)} %bitcast.69, ...), custom_call_target="tpu_custom_call" | custom-call | tf_op jit(solution)/shard_map/sum_weight_grads/pallas_call | solution.py:684
  673.0 2.0 copy.58
  675.0 3.3 convert_bitcast_fusion
  679.9 2.2 reshape.241
  682.0 3.3 copy.54
  685.3 2.2 reshape.239
  687.5 3.3 copy.55
  690.7 2.2 reshape.240
  692.9 4.1 fusion.6
  (115 shorter events, 34.1 us)
Async XLA Ops:
  0.6 1.2 copy-start
  0.7 6.8 copy-start.10
  0.7 6.8 copy-start.12
  0.7 6.8 copy-start.13
  0.7 6.8 copy-start.11
  291.4 29.3 %copy-start.9 = (s32[192]{0:T(256)S(1)}, s32[192]{0:T(256)}, u32[]{:S(2)}) copy-start(s32[192]{0:T(256)} %param.18) | copy-start | bytes 2308
  291.4 192.6 %all-to-all-start = ((bf16[8,320,640]{2,1,0:T(8,128)(2,1)}), bf16[8,320,640]{2,1,0:T(8,128)(2,1)S(1)}, u32[]{:S(2)}, u32[]{:S(2)}) async-start(bf16[8,320,640]{2,1,0:T(8,128)(2,1)} %bitcast.60), calls=%async_computation | async-start | bytes 6553600 | tf_op jit(solution)/shard_map/all_to_all | solution.py:60
  322.4 133.0 %copy-start.4 = (f32[48,2560]{1,0:T(8,128)S(1)}, f32[48,2560]{1,0:T(8,128)}, u32[]{:S(2)}) copy-start(f32[48,2560]{1,0:T(8,128)} %get-tuple-element.58.refs_1_) | copy-start | bytes 1474564
  479.0 4.0 copy-start.2
  496.2 4.2 copy-start.3
  692.9 4.1 copy-start.5
  697.1 1.3 copy-start.7
  697.1 2.0 copy-start.8
  697.1 2.7 copy-start.6
  697.1 3.6 copy-start.1

commit v4 on v3

--- a/solution.py
+++ b/solution.py
@@ -169,10 +169,11 @@
     return order
 
 
-def every_gather(links, copies, block, out):
+def every_gather(links, copies, block, out, cut=None):
     n_high = links.n_high
-    cut = out.shape[-1] // 256 * 128
-    halves = (pl.ds(0, cut), pl.ds(cut, out.shape[-1] - cut))
+    columns = out.shape[-1]
+    cut = columns // 256 * 128 if cut is None else cut
+    halves = (pl.ds(0, cut), pl.ds(cut, columns - cut))
 
     def slot(high, low, side):
         return out.at[high * 2 + low, side * 2 + links.core]
@@ -203,13 +204,16 @@
         last.append(copies.go(here, here, links.over_core()))
         over_side[k].wait_recv()
         here = slot(links.behind(k), links.low, 1 - links.side)
-        part = here.at[:, halves[1]]
-        corner_b[k] = copies.go(part, part, links.over_low())
+        if cut < columns:
+            part = here.at[:, halves[1]]
+            corner_b[k] = copies.go(part, part, links.over_low())
         last.append(copies.go(here, here, links.over_core()))
 
     def third(k):
         here = slot(links.behind(k), 1 - links.low, 1 - links.side)
         for corner, half in ((corner_a, halves[0]), (corner_b, halves[1])):
+            if k not in corner:
+                continue
             corner[k].wait_recv()
             part = here.at[:, half]
             last.append(copies.go(part, part, links.over_core()))
@@ -235,6 +239,7 @@
     arrive, last = {}, []
     for k in steps_by_distance(links.n_high):
         arrive[k] = copies.go(block, mine, links.device(high=links.ahead(k)))
+    yield
     last.append(copies.go(block, mine, links.over_low()))
     yield
     for k in steps_by_distance(links.n_high):
@@ -262,90 +267,125 @@
     own.wait()
 
 
-def every_scatter(links, copies, part, bufs, result):
-    own, from_core, low_a, side_b, side_a, low_b, done, from_high = bufs
-    n_high = links.n_high
-    columns = part.shape[-1]
-    cut = columns // 256 * 128
-    half_a, half_b = pl.ds(0, cut), pl.ds(cut, columns - cut)
-    order = steps_by_distance(n_high) + [0]
-    loads, core_in, a_in, b_in, a_last, b_last, high_in = {}, {}, {}, {}, {}, {}, {}
-    for k in order:
-        there = links.ahead(k)
-        core_in[k] = copies.go(
-            part.at[there, :, :, 1 - links.core], from_core.at[k], links.over_core()
-        )
-        loads[k] = copies.near(part.at[there, :, :, links.core], own.at[k])
-    yield
-
-    def first(k):
-        core_in[k].wait_recv()
-        loads[k].wait()
+class EveryScatter:
+    def __init__(self, links, copies, part, bufs, result, cut):
+        self.links, self.copies, self.part, self.result = links, copies, part, result
+        self.own, self.chip, *bufs = bufs
+        self.low_a, self.side_a = (bufs.pop(0), bufs.pop(0)) if cut else (None, None)
+        self.side_b, self.low_b, self.done, self.from_high = bufs
+        self.cut = cut
+        self.half_a, self.half_b = pl.ds(0, cut), pl.ds(cut, part.shape[-1] - cut)
+        self.order = steps_by_distance(links.n_high) + [0]
+        self.loads, self.core_in, self.a_in, self.b_in = {}, {}, {}, {}
+        self.a_last, self.b_last, self.high_in = {}, {}, {}
+
+    def load(self, i):
+        there = self.links.ahead(self.order[i])
+        self.loads[i] = self.copies.near(
+            self.part.at[there, :, :, self.links.core], self.own.at[i % 2]
+        )
+
+    def start(self):
+        for i, k in enumerate(self.order):
+            self.core_in[k] = self.copies.go(
+                self.part.at[self.links.ahead(k), :, :, 1 - self.links.core],
+                self.chip.at[k],
+                self.links.over_core(),
+            )
+            if i < 2:
+                self.load(i)
+
+    def first(self, i):
+        links, copies, chip, k = self.links, self.copies, self.chip, self.order[i]
+        self.core_in[k].wait_recv()
+        self.loads[i].wait()
         for low in range(2):
             for side in range(2):
-                own[k, low, side] = (
-                    own[k, low, side].astype(F32) + from_core[k, low, side].astype(F32)
+                chip[k, low, side] = (
+                    self.own[i % 2, low, side].astype(F32) + chip[k, low, side].astype(F32)
                 ).astype(BF)
-        a_in[k] = copies.go(
-            own.at[k, 1 - links.low, :, :, half_a], low_a.at[k], links.over_low()
-        )
-        b_in[k] = copies.go(
-            own.at[k, :, 1 - links.side, :, half_b], side_b.at[k], links.over_side()
-        )
-
-    def second(k):
-        a_in[k].wait_recv()
-        for side in range(2):
-            low_a[k, side] = (
-                low_a[k, side].astype(F32) + own[k, links.low, side, :, half_a].astype(F32)
-            ).astype(BF)
-        a_last[k] = copies.go(low_a.at[k, 1 - links.side], side_a.at[k], links.over_side())
-        b_in[k].wait_recv()
+        if i + 2 < links.n_high:
+            self.load(i + 2)
+        if self.cut:
+            self.a_in[k] = copies.go(
+                chip.at[k, 1 - links.low, :, :, self.half_a], self.low_a.at[k], links.over_low()
+            )
+        self.b_in[k] = copies.go(
+            chip.at[k, :, 1 - links.side, :, self.half_b], self.side_b.at[k], links.over_side()
+        )
+
+    def second(self, i):
+        links, copies, chip, k = self.links, self.copies, self.chip, self.order[i]
+        low_a, side_b = self.low_a, self.side_b
+        if self.cut:
+            self.a_in[k].wait_recv()
+            for side in range(2):
+                low_a[k, side] = (
+                    low_a[k, side].astype(F32)
+                    + chip[k, links.low, side, :, self.half_a].astype(F32)
+                ).astype(BF)
+            self.a_last[k] = copies.go(
+                low_a.at[k, 1 - links.side], self.side_a.at[k], links.over_side()
+            )
+        self.b_in[k].wait_recv()
         for low in range(2):
             side_b[k, low] = (
-                side_b[k, low].astype(F32) + own[k, low, links.side, :, half_b].astype(F32)
+                side_b[k, low].astype(F32) + chip[k, low, links.side, :, self.half_b].astype(F32)
             ).astype(BF)
-        b_last[k] = copies.go(side_b.at[k, 1 - links.low], low_b.at[k], links.over_low())
-
-    def third(k):
-        a_last[k].wait_recv()
-        done[k, :, half_a] = (
-            side_a[k].astype(F32) + low_a[k, links.side].astype(F32)
-        ).astype(BF)
-        b_last[k].wait_recv()
-        done[k, :, half_b] = (
-            low_b[k].astype(F32) + side_b[k, links.low].astype(F32)
+        self.b_last[k] = copies.go(side_b.at[k, 1 - links.low], self.low_b.at[k], links.over_low())
+
+    def third(self, i):
+        links, k = self.links, self.order[i]
+        if self.cut:
+            self.a_last[k].wait_recv()
+            self.done[k, :, self.half_a] = (
+                self.side_a[k].astype(F32) + self.low_a[k, links.side].astype(F32)
+            ).astype(BF)
+        self.b_last[k].wait_recv()
+        self.done[k, :, self.half_b] = (
+            self.low_b[k].astype(F32) + self.side_b[k, links.low].astype(F32)
         ).astype(BF)
         if k:
-            high_in[k] = copies.go(
-                done.at[k], from_high.at[k - 1], links.device(high=links.ahead(k))
+            self.high_in[k] = self.copies.go(
+                self.done.at[k], self.from_high.at[k - 1], links.device(high=links.ahead(k))
             )
 
-    for i in range(n_high + 2):
-        if i < n_high:
-            first(order[i])
+    def finish(self):
+        total = self.done[0].astype(F32)
+        for k in steps_by_distance(self.links.n_high):
+            self.high_in[k].wait_recv()
+            total = total + self.from_high[k - 1].astype(F32)
+        self.result[...] = total
+
+
+def every_scatter(links, copies, part, bufs, result):
+    work = EveryScatter(links, copies, part, bufs, result, part.shape[-1] // 256 * 128)
+    work.start()
+    yield
+    for i in range(links.n_high + 2):
+        if i < links.n_high:
+            work.first(i)
             yield
-        if 0 <= i - 1 < n_high:
-            second(order[i - 1])
+        if 0 <= i - 1 < links.n_high:
+            work.second(i - 1)
             yield
         if 0 <= i - 2:
-            third(order[i - 2])
+            work.third(i - 2)
             yield
-    total = done[0].astype(F32)
-    for k in steps_by_distance(n_high):
-        high_in[k].wait_recv()
-        total = total + from_high[k - 1].astype(F32)
-    result[...] = total
-
-
-def every_scatter_scratch(n_high, rows, columns):
-    cut = columns // 256 * 128
+    work.finish()
+
+
+def every_scatter_scratch(n_high, rows, columns, cut=None):
+    cut = columns // 256 * 128 if cut is None else cut
+    over_low = [
+        pltpu.VMEM((n_high, 2, rows, cut), BF),
+        pltpu.VMEM((n_high, rows, cut), BF),
+    ]
     return [
+        pltpu.VMEM((2, 2, 2, rows, columns), BF),
         pltpu.VMEM((n_high, 2, 2, rows, columns), BF),
-        pltpu.VMEM((n_high, 2, 2, rows, columns), BF),
-        pltpu.VMEM((n_high, 2, rows, cut), BF),
+        *(over_low if cut else []),
         pltpu.VMEM((n_high, 2, rows, columns - cut), BF),
-        pltpu.VMEM((n_high, rows, cut), BF),
         pltpu.VMEM((n_high, rows, columns - cut), BF),
         pltpu.VMEM((n_high, rows, columns), BF),
         pltpu.VMEM((n_high - 1, rows, columns), BF),
@@ -395,9 +435,9 @@
     ]
 
 
-def params(number):
+def params(number, mebibytes=60):
     return pltpu.CompilerParams(
-        collective_id=number, has_side_effects=True, vmem_limit_bytes=VMEM_BYTES
+        collective_id=number, has_side_effects=True, vmem_limit_bytes=mebibytes * 1024 * 1024
     )
 
 
@@ -827,14 +867,25 @@
     yield from stream
 
 
-def swap_start(links, copies, blocks, out, n_dp):
-    me = links.high * 2 + links.low
-    own = copies.near(blocks.at[me], out.at[me])
-    arrive = []
-    for k in range(1, n_dp):
-        there = (me + k) % n_dp
-        arrive.append(copies.go(blocks.at[there], out.at[me], {"dp": there}))
-    return own, arrive
+class Swap:
+    def __init__(self, links, copies, blocks, out):
+        self.me = links.high * 2 + links.low
+        self.copies, self.blocks, self.out = copies, blocks, out
+        self.own = copies.near(blocks.at[self.me], out.at[self.me])
+        self.arrive = []
+
+    def send(self, steps):
+        n_dp = self.blocks.shape[0]
+        for k in steps:
+            there = (self.me + k) % n_dp
+            self.arrive.append(
+                self.copies.go(self.blocks.at[there], self.out.at[self.me], {"dp": there})
+            )
+
+    def finish(self):
+        for copy in self.arrive:
+            copy.wait_recv()
+        self.own.wait()
 
 
 def pack_stream(w_gate, w_up, w_down, packed):
@@ -871,7 +922,7 @@
         dp_gather(links, copies, q_up, f_q),
         dp_gather(links, copies, kv_up, f_kv),
         pack_stream(w_gate, w_up, w_down, packed),
-        later(itertools.islice(o_stream, 1), 7),
+        later(itertools.islice(o_stream, 1), 1),
     )
 
     def gain_of(row, count):
@@ -879,6 +930,9 @@
             [f_g[k].astype(F32)[row : row + 1, :count] for k in range(n_dp)], axis=1
         )
 
+    swap = Swap(links, copies, packed, f_w)
+    swap.send(range(2, n_dp, 2))
+    next(o_stream)
     width = down.shape[0] * 4
     full_down = f_down[...].reshape(n_dp * width, down.shape[1])
     full_q = f_q[...].reshape(n_dp * q_up.shape[0], q_up.shape[1])
@@ -890,8 +944,7 @@
     )
     for _ in range(links.n_high - 1):
         next(o_stream)
-    own, arrive = swap_start(links, copies, packed, f_w, n_dp)
-    cot_stream = every_gather(links, copies, cot, f_cot)
+    cot_stream = every_gather(links, copies, cot, f_cot, cot.shape[-1])
     next(cot_stream)
     next(cot_stream)
     take_turns(o_stream)
@@ -920,10 +973,11 @@
         block[...] = (stream * inverse_rms(stream) * gain_mlp[...]).astype(BF)
         yield from every_gather(links, copies, block, f_normed)
 
-    take_turns(resid_stream(), cot_stream)
-    for copy in arrive:
-        copy.wait_recv()
-    own.wait()
+    normed_stream = resid_stream()
+    next(normed_stream)
+    swap.send(range(1, n_dp, 2))
+    take_turns(normed_stream, cot_stream)
+    swap.finish()
     copies.finish()
 
 
@@ -1125,6 +1179,367 @@
     )
 
 
+class ScatterInto:
+    def __init__(self, links, copies, bufs, result):
+        self.links, self.copies, self.result = links, copies, result
+        self.part, self.from_low, self.from_high = bufs
+        self.order = steps_by_distance(links.n_high) + [0]
+        self.low_in, self.high_in = {}, {}
+
+    def start(self):
+        for k in self.order:
+            self.low_in[k] = self.copies.go(
+                self.part.at[self.links.ahead(k), 1 - self.links.low],
+                self.from_low.at[k],
+                self.links.over_low(),
+            )
+
+    def steps(self):
+        links, part = self.links, self.part
+        for k in self.order:
+            there = links.ahead(k)
+            self.low_in[k].wait_recv()
+            part[there, links.low] = (
+                part[there, links.low].astype(F32) + self.from_low[k].astype(F32)
+            ).astype(BF)
+            if k:
+                self.high_in[k] = self.copies.go(
+                    part.at[there, links.low], self.from_high.at[k - 1], links.device(high=there)
+                )
+
+    def finish(self):
+        total = self.part[self.links.high, self.links.low].astype(F32)
+        for k in steps_by_distance(self.links.n_high):
+            self.high_in[k].wait_recv()
+            total = total + self.from_high[k - 1].astype(F32)
+        self.result[...] = total.astype(self.result.dtype)
+
+
+def scatter_into_scratch(n_high, shape):
+    return [
+        pltpu.VMEM((n_high, 2, *shape), BF),
+        pltpu.VMEM((n_high, *shape), BF),
+        pltpu.VMEM((n_high - 1, *shape), BF),
+    ]
+
+
+def small_stream(links, copies, small, small_in, stats, stats_in, stats_block, small_block, small_full):
+    n_high = links.n_high
+    low_in = copies.go(
+        small.at[:, 1 - links.low], small_in.at[pl.ds(0, n_high)], links.over_low()
+    )
+    stats_low = copies.go(stats, stats_in.at[0], links.over_low())
+    yield
+    low_in.wait_recv()
+    stats_low.wait_recv()
+    for k in range(n_high):
+        small_in[k] = small_in[k] + small[k, links.low]
+    stats_block[...] = stats[...] + stats_in[0]
+    waits = []
+    for k in range(1, n_high):
+        there = links.ahead(k)
+        waits.append(
+            copies.go(small_in.at[there], small_in.at[n_high + k - 1], links.device(high=there))
+        )
+        waits.append(copies.go(stats_block, stats_in.at[k], links.device(high=there)))
+    yield
+    for wait in waits:
+        wait.wait_recv()
+    total = small_in[links.high]
+    everything = stats_block[...]
+    for k in range(1, n_high):
+        total = total + small_in[n_high + k - 1]
+        everything = everything + stats_in[k]
+    small_block[0] = total
+    small_block[1] = everything
+    yield from tensor_gather(links, copies, small_block, small_full)
+
+
+def back_kernel(
+    n_dp, g_part, m_part, w_part, resid, branch, cot, weight, x, normed, latents, q_normed, kv_normed,
+    q_rows, kv_rows, key_rot, mixed, f_down, f_o, f_q, f_kv, f_g, seg_col, seg_row, valid_row,
+    cos_full, sin_full,
+    block_full, grad_input, d_full, o_sum, q_sum, kv_sum, small_full, w_full,
+    attn_full, grad_rows, g_rows, m_rows, grad_q, grad_kv, lat, lat_in, lat_half, lat_side,
+    lat_full, d_block, small, small_in, stats, stats_in, stats_block, small_block, *rest,
+):
+    g_bufs, m_bufs = rest[:8], (rest[0], *rest[8:13])
+    d_bufs, o_bufs, q_bufs, kv_bufs = rest[13:16], rest[16:19], rest[19:22], rest[22:25]
+    links = Links(n_dp)
+    copies = Copies(*rest[25:])
+    links.meet(swap=True)
+    length = x.shape[0]
+    rank_q, rank_kv = q_normed.shape[1], kv_normed.shape[1]
+    width = o_sum.shape[0]
+
+    def gain_of(row, count):
+        return jnp.concatenate(
+            [f_g[k].astype(F32)[row : row + 1, :count] for k in range(n_dp)], axis=1
+        )
+
+    half_columns = x.shape[1] // 256 * 128
+    g = EveryScatter(links, copies, g_part, g_bufs, g_rows, half_columns)
+    m = EveryScatter(links, copies, m_part, m_bufs, m_rows, 0)
+    swap = Swap(links, copies, w_part, w_full)
+    high = range(links.n_high)
+    g.start()
+    swap.send(range(2, n_dp, 2))
+    for i in range(links.n_high + 1):
+        if i in high:
+            g.first(i)
+        if i - 1 in high:
+            g.second(i - 1)
+        if i - 2 in high:
+            g.third(i - 2)
+    m.start()
+    swap.send(range(1, n_dp, 2))
+    g.third(links.n_high - 1)
+    m.first(0)
+    m.first(1)
+    g.finish()
+    stream = resid[...]
+    inv_two = inverse_rms(stream)
+    unit_two = stream * inv_two
+    gain_mlp = gain_of(3, width)
+    grad = cot[...].astype(F32) + norm_back(g_rows[...] * gain_mlp, unit_two, inv_two)
+    grad_rows[...] = (RESIDUAL_SCALE * grad).astype(BF)
+    t_stream = tensor_gather(links, copies, grad_rows, attn_full)
+    next(t_stream)
+    m.first(2)
+    m.first(3)
+    mlp_gain = jnp.sum(g_rows[...] * unit_two, axis=0, keepdims=True)
+    bias = attention_mask(seg_col, seg_row, valid_row)
+    for _ in t_stream:
+        pass
+
+    grad_attn = attn_full[...].reshape(length, x.shape[1])
+    for k in range(n_dp):
+        o_bufs[0][k // 2, k % 2] = dot_tn(
+            grad_attn[:, k * width : k * width + width], mixed[...]
+        ).astype(BF)
+    o = ScatterInto(links, copies, o_bufs, o_sum)
+    o.start()
+
+    grad_mixed = dot(grad_attn, f_o[...].reshape(n_dp * width, mixed.shape[1])).astype(BF)
+    inv_root = 1.0 / math.sqrt(NOPE + ROPE)
+    grad_rot = jnp.zeros((length, ROPE), F32)
+    for head in range(q_rows.shape[1] // (NOPE + ROPE)):
+        base = head * (NOPE + ROPE)
+        start = head * (NOPE + VD)
+        query = q_rows[:, base : base + NOPE + ROPE]
+        key = jnp.concatenate([kv_rows[:, start : start + NOPE], key_rot[...]], axis=1)
+        value = kv_rows[:, start + NOPE : start + NOPE + VD]
+        grad_head = grad_mixed[:, head * VD : head * VD + VD]
+        probs = head_probs(query, key, bias, inv_root)
+        grad_value = dot_tn(probs.astype(BF), grad_head)
+        grad_probs = dot_nt(grad_head, value)
+        inner = jnp.sum(probs * grad_probs, axis=-1, keepdims=True)
+        grad_scores = (probs * (grad_probs - inner)).astype(BF)
+        grad_query = dot(grad_scores, key) * inv_root
+        grad_key = dot_tn(grad_scores, query) * inv_root
+        grad_q[:, base : base + NOPE + ROPE] = jnp.concatenate(
+            [grad_query[:, :NOPE], turn(grad_query[:, NOPE:], cos_full[...], -sin_full[...])],
+            axis=1,
+        ).astype(BF)
+        grad_kv[:, start : start + NOPE + VD] = jnp.concatenate(
+            [grad_key[:, :NOPE], grad_value], axis=1
+        ).astype(BF)
+        grad_rot = grad_rot + grad_key[:, NOPE:]
+
+    half = length // 2
+    lat[...] = jnp.zeros_like(lat)
+    full_q = f_q[...].reshape(rank_q, q_rows.shape[1])
+    full_kv = f_kv[...].reshape(rank_kv, kv_rows.shape[1])
+    grad_turned = turn(grad_rot, cos_full[...], -sin_full[...]).astype(BF)
+    for core in range(2):
+        at = core * half
+        lat[core, :, :rank_q] = dot_nt(grad_q[at : at + half], full_q).astype(BF)
+        lat[core, :, rank_q : rank_q + rank_kv] = dot_nt(
+            grad_kv[at : at + half], full_kv
+        ).astype(BF)
+        lat[core, :, rank_q + rank_kv : rank_q + rank_kv + ROPE] = grad_turned[at : at + half]
+    over = copies.go(lat.at[1 - links.core], lat_in, links.over_core())
+    rows_q = q_sum.shape[0]
+    for k in range(n_dp):
+        q_bufs[0][k // 2, k % 2] = dot_tn(
+            q_normed[:, k * rows_q : k * rows_q + rows_q], grad_q[...]
+        ).astype(BF)
+    q = ScatterInto(links, copies, q_bufs, q_sum)
+    q.start()
+    over.wait_recv()
+    lat_half[...] = (lat[links.core].astype(F32) + lat_in[...].astype(F32)).astype(BF)
+    over = copies.go(lat_half, lat_side, links.over_side())
+    rows_kv = kv_sum.shape[0]
+    for k in range(n_dp):
+        kv_bufs[0][k // 2, k % 2] = dot_tn(
+            kv_normed[:, k * rows_kv : k * rows_kv + rows_kv], grad_kv[...]
+        ).astype(BF)
+    kv = ScatterInto(links, copies, kv_bufs, kv_sum)
+    kv.start()
+    over.wait_recv()
+    lat_full[links.core] = (lat_half[...].astype(F32) + lat_side[...].astype(F32)).astype(BF)
+    mine = lat_full.at[links.core]
+    over = copies.go(mine, mine, links.over_core())
+    q_latent = latents[:, :rank_q]
+    inv_q = inverse_rms(q_latent)
+    unit_q = q_latent * inv_q
+    kv_latent = latents[:, rank_q : rank_q + rank_kv]
+    inv_kv = inverse_rms(kv_latent)
+    unit_kv = kv_latent * inv_kv
+    over.wait_recv()
+    lat_sum = lat_full[...].reshape(length, lat.shape[2]).astype(F32)
+    grad_q_latent, grad_kv_latent = lat_sum[:, :rank_q], lat_sum[:, rank_q : rank_q + rank_kv]
+    q_gain = jnp.sum(grad_q_latent * unit_q, axis=0, keepdims=True)
+    kv_gain = jnp.sum(grad_kv_latent * unit_kv, axis=0, keepdims=True)
+    grad_down = jnp.concatenate(
+        [
+            norm_back(grad_q_latent * gain_of(1, rows_q), unit_q, inv_q),
+            norm_back(grad_kv_latent * gain_of(2, rows_kv), unit_kv, inv_kv),
+            lat_sum[:, rank_q + rank_kv :],
+        ],
+        axis=1,
+    ).astype(BF)
+
+    rows_down = d_block.shape[0]
+    m.second(0)
+    m.second(1)
+    copies.near(normed, g_bufs[0].at[0]).wait()
+    normed_rows = g_bufs[0][0].reshape(length, x.shape[1])
+    rank = links.side * 2 + links.core
+    for k in range(n_dp):
+        rows_all = dot_tn(normed_rows[:, k * width : k * width + width], grad_down)
+        mine = rows_all[:rows_down]
+        for quarter in range(1, 4):
+            at = quarter * rows_down
+            mine = jnp.where(rank == quarter, rows_all[at : at + rows_down], mine)
+        d_bufs[0][k // 2, k % 2] = mine.astype(BF)
+
+    d = ScatterInto(links, copies, d_bufs, d_block)
+    d.start()
+    o.steps()
+    m.second(2)
+    m.second(3)
+    grad_input[...] = dot_nt(grad_down, f_down[...].reshape(n_dp * width, grad_down.shape[1]))
+    q.steps()
+    kv.steps()
+    for i in high:
+        m.third(i)
+    d.steps()
+    m.finish()
+    mlp = RESIDUAL_SCALE * m_rows[...]
+    g_rows[...] = resid[...] + mlp
+    block_gather = tensor_gather(links, copies, g_rows, block_full)
+    next(block_gather)
+    weights = weight[...]
+    lane = lax.broadcasted_iota(jnp.int32, stats.shape, 1)
+    sums = [
+        jnp.sum(jnp.sum(weights * rows * rows, axis=1, keepdims=True), axis=0, keepdims=True)
+        for rows in (resid[...], branch[...], mlp)
+    ] + [jnp.sum(weights, axis=0, keepdims=True)]
+    packed = jnp.zeros(stats.shape, F32)
+    for index, value in enumerate(sums):
+        packed = jnp.where(lane == index, value, packed)
+    stats[...] = packed
+    stream = x[...].astype(F32)
+    inv_one = inverse_rms(stream)
+    unit_one = stream * inv_one
+    attn_gain = jnp.sum(grad_input[...] * unit_one, axis=0, keepdims=True)
+    grad_input[...] = grad_attn.astype(F32) * (1.0 / RESIDUAL_SCALE) + norm_back(
+        grad_input[...] * gain_of(0, width), unit_one, inv_one
+    )
+
+    def piece(vector, k):
+        count = vector.shape[1] // n_dp
+        cut = vector[:, k * count : k * count + count]
+        return jnp.concatenate([cut, jnp.zeros((1, small.shape[3] - count), F32)], axis=1)
+
+    for k in range(n_dp):
+        small[k // 2, k % 2] = jnp.concatenate(
+            [piece(v, k) for v in (attn_gain, q_gain, kv_gain, mlp_gain)]
+            + [jnp.zeros((4, small.shape[3]), F32)],
+            axis=0,
+        )
+    small_rows = small_stream(
+        links, copies, small, small_in, stats, stats_in, stats_block, small_block, small_full
+    )
+    next(small_rows)
+    d.finish()
+    down_gather = tensor_gather(links, copies, d_block, d_full)
+    take_turns(small_rows, down_gather, block_gather)
+    o.finish()
+    q.finish()
+    kv.finish()
+    swap.finish()
+    copies.finish()
+
+
+def back(
+    n_dp, g_part, m_part, w_part, resid, branch, cot, weight, x, normed, latents, q_normed, kv_normed,
+    q_rows, kv_rows, key_rot, mixed, f_down, f_o, f_q, f_kv, f_g, segments, valid, cos_full, sin_full,
+):
+    n_high = n_dp // 2
+    rows, columns = resid.shape
+    length = x.shape[0]
+    lanes = f_g.shape[2]
+    half = (length // 2, latents.shape[1])
+    shape = (n_high, 2, 2, 2, rows, columns)
+    d_shape, o_shape, q_shape, kv_shape = f_down.shape[2:], f_o.shape[1:], f_q.shape[1:], f_kv.shape[1:]
+    one = (8, lanes)
+    count = 2 * (6 * n_high - 1) + 4 * (2 * n_high - 1) + 4 * 3 + (n_dp - 1) + 2 * n_high + 3
+
+    def out(shape, kind=F32):
+        return jax.ShapeDtypeStruct(shape, kind)
+
+    return pl.pallas_call(
+        functools.partial(back_kernel, n_dp),
+        out_shape=(
+            out((4, rows, columns)),
+            out((length, columns)),
+            out((4, *d_shape), BF),
+            out(o_shape),
+            out(q_shape),
+            out(kv_shape),
+            out((4, 2, *one)),
+            out(w_part.shape, BF),
+        ),
+        in_specs=[ANY] * 3 + [VMEM] * 5 + [ANY] + [VMEM] * 17,
+        out_specs=[ANY] + [VMEM] * 6 + [ANY],
+        scratch_shapes=[
+            pltpu.VMEM((4, rows, columns), BF),
+            pltpu.VMEM((rows, columns), BF),
+            pltpu.VMEM((rows, columns), F32),
+            pltpu.VMEM((rows, columns), F32),
+            pltpu.VMEM(q_rows.shape, BF),
+            pltpu.VMEM(kv_rows.shape, BF),
+            pltpu.VMEM((2, *half), BF),
+            pltpu.VMEM(half, BF),
+            pltpu.VMEM(half, BF),
+            pltpu.VMEM(half, BF),
+            pltpu.VMEM((2, *half), BF),
+            pltpu.VMEM(d_shape, BF),
+            pltpu.VMEM((n_high, 2, *one), F32),
+            pltpu.VMEM((2 * n_high - 1, *one), F32),
+            pltpu.VMEM(one, F32),
+            pltpu.VMEM((n_high, *one), F32),
+            pltpu.VMEM(one, F32),
+            pltpu.VMEM((2, *one), F32),
+            *every_scatter_scratch(n_high, rows, columns),
+            *every_scatter_scratch(n_high, rows, columns, 0)[1:],
+            *scatter_into_scratch(n_high, d_shape),
+            *scatter_into_scratch(n_high, o_shape),
+            *scatter_into_scratch(n_high, q_shape),
+            *scatter_into_scratch(n_high, kv_shape),
+            *semaphores(count, 2 * n_high + 6),
+        ],
+        compiler_params=params(8, 62),
+        name="back",
+    )(
+        g_part.reshape(shape), m_part.reshape(shape), w_part, resid, branch, cot, weight, x,
+        normed.reshape(2, 2, rows, columns), latents, q_normed, kv_normed, q_rows, kv_rows, key_rot, mixed, f_down, f_o, f_q, f_kv, f_g,
+        segments[:, None], segments[None, :], valid[None, :], cos_full, sin_full,
+    )
+
+
 def per_device(
     layer_input,
     segment_ids,
@@ -1224,9 +1639,6 @@
         f_normed, resid_rows, attn_rows = attention_residual(
             n_dp, dot_nt(mixed, full_o).astype(BF), x_rows, gain_mlp[None, :]
         )
-    inv_two = inverse_rms(resid_rows)
-    unit_two = resid_rows * inv_two
-
     mlp_part, normed_part, grad_packed = feed_forward(
         f_normed.reshape(n_dp * length, -1),
         f_cot.reshape(n_dp * length, -1),
@@ -1234,86 +1646,97 @@
         slice_ff,
         length,
     )
-    swapped = swap_dp(grad_packed.reshape(n_dp, width, -1))
-    normed_part, grad_packed = lax.optimization_barrier((normed_part, grad_packed))
-    f_attn, grad_normed_two, f_block, mlp_rows = residual_grads(
-        n_dp, normed_part, mlp_part, resid_rows, cot_rows, gain_mlp[None, :]
-    )
-    grad_attn = f_attn.reshape(length, -1)
-    block_full = f_block.reshape(length, -1)
+    weight_rows = rows_of(valid_mask.astype(F32)[:, None], share)
+    if fused:
+        f_block, grad_input, s_down, s_o, s_q, s_kv, s_small, swapped = back(
+            n_dp, normed_part, mlp_part, grad_packed.reshape(n_dp, width, -1), resid_rows, attn_rows,
+            cot_rows, weight_rows, layer_input, normed, latents, q_normed, kv_normed, q_rows, kv_rows,
+            key_rot, mixed, f_down, f_o, f_q, f_kv, f_g, segment_ids, valid_mask, cos_full, sin_full,
+        )
+        block_full = f_block.reshape(length, -1)
+    else:
+        inv_two = inverse_rms(resid_rows)
+        unit_two = resid_rows * inv_two
+        swapped = swap_dp(grad_packed.reshape(n_dp, width, -1))
+        normed_part, grad_packed = lax.optimization_barrier((normed_part, grad_packed))
+        f_attn, grad_normed_two, f_block, mlp_rows = residual_grads(
+            n_dp, normed_part, mlp_part, resid_rows, cot_rows, gain_mlp[None, :]
+        )
+        grad_attn = f_attn.reshape(length, -1)
+        block_full = f_block.reshape(length, -1)
+
+        grad_mlp_gain = jnp.sum(grad_normed_two * unit_two, axis=0)
+
+        grad_part, grad_o, grad_q_up, grad_kv_up = attend_back(
+            grad_attn, mixed, full_o, q_rows, kv_rows, key_rot, q_normed, kv_normed,
+            full_q_up, full_kv_up, segment_ids, valid_mask, cos_full, sin_full,
+            columns_down + pad_down,
+        )
+        grad_part, swapped = lax.optimization_barrier((grad_part, swapped))
+        grad_latents = sum_latents(n_dp, grad_part).astype(F32)
+        stream = layer_input.astype(F32)
+        inv_one = inverse_rms(stream)
+        unit_one = stream * inv_one
+        q_latent = latents[:, :rank_q]
+        inv_q = inverse_rms(q_latent)
+        unit_q = q_latent * inv_q
+        kv_latent = latents[:, rank_q : rank_q + KR]
+        inv_kv = inverse_rms(kv_latent)
+        unit_kv = kv_latent * inv_kv
+        grad_q_normed = grad_latents[:, :rank_q]
+        grad_kv_normed = grad_latents[:, rank_q : rank_q + KR]
+        grad_kv_rot = grad_latents[:, rank_q + KR : columns_down]
+        grad_q_gain = jnp.sum(grad_q_normed * unit_q, axis=0)
+        grad_kv_gain = jnp.sum(grad_kv_normed * unit_kv, axis=0)
+        grad_down = jnp.concatenate(
+            [
+                norm_back(grad_q_normed * gain_q, unit_q, inv_q),
+                norm_back(grad_kv_normed * gain_kv, unit_kv, inv_kv),
+                grad_kv_rot,
+                jnp.zeros((length, pad_down), F32),
+            ],
+            axis=-1,
+        ).astype(BF)
+        grad_normed = dot_nt(grad_down, full_down)
+        grad_attn_gain = jnp.sum(grad_normed * unit_one, axis=0)
+        grad_input = grad_attn.astype(F32) * (1.0 / RESIDUAL_SCALE) + norm_back(
+            grad_normed * gain_attn, unit_one, inv_one
+        )
+
+        quarter = lax.dynamic_index_in_dim(
+            normed.reshape(length, n_dp, n_tensor, rows_down), me, 2, keepdims=False
+        ).reshape(length, n_dp * rows_down)
+        def by_dp(vector):
+            return vector.reshape(n_dp, -1)
+
+        def small_rows(vectors):
+            return jnp.stack(
+                [jnp.pad(by_dp(v), ((0, 0), (0, lanes - v.shape[0] // n_dp))) for v in vectors]
+                + [jnp.zeros((n_dp, lanes), F32)] * (8 - len(vectors)),
+                axis=1,
+            )
+
+        stats = jnp.stack(
+            [
+                jnp.sum(weight_rows * resid_rows * resid_rows),
+                jnp.sum(weight_rows * attn_rows * attn_rows),
+                jnp.sum(weight_rows * mlp_rows * mlp_rows),
+                jnp.sum(weight_rows),
+            ]
+        )
+        s_down, s_o, s_q, s_kv, s_small = sum_weight_grads(
+            n_dp,
+            dot_tn(quarter, grad_down).astype(BF),
+            grad_o,
+            grad_q_up,
+            grad_kv_up,
+            small_rows([grad_attn_gain, grad_q_gain, grad_kv_gain, grad_mlp_gain]),
+            lane_rows([stats], 8, F32),
+        )
 
     def unpack(part):
         return part.transpose(1, 0, 2).reshape(width, n_dp * slice_ff).astype(F32)
 
-    weight_rows = rows_of(valid_mask.astype(F32)[:, None], share)
-    grad_mlp_gain = jnp.sum(grad_normed_two * unit_two, axis=0)
-
-    grad_part, grad_o, grad_q_up, grad_kv_up = attend_back(
-        grad_attn, mixed, full_o, q_rows, kv_rows, key_rot, q_normed, kv_normed,
-        full_q_up, full_kv_up, segment_ids, valid_mask, cos_full, sin_full,
-        columns_down + pad_down,
-    )
-    grad_part, swapped = lax.optimization_barrier((grad_part, swapped))
-    grad_latents = sum_latents(n_dp, grad_part).astype(F32)
-    stream = layer_input.astype(F32)
-    inv_one = inverse_rms(stream)
-    unit_one = stream * inv_one
-    q_latent = latents[:, :rank_q]
-    inv_q = inverse_rms(q_latent)
-    unit_q = q_latent * inv_q
-    kv_latent = latents[:, rank_q : rank_q + KR]
-    inv_kv = inverse_rms(kv_latent)
-    unit_kv = kv_latent * inv_kv
-    grad_q_normed = grad_latents[:, :rank_q]
-    grad_kv_normed = grad_latents[:, rank_q : rank_q + KR]
-    grad_kv_rot = grad_latents[:, rank_q + KR : columns_down]
-    grad_q_gain = jnp.sum(grad_q_normed * unit_q, axis=0)
-    grad_kv_gain = jnp.sum(grad_kv_normed * unit_kv, axis=0)
-    grad_down = jnp.concatenate(
-        [
-            norm_back(grad_q_normed * gain_q, unit_q, inv_q),
-            norm_back(grad_kv_normed * gain_kv, unit_kv, inv_kv),
-            grad_kv_rot,
-            jnp.zeros((length, pad_down), F32),
-        ],
-        axis=-1,
-    ).astype(BF)
-    grad_normed = dot_nt(grad_down, full_down)
-    grad_attn_gain = jnp.sum(grad_normed * unit_one, axis=0)
-    grad_input = grad_attn.astype(F32) * (1.0 / RESIDUAL_SCALE) + norm_back(
-        grad_normed * gain_attn, unit_one, inv_one
-    )
-
-    quarter = lax.dynamic_index_in_dim(
-        normed.reshape(length, n_dp, n_tensor, rows_down), me, 2, keepdims=False
-    ).reshape(length, n_dp * rows_down)
-    def by_dp(vector):
-        return vector.reshape(n_dp, -1)
-
-    def small_rows(vectors):
-        return jnp.stack(
-            [jnp.pad(by_dp(v), ((0, 0), (0, lanes - v.shape[0] // n_dp))) for v in vectors]
-            + [jnp.zeros((n_dp, lanes), F32)] * (8 - len(vectors)),
-            axis=1,
-        )
-
-    stats = jnp.stack(
-        [
-            jnp.sum(weight_rows * resid_rows * resid_rows),
-            jnp.sum(weight_rows * attn_rows * attn_rows),
-            jnp.sum(weight_rows * mlp_rows * mlp_rows),
-            jnp.sum(weight_rows),
-        ]
-    )
-    s_down, s_o, s_q, s_kv, s_small = sum_weight_grads(
-        n_dp,
-        dot_tn(quarter, grad_down).astype(BF),
-        grad_o,
-        grad_q_up,
-        grad_kv_up,
-        small_rows([grad_attn_gain, grad_q_gain, grad_kv_gain, grad_mlp_gain]),
-        lane_rows([stats], 8, F32),
-    )
     grad_w_gate = unpack(swapped[:, :, :slice_ff])
     grad_w_up = unpack(swapped[:, :, slice_ff : 2 * slice_ff])
     grad_w_down = unpack(swapped[:, :, 2 * slice_ff : 3 * slice_ff]).T

time: 710 us -> 573 us (0.81)
  Pallas kernels: 589 us -> 516 us
  starting transfers between devices: 29.3 us -> 0 us
  other arithmetic: 27.3 us -> 9.66 us
  matrix products: 9.25 us -> 0 us
  local copies, waits for them, and re-layouts: 44.7 us -> 36.7 us
    pallas_call x4 -> x1, Pallas kernels: 309 us -> 250 us  [back(): pl.pallas_call(functools.partial(back_kernel, n_dp), out_shape=(out((4, r...]
    all_to_all x1 -> x0, starting transfers between devices: 29.3 us -> none  [swap_dp(): return lax.all_to_all(blocks, 'dp', 0, 0, tiled=True)]
    pallas_call x1, Pallas kernels: 239 us -> 225 us  [front(): pl.pallas_call(functools.partial(front_kernel, n_dp), out_shape=(over(dow...]
    dot_general x2 -> x0, matrix products: 9.25 us -> none  [the longest x1 6.44 us: dot_nt(): return jnp.einsum('ac,bc->ab', left, right, preferred_element_type=F32)]
  transfers between devices with their start and end apart: 1 -> 0, of which waited for: 0 -> 0; matrix products, arithmetic and copies ran while one was open for 2% -> 0% of each run, Pallas kernels for 21% -> 0%
where the time goes in v4:
time: 573 us; the launch traced here: 564 us
  Pallas kernels  516 us (90%)
  local copies, waits for them, and re-layouts  36.7 us (6%)
  other arithmetic  9.66 us (2%)
    pallas_call x1, Pallas kernels, back(): pl.pallas_call(functools.partial(back_kernel, n_dp), out_shape=(out((4, r...  250 us
    pallas_call x1, Pallas kernels, front(): pl.pallas_call(functools.partial(front_kernel, n_dp), out_shape=(over(dow...  225 us
    pallas_call x1, Pallas kernels, feed_forward(): pl.pallas_call(functools.partial(feed_forward_kernel, slice_ff), grid=(to...  40.9 us

profile of v4, /device:TPU:1, one launch (start us, length us, event | category | flops | bytes accessed | tf_op | source)
XLA Modules:
  0.0 564.4 jit_solution(13847669336854725659)
XLA Ops:
  0.7 1.1 constant_dynamic-slice_fusion
  2.0 0.8 concatenate.9.down
  2.8 1.9 constant_dynamic-slice_fusion.2
  6.3 1.4 copy.46.seg_col
  7.7 1.5 copy.45.w_down
  9.4 1.2 stack.27.gains
  10.6 225.2 %front.1 = (bf16[8,4,80,1152]{3,2,1,0:T(8,128)(2,1)}, bf16[8,320,640]{2,1,0:T(8,128)(2,1)}, bf16[8,96,960]{2,1,0:T(8,128)(2,1)}, bf16[8,32,1280]{2,1,0:T(8,128)(...) custom-call(bf16[192,2560]{1,0:T(8,128)(2,1)} %x.11, ...), custom_call_target="tpu_custom_call" | custom-call | tf_op jit(solution)/shard_map/front/pallas_call | solution.py:995
  235.8 40.9 %feed_forward.1 = (bf16[1536,2560]{1,0:T(8,128)(2,1)}, bf16[1536,2560]{1,0:T(8,128)(2,1)}, bf16[2560,640]{1,0:T(8,128)(2,1)}) custom-call(bf16[1536,2560]{1,0:T(8,128)(2,1)} %bitcast.34, bf16[1536,2560]{1,0:T(8,128)(2,1)} %bitcast.33, bf16[2560,640]{1,0:T(8,128)(2,1)} %bitcast.38), custom_call_target="tpu_custom_call" | custom-call | tf_op jit(solution)/shard_map/feed_forward/pallas_call | solution.py:1096
  277.5 250.3 %back.1 = (f32[4,48,2560]{2,1,0:T(8,128)}, f32[192,2560]{1,0:T(8,128)}, bf16[4,80,1152]{2,1,0:T(8,128)(2,1)}, f32[320,640]{1,0:T(8,128)}, f32[96,960]{1,0:T(8,12...) custom-call(bf16[4,2,2,2,48,2560]{5,4,3,2,1,0:T(8,128)(2,1)} %bitcast.36, ...), custom_call_target="tpu_custom_call" | custom-call | tf_op jit(solution)/shard_map/back/pallas_call | solution.py:1493
  530.2 5.6 convert_bitcast_fusion
  535.9 1.5 copy.56
  537.4 2.2 reshape.85
  539.6 3.3 copy.54
  542.8 2.4 reshape.83
  545.2 3.3 copy.55
  548.5 2.2 reshape.84
  550.6 1.2 bitcast_convert_fusion
  551.9 1.0 slice.53
  552.9 1.0 copy.58
  556.2 1.4 slice_reduce_fusion
  557.6 3.0 copy.64
  560.6 1.3 copy.65
  561.9 0.7 copy.66
  563.3 0.9 copy.68
  (54 shorter events, 7.6 us)
Async XLA Ops:
  0.6 1.3 copy-start
  0.7 7.1 %copy-start.3 = (bf16[1600,320]{0,1:T(8,128)(2,1)S(1)}, bf16[1600,320]{0,1:T(8,128)(2,1)}, u32[]{:S(2)}) copy-start(bf16[1600,320]{0,1:T(8,128)(2,1)} %param.31) | copy-start | bytes 3072004
  0.7 8.6 %copy-start.8 = (bf16[320]{0:T(512)(128)(2,1)S(1)}, bf16[320]{0:T(512)(128)(2,1)}, u32[]{:S(2)}) copy-start(bf16[320]{0:T(512)(128)(2,1)} %param.20) | copy-start | bytes 1924
  0.7 8.6 %copy-start.10 = (bf16[96]{0:T(256)(128)(2,1)S(1)}, bf16[96]{0:T(256)(128)(2,1)}, u32[]{:S(2)}) copy-start(bf16[96]{0:T(256)(128)(2,1)} %param.22) | copy-start | bytes 580
  0.7 8.6 %copy-start.11 = (bf16[32]{0:T(256)(128)(2,1)S(1)}, bf16[32]{0:T(256)(128)(2,1)}, u32[]{:S(2)}) copy-start(bf16[32]{0:T(256)(128)(2,1)} %param.25) | copy-start | bytes 196
  0.7 8.6 %copy-start.9 = (bf16[320]{0:T(512)(128)(2,1)S(1)}, bf16[320]{0:T(512)(128)(2,1)}, u32[]{:S(2)}) copy-start(bf16[320]{0:T(512)(128)(2,1)} %param.28) | copy-start | bytes 1924
  235.8 40.9 %copy-start.7 = (s32[192]{0:T(256)S(1)}, s32[192]{0:T(256)}, u32[]{:S(2)}) copy-start(s32[192]{0:T(256)} %param.18) | copy-start | bytes 2308
  552.9 7.7 %copy-start.2 = (f32[192,2560]{1,0:T(8,128)S(1)}, f32[192,2560]{1,0:T(8,128)}, u32[]{:S(2)}) copy-start(f32[192,2560]{1,0:T(8,128)} %get-tuple-element.99) | copy-start | bytes 5898244
  557.6 6.6 %copy-start.1 = (bf16[320,768]{1,0:T(8,128)(2,1)S(1)}, bf16[320,768]{1,0:T(8,128)(2,1)}, u32[]{:S(2)}) copy-start(bf16[320,768]{1,0:T(8,128)(2,1)} %param.21) | copy-start | bytes 1474564
  560.6 1.3 copy-start.5
  560.6 2.0 copy-start.6
  560.6 2.7 copy-start.4

commit v5 on v4

--- a/solution.py
+++ b/solution.py
@@ -144,6 +144,10 @@
         self.local_started.append(copy)
         return copy
 
+    def sent(self, copy):
+        copy.wait_send()
+        self.started = [other for other in self.started if other is not copy]
+
     def finish(self):
         for copy in self.started:
             copy.wait_send()
@@ -169,68 +173,97 @@
     return order
 
 
+class EveryGather:
+    def __init__(self, links, copies, block, out, cut=None):
+        self.links, self.copies, self.block, self.out = links, copies, block, out
+        self.columns = out.shape[-1]
+        self.cut = self.columns // 256 * 128 if cut is None else cut
+        self.order = [0] + steps_by_distance(links.n_high)
+        self.arrive, self.over_low, self.over_side = {}, {}, {}
+        self.corners = {k: [] for k in self.order}
+        self.last = {k: [] for k in self.order}
+
+    def slot(self, high, low, side):
+        return self.out.at[high * 2 + low, side * 2 + self.links.core]
+
+    def start(self):
+        links = self.links
+        mine = self.slot(links.high, links.low, links.side)
+        self.own = self.copies.near(self.block, mine)
+        for k in self.order[1:]:
+            self.arrive[k] = self.copies.go(
+                self.block, mine, links.device(high=links.ahead(k))
+            )
+
+    def to_core(self, k, source, target):
+        self.last[k].append(self.copies.go(source, target, self.links.over_core()))
+
+    def first(self, i):
+        links, k = self.links, self.order[i]
+        here = self.slot(links.behind(k), links.low, links.side)
+        if k:
+            self.arrive[k].wait_recv()
+        source = here if k else self.block
+        self.over_low[k] = self.copies.go(source, here, links.over_low())
+        self.over_side[k] = self.copies.go(source, here, links.over_side())
+        self.to_core(k, source, here)
+
+    def second(self, i):
+        links, k = self.links, self.order[i]
+        self.over_low[k].wait_recv()
+        here = self.slot(links.behind(k), 1 - links.low, links.side)
+        if self.cut:
+            half = pl.ds(0, self.cut)
+            part = here.at[:, half]
+            self.corners[k].append((self.copies.go(part, part, links.over_side()), half))
+        self.to_core(k, here, here)
+        self.over_side[k].wait_recv()
+        here = self.slot(links.behind(k), links.low, 1 - links.side)
+        if self.cut < self.columns:
+            half = pl.ds(self.cut, self.columns - self.cut)
+            part = here.at[:, half]
+            self.corners[k].append((self.copies.go(part, part, links.over_low()), half))
+        self.to_core(k, here, here)
+
+    def third(self, i):
+        links, k = self.links, self.order[i]
+        here = self.slot(links.behind(k), 1 - links.low, 1 - links.side)
+        for corner, half in self.corners[k]:
+            corner.wait_recv()
+            part = here.at[:, half]
+            self.to_core(k, part, part)
+
+    def fourth(self, i):
+        k = self.order[i]
+        for copy in self.last[k]:
+            copy.wait_recv()
+        if k == 0:
+            self.own.wait()
+
+    def sent(self):
+        copies = [*self.arrive.values(), *self.over_low.values(), *self.over_side.values()]
+        copies += [corner for pairs in self.corners.values() for corner, _ in pairs]
+        copies += [copy for last in self.last.values() for copy in last]
+        for copy in copies:
+            self.copies.sent(copy)
+
+
 def every_gather(links, copies, block, out, cut=None):
-    n_high = links.n_high
-    columns = out.shape[-1]
-    cut = columns // 256 * 128 if cut is None else cut
-    halves = (pl.ds(0, cut), pl.ds(cut, columns - cut))
-
-    def slot(high, low, side):
-        return out.at[high * 2 + low, side * 2 + links.core]
-
-    mine = slot(links.high, links.low, links.side)
-    own = copies.near(block, mine)
-    arrive = {}
-    for k in steps_by_distance(n_high):
-        arrive[k] = copies.go(block, mine, links.device(high=links.ahead(k)))
+    work = EveryGather(links, copies, block, out, cut)
+    work.start()
     yield
-    order = [0] + steps_by_distance(n_high)
-    last, over_low, over_side, corner_a, corner_b = [], {}, {}, {}, {}
-
-    def first(k):
-        here = slot(links.behind(k), links.low, links.side)
-        if k:
-            arrive[k].wait_recv()
-        source = here if k else block
-        over_low[k] = copies.go(source, here, links.over_low())
-        over_side[k] = copies.go(source, here, links.over_side())
-        last.append(copies.go(source, here, links.over_core()))
-
-    def second(k):
-        over_low[k].wait_recv()
-        here = slot(links.behind(k), 1 - links.low, links.side)
-        part = here.at[:, halves[0]]
-        corner_a[k] = copies.go(part, part, links.over_side())
-        last.append(copies.go(here, here, links.over_core()))
-        over_side[k].wait_recv()
-        here = slot(links.behind(k), links.low, 1 - links.side)
-        if cut < columns:
-            part = here.at[:, halves[1]]
-            corner_b[k] = copies.go(part, part, links.over_low())
-        last.append(copies.go(here, here, links.over_core()))
-
-    def third(k):
-        here = slot(links.behind(k), 1 - links.low, 1 - links.side)
-        for corner, half in ((corner_a, halves[0]), (corner_b, halves[1])):
-            if k not in corner:
-                continue
-            corner[k].wait_recv()
-            part = here.at[:, half]
-            last.append(copies.go(part, part, links.over_core()))
-
-    for i in range(n_high + 2):
-        if i < n_high:
-            first(order[i])
+    for i in range(links.n_high + 2):
+        if i < links.n_high:
+            work.first(i)
             yield
-        if 0 <= i - 1 < n_high:
-            second(order[i - 1])
+        if 0 <= i - 1 < links.n_high:
+            work.second(i - 1)
             yield
         if 0 <= i - 2:
-            third(order[i - 2])
+            work.third(i - 2)
             yield
-    for copy in last:
-        copy.wait_recv()
-    own.wait()
+    for i in range(links.n_high):
+        work.fourth(i)
 
 
 def dp_gather(links, copies, block, out):
@@ -749,12 +782,13 @@
     )(down, o_t, q_up, kv_up, small, stats)
 
 
-def attention_mask(seg_col, seg_row, valid_row):
-    length = seg_col.shape[0]
+def attention_mask(seg_row, valid_row):
+    length = seg_row.shape[1]
     row = lax.broadcasted_iota(jnp.int32, (length, length), 0)
     column = lax.broadcasted_iota(jnp.int32, (length, length), 1)
+    segments = jnp.broadcast_to(seg_row[...].astype(F32), (length, length))
     allowed = (
-        (seg_col[...] == seg_row[...])
+        (segments == segments.T)
         & (column <= row)
         & ((valid_row[...] == 1) | (column == row))
     )
@@ -813,12 +847,12 @@
 
 
 def attend_kernel(
-    x, gain_attn, gain_q, gain_kv, down, q_up, kv_up, seg_col, seg_row, valid_row, cos_full, sin_full,
+    x, gain_attn, gain_q, gain_kv, down, q_up, kv_up, seg_row, valid_row, cos_full, sin_full,
     *outs,
 ):
     attend_rows(
         x, gain_attn[...], gain_q[...], gain_kv[...], down[...], q_up[...], kv_up[...],
-        attention_mask(seg_col, seg_row, valid_row), cos_full, sin_full, *outs,
+        attention_mask(seg_row, valid_row), cos_full, sin_full, *outs,
     )
 
 
@@ -841,7 +875,7 @@
             rows(ROPE, BF),
             rows(heads * VD, BF),
         ),
-        in_specs=[VMEM] * 12,
+        in_specs=[VMEM] * 11,
         out_specs=[VMEM] * 8,
         compiler_params=pltpu.CompilerParams(vmem_limit_bytes=VMEM_BYTES),
         name="attend",
@@ -853,7 +887,6 @@
         down,
         q_up,
         kv_up,
-        segments[:, None],
         segments[None, :],
         valid[None, :],
         cos_full,
@@ -887,8 +920,12 @@
             copy.wait_recv()
         self.own.wait()
 
-
-def pack_stream(w_gate, w_up, w_down, packed):
+    def sent(self):
+        for copy in self.arrive:
+            self.copies.sent(copy)
+
+
+def pack_stream(w_gate, w_up, w_down_t, packed):
     n_dp, width, lanes = packed.shape
     slice_ff = w_gate.shape[1] // n_dp
     for k in range(n_dp):
@@ -897,7 +934,7 @@
             [
                 w_gate[:, at : at + slice_ff],
                 w_up[:, at : at + slice_ff],
-                w_down[at : at + slice_ff, :].T,
+                w_down_t[:, at : at + slice_ff],
                 jnp.zeros((width, lanes - 3 * slice_ff), BF),
             ],
             axis=1,
@@ -905,15 +942,41 @@
         yield
 
 
-def front_kernel(
-    n_dp, x, x_rows, cot, down, gains, q_up, kv_up, o_t, w_gate, w_up, w_down,
-    seg_col, seg_row, valid_row, cos_full, sin_full,
-    f_down, f_o, f_q, f_kv, f_g, f_cot, f_w, f_normed,
-    normed, latents, q_normed, kv_normed, q_rows, kv_rows, key_rot, mixed, resid, branch, gain_mlp,
-    packed, part, from_core, out_side, from_side, block, send, recv, local,
+def quarter_of(values, rank):
+    rows = values.shape[0] // 4
+    mine = values[:rows]
+    for other in range(1, 4):
+        mine = jnp.where(rank == other, values[other * rows : other * rows + rows], mine)
+    return mine
+
+
+def forward_kernel(
+    n_dp, x, cotangent, q_down, kv_down_t, gain_attn, gain_q, gain_kv, gain_mlp, q_up, kv_up, o_t,
+    w_gate, w_up, w_down_t, seg_row, valid_row, turns,
+    f_down, f_o, f_q, f_kv, f_g, m_part, g_part, w_grads,
+    normed, latents, q_normed, kv_normed, q_rows, kv_rows, key_rot, mixed, resid, branch, cot,
+    down, gains, packed, f_w, f_cot, f_normed, hidden_all, both_all, m_block, g_block,
+    part, from_core, out_side, from_side, block, send, recv, local,
 ):
     links = Links(n_dp)
     copies = Copies(send, recv, local)
+    cos_full, sin_full = turns[:, :ROPE], turns[:, ROPE:]
+    rank = links.side * 2 + links.core
+    rows_down, rank_q = down.shape[0], q_down.shape[1]
+    quarter = pl.ds(pl.multiple_of(rank * rows_down, 16), rows_down)
+    down[:, :rank_q] = q_down[quarter, :]
+    kv_rows_down = quarter_of(kv_down_t[...].T, rank)
+    pad = down.shape[1] - rank_q - kv_rows_down.shape[1]
+    down[:, rank_q:] = jnp.concatenate([kv_rows_down, jnp.zeros((rows_down, pad), BF)], axis=1)
+    lanes = gains.shape[1]
+    gain_rows = [
+        jnp.concatenate([g[...].astype(F32), jnp.zeros((1, lanes - g.shape[1]), F32)], axis=1)
+        for g in (gain_attn, gain_q, gain_kv, gain_mlp)
+    ]
+    gains[...] = jnp.concatenate(gain_rows + [jnp.zeros((12, lanes), F32)], axis=0).astype(BF)
+    rows = block.shape[0]
+    own_rows = pl.ds(pl.multiple_of(rank * rows, 16), rows)
+    cot[...] = cotangent[own_rows, :]
     links.meet(swap=True)
     o_stream = dp_gather(links, copies, o_t, f_o)
     take_turns(
@@ -921,7 +984,7 @@
         dp_gather(links, copies, gains, f_g),
         dp_gather(links, copies, q_up, f_q),
         dp_gather(links, copies, kv_up, f_kv),
-        pack_stream(w_gate, w_up, w_down, packed),
+        pack_stream(w_gate, w_up, w_down_t, packed),
         later(itertools.islice(o_stream, 1), 1),
     )
 
@@ -933,104 +996,198 @@
     swap = Swap(links, copies, packed, f_w)
     swap.send(range(2, n_dp, 2))
     next(o_stream)
-    width = down.shape[0] * 4
+    width = o_t.shape[0]
     full_down = f_down[...].reshape(n_dp * width, down.shape[1])
     full_q = f_q[...].reshape(n_dp * q_up.shape[0], q_up.shape[1])
     full_kv = f_kv[...].reshape(n_dp * kv_up.shape[0], kv_up.shape[1])
     attend_rows(
         x, gain_of(0, width), gain_of(1, q_up.shape[0]), gain_of(2, kv_up.shape[0]),
-        full_down, full_q, full_kv, attention_mask(seg_col, seg_row, valid_row), cos_full, sin_full,
+        full_down, full_q, full_kv, attention_mask(seg_row, valid_row), cos_full, sin_full,
         normed, latents, q_normed, kv_normed, q_rows, kv_rows, key_rot, mixed,
     )
     for _ in range(links.n_high - 1):
         next(o_stream)
-    cot_stream = every_gather(links, copies, cot, f_cot, cot.shape[-1])
-    next(cot_stream)
-    next(cot_stream)
+    cots = EveryGather(links, copies, cot, f_cot, cot.shape[-1])
+    cots.start()
+    cots.first(0)
+    swap.send(range(1, n_dp, 2))
     take_turns(o_stream)
-    gain_mlp[...] = gain_of(3, width)
     full_o = f_o[...].reshape(n_dp * width, o_t.shape[1])
-    rows = block.shape[0]
     attn_part = dot_nt(mixed[...], full_o).astype(BF)
     for side in range(2):
         for core in range(2):
             at = (side * 2 + core) * rows
             part[side, core] = attn_part[at : at + rows]
-
-    def resid_stream():
-        over = copies.go(part.at[:, 1 - links.core], from_core, links.over_core())
-        over.wait_recv()
-        out_side[...] = (
-            part[1 - links.side, links.core].astype(F32) + from_core[1 - links.side].astype(F32)
+    over = copies.go(part.at[:, 1 - links.core], from_core, links.over_core())
+    over.wait_recv()
+    out_side[...] = (
+        part[1 - links.side, links.core].astype(F32) + from_core[1 - links.side].astype(F32)
+    ).astype(BF)
+    over = copies.go(out_side, from_side, links.over_side())
+    mine = part[links.side, links.core].astype(F32) + from_core[links.side].astype(F32)
+    over.wait_recv()
+    attn = RESIDUAL_SCALE * (mine + from_side[...].astype(F32))
+    stream = x[own_rows, :].astype(F32) + attn
+    branch[...] = attn
+    resid[...] = stream
+    block[...] = (stream * inverse_rms(stream) * gain_of(3, width)).astype(BF)
+    normeds = EveryGather(links, copies, block, f_normed)
+    normeds.start()
+    normeds.first(0)
+    n_high = links.n_high
+    for i in range(n_high + 2):
+        if 1 <= i < n_high:
+            cots.first(i)
+        if 0 <= i - 1 < n_high:
+            cots.second(i - 1)
+        if 0 <= i - 2:
+            cots.third(i - 2)
+    normeds.second(0)
+    for i in range(n_high):
+        cots.fourth(i)
+    swap.finish()
+    cots.sent()
+    normeds.third(0)
+    normeds.fourth(0)
+
+    lanes = f_w.shape[2]
+    slice_ff = w_gate.shape[1] // n_dp
+    wide = both_all.shape[1]
+    cut = lanes - hidden_all.shape[1]
+    before = 2 * slice_ff - cut
+    columns = x.shape[1]
+    tokens = 2 * x.shape[0]
+    stores = []
+
+    def zeros(count):
+        return jnp.zeros((tokens, count), F32)
+
+    def feed_forward_of(high):
+        pair = pl.ds(high * 2, 2)
+        at = pl.ds(pl.multiple_of(high * tokens, 128), tokens)
+        w_in = f_w[:, :, :wide].reshape(columns, wide)
+        w_out = f_w[:, :, cut:].reshape(columns, lanes - cut)
+        grad_mlp = (RESIDUAL_SCALE * f_cot[pair].astype(F32)).astype(BF)
+        f_cot[pair] = grad_mlp
+        both = dot(f_normed[pair].reshape(tokens, columns), w_in)
+        gate, upper = both[:, :slice_ff], both[:, slice_ff : 2 * slice_ff]
+        sigma = jax.nn.sigmoid(gate)
+        swish = gate * sigma
+        after = lanes - cut - before - slice_ff
+        hidden = jnp.concatenate([zeros(before), swish * upper, zeros(after)], axis=1).astype(BF)
+        grad_hidden = dot(grad_mlp.reshape(tokens, columns), w_out)[:, before : before + slice_ff]
+        grad_both = jnp.concatenate(
+            [
+                grad_hidden * upper * (sigma * (1.0 + gate * (1.0 - sigma))),
+                grad_hidden * swish,
+                zeros(wide - 2 * slice_ff),
+            ],
+            axis=1,
         ).astype(BF)
-        over = copies.go(out_side, from_side, links.over_side())
-        mine = part[links.side, links.core].astype(F32) + from_core[links.side].astype(F32)
-        over.wait_recv()
-        attn = RESIDUAL_SCALE * (mine + from_side[...].astype(F32))
-        stream = x_rows[...].astype(F32) + attn
-        branch[...] = attn
-        resid[...] = stream
-        block[...] = (stream * inverse_rms(stream) * gain_mlp[...]).astype(BF)
-        yield from every_gather(links, copies, block, f_normed)
-
-    normed_stream = resid_stream()
-    next(normed_stream)
-    swap.send(range(1, n_dp, 2))
-    take_turns(normed_stream, cot_stream)
-    swap.finish()
+        hidden_all[at, :] = hidden
+        both_all[at, :] = grad_both
+        while stores:
+            stores.pop().wait()
+        m_block[...] = dot_nt(hidden, w_out).astype(BF).reshape(m_block.shape)
+        stores.append(copies.near(m_block, m_part.at[pair]))
+        g_block[...] = dot_nt(grad_both, w_in).astype(BF).reshape(g_block.shape)
+        stores.append(copies.near(g_block, g_part.at[pair]))
+
+    for i in range(1, n_high):
+        normeds.first(i)
+        if i == 1:
+            feed_forward_of(links.behind(normeds.order[0]))
+        normeds.second(i)
+        normeds.third(i)
+        if i > 1:
+            feed_forward_of(links.behind(normeds.order[i - 1]))
+        normeds.fourth(i)
+    feed_forward_of(links.behind(normeds.order[n_high - 1]))
+    swap.sent()
+    all_tokens = n_dp * x.shape[0]
+    for k in range(n_dp):
+        at = k * width
+        slab_in = dot_tn(
+            f_normed[:, :, :, at : at + width].reshape(all_tokens, width), both_all[...]
+        )
+        slab_out = dot_tn(
+            f_cot[:, :, :, at : at + width].reshape(all_tokens, width), hidden_all[...]
+        )
+        packed[k, :, :cut] = slab_in[:, :cut].astype(BF)
+        packed[k, :, cut:wide] = (slab_in[:, cut:] + slab_out[:, : wide - cut]).astype(BF)
+        packed[k, :, wide:] = slab_out[:, wide - cut :].astype(BF)
+        stores.append(copies.near(packed.at[k], w_grads.at[k]))
+    while stores:
+        stores.pop().wait()
     copies.finish()
 
 
-def front(n_dp, x, x_rows, cot, down, gains, q_up, kv_up, o_t, w_gate, w_up, w_down, segments, valid, cos_full, sin_full):
+def forward(
+    n_dp, x, cotangent, q_down, kv_down_t, gains, q_up, kv_up, o_t, w_gate, w_up, w_down_t,
+    segments, valid, turns, down_shape, gain_lanes,
+):
     n_high = n_dp // 2
     length, columns = x.shape
-    rows = x_rows.shape[0]
-    lanes = -(-3 * (w_gate.shape[1] // n_dp) // 128) * 128
+    rows = length // 4
+    slice_ff = w_gate.shape[1] // n_dp
+    lanes = -(-3 * slice_ff // 128) * 128
+    wide = -(-2 * slice_ff // 128) * 128
+    cut = 2 * slice_ff // 128 * 128
     heads = q_up.shape[1] // (NOPE + ROPE)
     count = 3 * count_every_gather(n_high) + 4 * (2 * n_high - 1) + n_dp + 1
+    block = (rows, columns)
 
     def over(block, *lead, kind=BF):
         return jax.ShapeDtypeStruct((*lead, *block), kind)
 
     return pl.pallas_call(
-        functools.partial(front_kernel, n_dp),
+        functools.partial(forward_kernel, n_dp),
         out_shape=(
-            over(down.shape, n_dp, 4),
+            over(down_shape, n_dp, 4),
             over(o_t.shape, n_dp),
             over(q_up.shape, n_dp),
             over(kv_up.shape, n_dp),
-            over(gains.shape, n_dp),
-            over(cot.shape, n_dp, 4),
+            over((16, gain_lanes), n_dp),
+            over(block, n_dp, 4),
+            over(block, n_dp, 4),
             over((w_gate.shape[0], lanes), n_dp),
-            over(cot.shape, n_dp, 4),
             over((columns,), length),
-            over((down.shape[1],), length, kind=F32),
+            over((down_shape[1],), length, kind=F32),
             over((q_up.shape[0] * n_dp,), length),
             over((kv_up.shape[0] * n_dp,), length),
             over((q_up.shape[1],), length),
             over((kv_up.shape[1],), length),
             over((ROPE,), length),
             over((heads * VD,), length),
-            over((columns,), rows, kind=F32),
-            over((columns,), rows, kind=F32),
-            over((columns,), 1, kind=F32),
+            over(block, kind=F32),
+            over(block, kind=F32),
+            over(block),
         ),
-        in_specs=[VMEM] * 16,
+        in_specs=[VMEM] * 17,
         out_specs=[VMEM] * 5 + [ANY] * 3 + [VMEM] * 11,
         scratch_shapes=[
+            pltpu.VMEM(down_shape, BF),
+            pltpu.VMEM((16, gain_lanes), BF),
             pltpu.VMEM((n_dp, w_gate.shape[0], lanes), BF),
-            pltpu.VMEM((2, 2, rows, columns), BF),
-            pltpu.VMEM((2, rows, columns), BF),
-            pltpu.VMEM((rows, columns), BF),
-            pltpu.VMEM((rows, columns), BF),
-            pltpu.VMEM((rows, columns), BF),
-            *semaphores(count, 8),
+            pltpu.VMEM((n_dp, w_gate.shape[0], lanes), BF),
+            pltpu.VMEM((n_dp, 4, *block), BF),
+            pltpu.VMEM((n_dp, 4, *block), BF),
+            pltpu.VMEM((n_dp * length, lanes - cut), BF),
+            pltpu.VMEM((n_dp * length, wide), BF),
+            pltpu.VMEM((2, 4, *block), BF),
+            pltpu.VMEM((2, 4, *block), BF),
+            pltpu.VMEM((2, 2, *block), BF),
+            pltpu.VMEM((2, *block), BF),
+            pltpu.VMEM(block, BF),
+            pltpu.VMEM(block, BF),
+            pltpu.VMEM(block, BF),
+            *semaphores(count, 8 + 2 * n_high + n_dp),
         ],
-        compiler_params=params(7),
-        name="front",
+        compiler_params=params(7, 62),
+        name="forward",
     )(
-        x, x_rows, cot, down, gains, q_up, kv_up, o_t, w_gate, w_up, w_down,
-        segments[:, None], segments[None, :], valid[None, :], cos_full, sin_full,
+        x, cotangent, q_down, kv_down_t, *(g[None, :] for g in gains), q_up, kv_up, o_t,
+        w_gate, w_up, w_down_t, segments[None, :], valid[None, :], turns,
     )
 
 
@@ -1110,13 +1267,13 @@
 
 def attend_back_kernel(
     grad_attn, mixed, o_t, q_rows, kv_rows, key_rot, q_normed, kv_normed, q_up, kv_up,
-    seg_col, seg_row, valid_row, cos_full, sin_full,
+    seg_row, valid_row, cos_full, sin_full,
     grad_latents, grad_o, grad_q_up, grad_kv_up, grad_q, grad_kv,
 ):
     rank_q = q_up.shape[0]
     grad_o[...] = dot_tn(grad_attn[...], mixed[...]).astype(BF)
     grad_mixed = dot(grad_attn[...], o_t[...]).astype(BF)
-    bias = attention_mask(seg_col, seg_row, valid_row)
+    bias = attention_mask(seg_row, valid_row)
     inv_root = 1.0 / math.sqrt(NOPE + ROPE)
     grad_rot = jnp.zeros((grad_attn.shape[0], ROPE), F32)
     for head in range(q_rows.shape[1] // (NOPE + ROPE)):
@@ -1168,14 +1325,14 @@
             out(q_up.shape),
             out(kv_up.shape),
         ),
-        in_specs=[VMEM] * 15,
+        in_specs=[VMEM] * 14,
         out_specs=[VMEM] * 4,
         scratch_shapes=[pltpu.VMEM(q_rows.shape, BF), pltpu.VMEM(kv_rows.shape, BF)],
         compiler_params=pltpu.CompilerParams(vmem_limit_bytes=VMEM_BYTES),
         name="attend_back",
     )(
         grad_attn, mixed, o_t, q_rows, kv_rows, key_rot, q_normed, kv_normed, q_up, kv_up,
-        segments[:, None], segments[None, :], valid[None, :], cos_full, sin_full,
+        segments[None, :], valid[None, :], cos_full, sin_full,
     )
 
 
@@ -1256,9 +1413,9 @@
 
 
 def back_kernel(
-    n_dp, g_part, m_part, w_part, resid, branch, cot, weight, x, normed, latents, q_normed, kv_normed,
-    q_rows, kv_rows, key_rot, mixed, f_down, f_o, f_q, f_kv, f_g, seg_col, seg_row, valid_row,
-    cos_full, sin_full,
+    n_dp, g_part, m_part, w_part, resid, branch, cot, x, normed, latents, q_normed, kv_normed,
+    q_rows, kv_rows, key_rot, mixed, f_down, f_o, f_q, f_kv, f_g, seg_row, valid_row,
+    turns,
     block_full, grad_input, d_full, o_sum, q_sum, kv_sum, small_full, w_full,
     attn_full, grad_rows, g_rows, m_rows, grad_q, grad_kv, lat, lat_in, lat_half, lat_side,
     lat_full, d_block, small, small_in, stats, stats_in, stats_block, small_block, *rest,
@@ -1268,6 +1425,7 @@
     links = Links(n_dp)
     copies = Copies(*rest[25:])
     links.meet(swap=True)
+    cos_full, sin_full = turns[:, :ROPE], turns[:, ROPE:]
     length = x.shape[0]
     rank_q, rank_kv = q_normed.shape[1], kv_normed.shape[1]
     width = o_sum.shape[0]
@@ -1308,7 +1466,7 @@
     m.first(2)
     m.first(3)
     mlp_gain = jnp.sum(g_rows[...] * unit_two, axis=0, keepdims=True)
-    bias = attention_mask(seg_col, seg_row, valid_row)
+    bias = attention_mask(seg_row, valid_row)
     for _ in t_stream:
         pass
 
@@ -1408,11 +1566,7 @@
     rank = links.side * 2 + links.core
     for k in range(n_dp):
         rows_all = dot_tn(normed_rows[:, k * width : k * width + width], grad_down)
-        mine = rows_all[:rows_down]
-        for quarter in range(1, 4):
-            at = quarter * rows_down
-            mine = jnp.where(rank == quarter, rows_all[at : at + rows_down], mine)
-        d_bufs[0][k // 2, k % 2] = mine.astype(BF)
+        d_bufs[0][k // 2, k % 2] = quarter_of(rows_all, rank).astype(BF)
 
     d = ScatterInto(links, copies, d_bufs, d_block)
     d.start()
@@ -1430,7 +1584,8 @@
     g_rows[...] = resid[...] + mlp
     block_gather = tensor_gather(links, copies, g_rows, block_full)
     next(block_gather)
-    weights = weight[...]
+    valid = jnp.broadcast_to((valid_row[...] == 1).astype(F32), (length, length)).T
+    weights = quarter_of(valid, rank)[:, :1]
     lane = lax.broadcasted_iota(jnp.int32, stats.shape, 1)
     sums = [
         jnp.sum(jnp.sum(weights * rows * rows, axis=1, keepdims=True), axis=0, keepdims=True)
@@ -1474,8 +1629,8 @@
 
 
 def back(
-    n_dp, g_part, m_part, w_part, resid, branch, cot, weight, x, normed, latents, q_normed, kv_normed,
-    q_rows, kv_rows, key_rot, mixed, f_down, f_o, f_q, f_kv, f_g, segments, valid, cos_full, sin_full,
+    n_dp, g_part, m_part, w_part, resid, branch, cot, x, normed, latents, q_normed, kv_normed,
+    q_rows, kv_rows, key_rot, mixed, f_down, f_o, f_q, f_kv, f_g, segments, valid, turns,
 ):
     n_high = n_dp // 2
     rows, columns = resid.shape
@@ -1502,7 +1657,7 @@
             out((4, 2, *one)),
             out(w_part.shape, BF),
         ),
-        in_specs=[ANY] * 3 + [VMEM] * 5 + [ANY] + [VMEM] * 17,
+        in_specs=[ANY] * 3 + [VMEM] * 4 + [ANY] + [VMEM] * 15,
         out_specs=[ANY] + [VMEM] * 6 + [ANY],
         scratch_shapes=[
             pltpu.VMEM((4, rows, columns), BF),
@@ -1534,10 +1689,71 @@
         compiler_params=params(8, 62),
         name="back",
     )(
-        g_part.reshape(shape), m_part.reshape(shape), w_part, resid, branch, cot, weight, x,
+        g_part.reshape(shape), m_part.reshape(shape), w_part, resid, branch, cot, x,
         normed.reshape(2, 2, rows, columns), latents, q_normed, kv_normed, q_rows, kv_rows, key_rot, mixed, f_down, f_o, f_q, f_kv, f_g,
-        segments[:, None], segments[None, :], valid[None, :], cos_full, sin_full,
+        segments[None, :], valid[None, :], turns,
     )
+
+
+def unpack_kernel(
+    slice_ff, rank_q, swapped, down, o_in, q_in, kv_in, block_in, input_in, small,
+    grad_gate, grad_upper, grad_down_t, grad_o_t, grad_q_down, grad_kv_down_t, grad_q_up, grad_kv_up,
+    block_out, grad_input,
+    attn_gain, q_gain, kv_gain, mlp_gain, stats,
+):
+    n_dp = swapped.shape[0]
+
+    def pieces(start):
+        return jnp.concatenate(
+            [swapped[k, :, start : start + slice_ff] for k in range(n_dp)], axis=1
+        ).astype(F32)
+
+    grad_gate[...] = pieces(0)
+    grad_upper[...] = pieces(slice_ff)
+    grad_down_t[...] = pieces(2 * slice_ff)
+    for target, source in (
+        (grad_o_t, o_in), (grad_q_up, q_in), (grad_kv_up, kv_in), (block_out, block_in), (grad_input, input_in),
+    ):
+        target[...] = source[...]
+    rows = down[...].reshape(grad_q_down.shape[0], down.shape[2]).astype(F32)
+    grad_q_down[...] = rows[:, :rank_q]
+    grad_kv_down_t[...] = rows[:, rank_q : rank_q + grad_kv_down_t.shape[0]].T
+    gains = small[0, 0]
+    for row, gain in ((0, attn_gain), (1, q_gain), (2, kv_gain)):
+        gain[...] = gains[row : row + 1, : gain.shape[1]]
+    total = small[0, 0] + small[1, 0] + small[2, 0] + small[3, 0]
+    mlp_gain[...] = total[3:4, : mlp_gain.shape[1]]
+    sums = (small[0, 1] + small[1, 1] + small[2, 1] + small[3, 1])[0:1]
+    stats[...] = jnp.sqrt(sums[:, :3] / (sums[:, 3:4] * D))
+
+
+def unpack(swapped, down, o_t, q_up, kv_up, block, grad_input, small, slice_ff, rank_q, columns_down, gains):
+    n_dp, width, _ = swapped.shape
+
+    def out(*shape):
+        return jax.ShapeDtypeStruct(shape, F32)
+
+    return pl.pallas_call(
+        functools.partial(unpack_kernel, slice_ff, rank_q),
+        out_shape=(
+            out(width, n_dp * slice_ff),
+            out(width, n_dp * slice_ff),
+            out(width, n_dp * slice_ff),
+            out(*o_t.shape),
+            out(width, rank_q),
+            out(columns_down - rank_q, width),
+            out(*q_up.shape),
+            out(*kv_up.shape),
+            out(*block.shape),
+            out(*grad_input.shape),
+            *(out(1, gain.shape[0]) for gain in gains),
+            out(1, 3),
+        ),
+        in_specs=[VMEM] * 8,
+        out_specs=[VMEM] * 15,
+        compiler_params=pltpu.CompilerParams(vmem_limit_bytes=VMEM_BYTES),
+        name="unpack",
+    )(swapped, down, o_t, q_up, kv_up, block, grad_input, small)
 
 
 def per_device(
@@ -1596,12 +1812,13 @@
     fused = n_dp == 8 and rows_down % 16 == 0 and q_up.shape[0] % 16 == 0
     if fused:
         (
-            f_down, f_o, f_q, f_kv, f_g, f_cot, f_w, f_normed,
+            f_down, f_o, f_q, f_kv, f_g, mlp_part, normed_part, grad_packed,
             normed, latents, q_normed, kv_normed, q_rows, kv_rows, key_rot, mixed,
-            resid_rows, attn_rows, _,
-        ) = front(
-            n_dp, layer_input, x_rows, cot_rows, down_rows, gains_block, q_up, kv_up, o_proj.T,
-            w_gate, w_up, w_down, segment_ids, valid_mask, cos_full, sin_full,
+            resid_rows, attn_rows, cot_rows,
+        ) = forward(
+            n_dp, layer_input, cotangent, q_down, kv_down.T, (attn_gain, q_gain, kv_gain, mlp_gain),
+            q_up, kv_up, o_proj.T, w_gate, w_up, w_down.T, segment_ids, valid_mask,
+            jnp.concatenate([cos_full, sin_full], axis=1), down_rows.shape, lanes,
         )
     else:
         f_down, f_o, f_q, f_kv, f_g, f_cot = gather_weights(
@@ -1639,21 +1856,47 @@
         f_normed, resid_rows, attn_rows = attention_residual(
             n_dp, dot_nt(mixed, full_o).astype(BF), x_rows, gain_mlp[None, :]
         )
-    mlp_part, normed_part, grad_packed = feed_forward(
-        f_normed.reshape(n_dp * length, -1),
-        f_cot.reshape(n_dp * length, -1),
-        f_w.reshape(n_dp * width, -1),
-        slice_ff,
-        length,
-    )
+    if not fused:
+        mlp_part, normed_part, grad_packed = feed_forward(
+            f_normed.reshape(n_dp * length, -1),
+            f_cot.reshape(n_dp * length, -1),
+            f_w.reshape(n_dp * width, -1),
+            slice_ff,
+            length,
+        )
     weight_rows = rows_of(valid_mask.astype(F32)[:, None], share)
     if fused:
         f_block, grad_input, s_down, s_o, s_q, s_kv, s_small, swapped = back(
             n_dp, normed_part, mlp_part, grad_packed.reshape(n_dp, width, -1), resid_rows, attn_rows,
-            cot_rows, weight_rows, layer_input, normed, latents, q_normed, kv_normed, q_rows, kv_rows,
-            key_rot, mixed, f_down, f_o, f_q, f_kv, f_g, segment_ids, valid_mask, cos_full, sin_full,
-        )
-        block_full = f_block.reshape(length, -1)
+            cot_rows, layer_input, normed, latents, q_normed, kv_normed, q_rows, kv_rows,
+            key_rot, mixed, f_down, f_o, f_q, f_kv, f_g, segment_ids, valid_mask,
+            jnp.concatenate([cos_full, sin_full], axis=1),
+        )
+        (
+            grad_w_gate, grad_w_up, grad_down_t, grad_o_t, grad_q_down, grad_kv_down_t, grad_q_up,
+            grad_kv_up, block_full, grad_input, grad_attn_gain, grad_q_gain, grad_kv_gain, grad_mlp_gain, rms_stats,
+        ) = unpack(
+            swapped, s_down, s_o, s_q, s_kv, f_block.reshape(length, -1), grad_input, s_small,
+            slice_ff, rank_q, columns_down,
+            (attn_gain, q_gain, kv_gain, mlp_gain),
+        )
+        return (
+            block_full,
+            grad_input,
+            grad_attn_gain.reshape(-1),
+            grad_q_down,
+            grad_q_gain.reshape(-1),
+            grad_q_up,
+            grad_kv_down_t.T,
+            grad_kv_gain.reshape(-1),
+            grad_kv_up,
+            grad_o_t.T,
+            grad_mlp_gain.reshape(-1),
+            grad_w_gate,
+            grad_w_up,
+            grad_down_t.T,
+            rms_stats.reshape(-1),
+        )
     else:
         inv_two = inverse_rms(resid_rows)
         unit_two = resid_rows * inv_two
@@ -1734,12 +1977,12 @@
             lane_rows([stats], 8, F32),
         )
 
-    def unpack(part):
+    def columns_of(part):
         return part.transpose(1, 0, 2).reshape(width, n_dp * slice_ff).astype(F32)
 
-    grad_w_gate = unpack(swapped[:, :, :slice_ff])
-    grad_w_up = unpack(swapped[:, :, slice_ff : 2 * slice_ff])
-    grad_w_down = unpack(swapped[:, :, 2 * slice_ff : 3 * slice_ff]).T
+    grad_w_gate = columns_of(swapped[:, :, :slice_ff])
+    grad_w_up = columns_of(swapped[:, :, slice_ff : 2 * slice_ff])
+    grad_w_down = columns_of(swapped[:, :, 2 * slice_ff : 3 * slice_ff]).T
 
     d_down = s_down.reshape(width, -1).astype(F32)
     gains = s_small[me, 0]

time: 573 us -> 514 us (0.90)
  local copies, waits for them, and re-layouts: 36.7 us -> 2.49 us
  Pallas kernels: 516 us -> 500 us
  other arithmetic: 9.66 us -> 3.72 us
    pallas_call x1, Pallas kernels: 250 us -> 230 us  [back(): pl.pallas_call(functools.partial(back_kernel, n_dp), out_shape=(out((4, r...]
    convert_element_type x4 -> x0, local copies, waits for them, and re-layouts: 11.1 us -> none  [unpack(): return part.transpose(1, 0, 2).reshape(width, n_dp * slice_ff).astype(F32)]
    unnamed x32 -> x0, local copies, waits for them, and re-layouts: 9.21 us -> none
where the time goes in v5:
time: 514 us; the launch traced here: 507 us
  Pallas kernels  500 us (97%)
    pallas_call x1, Pallas kernels, forward(): pl.pallas_call(functools.partial(forward_kernel, n_dp), out_shape=(over(d...  260 us
    pallas_call x1, Pallas kernels, back(): pl.pallas_call(functools.partial(back_kernel, n_dp), out_shape=(out((4, r...  230 us

profile of v5, /device:TPU:1, one launch (start us, length us, event | category | flops | bytes accessed | tf_op | source)
XLA Modules:
  0.0 507.4 jit_solution(3600331431765554924)
XLA Ops:
  0.7 1.2 broadcast_in_dim.22.gain_attn
  1.9 1.2 broadcast_in_dim.25.gain_mlp
  3.1 0.4 fusion.1
  3.5 0.8 pad_maximum_fusion.turns
  4.3 260.4 %forward.1 = (bf16[8,4,80,1152]{3,2,1,0:T(8,128)(2,1)}, bf16[8,320,640]{2,1,0:T(8,128)(2,1)}, bf16[8,96,960]{2,1,0:T(8,128)(2,1)}, bf16[8,32,1280]{2,1,0:T(8,128...) custom-call(bf16[192,2560]{1,0:T(8,128)(2,1)} %x.3, ...), custom_call_target="tpu_custom_call" | custom-call | tf_op jit(solution)/shard_map/forward/pallas_call | solution.py:1143
  264.7 230.4 %back.1 = (f32[4,48,2560]{2,1,0:T(8,128)}, f32[192,2560]{1,0:T(8,128)}, bf16[4,80,1152]{2,1,0:T(8,128)(2,1)}, f32[320,640]{1,0:T(8,128)}, f32[96,960]{1,0:T(8,12...) custom-call(bf16[4,2,2,2,48,2560]{5,4,3,2,1,0:T(8,128)(2,1)} %bitcast.18, ...), custom_call_target="tpu_custom_call" | custom-call | tf_op jit(solution)/shard_map/back/pallas_call | solution.py:1648
  495.2 9.4 %unpack.1 = (f32[320,1600]{1,0:T(8,128)}, f32[320,1600]{1,0:T(8,128)}, f32[320,1600]{1,0:T(8,128)}, f32[320,640]{1,0:T(8,128)}, f32[320,768]{1,0:T(8,128)}, /*in...) custom-call(bf16[8,320,640]{2,1,0:T(8,128)(2,1)} %get-tuple-element., ...), custom_call_target="tpu_custom_call" | custom-call | tf_op jit(solution)/shard_map/unpack/pallas_call | solution.py:1736
  504.6 1.3 reduce
  505.9 1.3 reduce.1
  (1 shorter events, 0.0 us)

commit v6 on v5

--- a/solution.py
+++ b/solution.py
@@ -121,7 +121,7 @@
         self.send, self.recv, self.local = send, recv, local
         self.count = self.local_count = 0
         self.started = []
-        self.local_started = []
+        self.maybe = []
 
     def go(self, source, target, device):
         copy = pltpu.make_async_remote_copy(
@@ -137,11 +137,15 @@
         self.started.append(copy)
         return copy
 
+    def sent_maybe(self):
+        for condition, copy in self.maybe:
+            pl.when(condition)(copy.wait_send)
+        self.maybe = []
+
     def near(self, source, target):
         copy = pltpu.make_async_copy(source, target, self.local.at[self.local_count])
         self.local_count += 1
         copy.start()
-        self.local_started.append(copy)
         return copy
 
     def sent(self, copy):
@@ -151,6 +155,8 @@
     def finish(self):
         for copy in self.started:
             copy.wait_send()
+        for condition, copy in self.maybe:
+            pl.when(condition)(copy.wait_send)
 
 
 def take_turns(*streams):
@@ -173,79 +179,154 @@
     return order
 
 
+class Line:
+    def __init__(self, links, copies, block, target):
+        self.links, self.copies, self.block, self.target = links, copies, block, target
+        self.count = links.n_high
+        self.first_tag = copies.count
+        copies.count += self.count
+        inner = steps_by_distance(self.count)
+        at_start = (self.count - 1 - links.high) // (self.count - 1)
+        at_end = links.high // (self.count - 1)
+        self.tags = [0] + [
+            at_start * (self.count - i) + at_end * i + (1 - at_start - at_end) * inner[i - 1]
+            for i in range(1, self.count)
+        ]
+
+    def source(self, i):
+        return (self.links.high + self.count - self.tags[i]) % self.count
+
+    def send(self, condition, source, to, tag):
+        copy = pltpu.make_async_remote_copy(
+            src_ref=source,
+            dst_ref=source if source is not self.block else self.target(self.links.high),
+            send_sem=self.copies.send.at[self.copies.count],
+            recv_sem=self.copies.recv.at[self.first_tag + tag],
+            device_id=self.links.device(high=to),
+            device_id_type=MESH,
+        )
+        self.copies.count += 1
+        pl.when(condition)(copy.start)
+        self.copies.maybe.append((condition, copy))
+
+    def start(self):
+        high = self.links.high
+        self.send(high < self.count - 1, self.block, (high + 1) % self.count, 1)
+        self.send(
+            high > 0, self.block, (high + self.count - 1) % self.count, self.count - 1
+        )
+
+    def arrived(self, i):
+        high, tag = self.links.high, self.tags[i]
+        here = self.target(self.source(i))
+        pltpu.make_async_remote_copy(
+            src_ref=here,
+            dst_ref=here,
+            send_sem=self.copies.send.at[self.first_tag],
+            recv_sem=self.copies.recv.at[self.first_tag + tag],
+            device_id=self.links.over_low(),
+            device_id_type=MESH,
+        ).wait_recv()
+        from_left = high >= tag
+        onward = (from_left & (high < self.count - 1)) | ((high < tag) & (high > 0))
+        way = jnp.where(from_left, 1, self.count - 1)
+        self.send(onward, here, (high + way) % self.count, (tag + way) % self.count)
+
+
+class Direct:
+    def __init__(self, links, copies, block, target):
+        self.links, self.copies, self.block, self.target = links, copies, block, target
+        self.order = [0] + steps_by_distance(links.n_high)
+
+    def source(self, i):
+        return self.links.behind(self.order[i])
+
+    def start(self):
+        mine = self.target(self.links.high)
+        self.arrive = [None] + [
+            self.copies.go(self.block, mine, self.links.device(high=self.links.ahead(k)))
+            for k in self.order[1:]
+        ]
+
+    def arrived(self, i):
+        self.arrive[i].wait_recv()
+
+
+def along_high(links, copies, block, target):
+    return (Line if links.n_high == 4 else Direct)(links, copies, block, target)
+
+
 class EveryGather:
     def __init__(self, links, copies, block, out, cut=None):
         self.links, self.copies, self.block, self.out = links, copies, block, out
         self.columns = out.shape[-1]
         self.cut = self.columns // 256 * 128 if cut is None else cut
-        self.order = [0] + steps_by_distance(links.n_high)
-        self.arrive, self.over_low, self.over_side = {}, {}, {}
-        self.corners = {k: [] for k in self.order}
-        self.last = {k: [] for k in self.order}
+        self.line = along_high(
+            links, copies, block, lambda high: self.slot(high, links.low, links.side)
+        )
+        self.over_low, self.over_side = {}, {}
+        self.corners = {i: [] for i in range(links.n_high)}
+        self.last = {i: [] for i in range(links.n_high)}
 
     def slot(self, high, low, side):
         return self.out.at[high * 2 + low, side * 2 + self.links.core]
 
     def start(self):
         links = self.links
-        mine = self.slot(links.high, links.low, links.side)
-        self.own = self.copies.near(self.block, mine)
-        for k in self.order[1:]:
-            self.arrive[k] = self.copies.go(
-                self.block, mine, links.device(high=links.ahead(k))
-            )
-
-    def to_core(self, k, source, target):
-        self.last[k].append(self.copies.go(source, target, self.links.over_core()))
+        self.own = self.copies.near(self.block, self.slot(links.high, links.low, links.side))
+        self.line.start()
+
+    def to_core(self, i, source, target):
+        self.last[i].append(self.copies.go(source, target, self.links.over_core()))
 
     def first(self, i):
-        links, k = self.links, self.order[i]
-        here = self.slot(links.behind(k), links.low, links.side)
-        if k:
-            self.arrive[k].wait_recv()
-        source = here if k else self.block
-        self.over_low[k] = self.copies.go(source, here, links.over_low())
-        self.over_side[k] = self.copies.go(source, here, links.over_side())
-        self.to_core(k, source, here)
+        links = self.links
+        here = self.slot(self.line.source(i), links.low, links.side)
+        if i:
+            self.line.arrived(i)
+        source = here if i else self.block
+        self.over_low[i] = self.copies.go(source, here, links.over_low())
+        self.over_side[i] = self.copies.go(source, here, links.over_side())
+        self.to_core(i, source, here)
 
     def second(self, i):
-        links, k = self.links, self.order[i]
-        self.over_low[k].wait_recv()
-        here = self.slot(links.behind(k), 1 - links.low, links.side)
+        links, high = self.links, self.line.source(i)
+        self.over_low[i].wait_recv()
+        here = self.slot(high, 1 - links.low, links.side)
         if self.cut:
             half = pl.ds(0, self.cut)
             part = here.at[:, half]
-            self.corners[k].append((self.copies.go(part, part, links.over_side()), half))
-        self.to_core(k, here, here)
-        self.over_side[k].wait_recv()
-        here = self.slot(links.behind(k), links.low, 1 - links.side)
+            self.corners[i].append((self.copies.go(part, part, links.over_side()), half))
+        self.to_core(i, here, here)
+        self.over_side[i].wait_recv()
+        here = self.slot(high, links.low, 1 - links.side)
         if self.cut < self.columns:
             half = pl.ds(self.cut, self.columns - self.cut)
             part = here.at[:, half]
-            self.corners[k].append((self.copies.go(part, part, links.over_low()), half))
-        self.to_core(k, here, here)
+            self.corners[i].append((self.copies.go(part, part, links.over_low()), half))
+        self.to_core(i, here, here)
 
     def third(self, i):
-        links, k = self.links, self.order[i]
-        here = self.slot(links.behind(k), 1 - links.low, 1 - links.side)
-        for corner, half in self.corners[k]:
+        links = self.links
+        here = self.slot(self.line.source(i), 1 - links.low, 1 - links.side)
+        for corner, half in self.corners[i]:
             corner.wait_recv()
             part = here.at[:, half]
-            self.to_core(k, part, part)
+            self.to_core(i, part, part)
 
     def fourth(self, i):
-        k = self.order[i]
-        for copy in self.last[k]:
+        for copy in self.last[i]:
             copy.wait_recv()
-        if k == 0:
+        if i == 0:
             self.own.wait()
 
     def sent(self):
-        copies = [*self.arrive.values(), *self.over_low.values(), *self.over_side.values()]
+        copies = [*self.over_low.values(), *self.over_side.values()]
         copies += [corner for pairs in self.corners.values() for corner, _ in pairs]
         copies += [copy for last in self.last.values() for copy in last]
         for copy in copies:
             self.copies.sent(copy)
+        self.copies.sent_maybe()
 
 
 def every_gather(links, copies, block, out, cut=None):
@@ -266,23 +347,41 @@
         work.fourth(i)
 
 
+class DpGather:
+    def __init__(self, links, copies, block, out):
+        self.links, self.copies, self.block, self.out = links, copies, block, out
+        self.line = along_high(links, copies, block, lambda high: out.at[high * 2 + links.low])
+        self.last = []
+        self.mine = out.at[links.high * 2 + links.low]
+
+    def start(self):
+        self.own = self.copies.near(self.block, self.mine)
+        self.line.start()
+
+    def own_low(self):
+        self.last.append(self.copies.go(self.block, self.mine, self.links.over_low()))
+
+    def step(self, i):
+        self.line.arrived(i + 1)
+        here = self.out.at[self.line.source(i + 1) * 2 + self.links.low]
+        self.last.append(self.copies.go(here, here, self.links.over_low()))
+
+    def finish(self):
+        for copy in self.last:
+            copy.wait_recv()
+        self.own.wait()
+
+
 def dp_gather(links, copies, block, out):
-    mine = out.at[links.high * 2 + links.low]
-    own = copies.near(block, mine)
-    arrive, last = {}, []
-    for k in steps_by_distance(links.n_high):
-        arrive[k] = copies.go(block, mine, links.device(high=links.ahead(k)))
+    work = DpGather(links, copies, block, out)
+    work.start()
     yield
-    last.append(copies.go(block, mine, links.over_low()))
+    work.own_low()
     yield
-    for k in steps_by_distance(links.n_high):
-        arrive[k].wait_recv()
-        here = out.at[links.behind(k) * 2 + links.low]
-        last.append(copies.go(here, here, links.over_low()))
+    for i in range(links.n_high - 1):
+        work.step(i)
         yield
-    for copy in last:
-        copy.wait_recv()
-    own.wait()
+    work.finish()
 
 
 def tensor_gather(links, copies, block, out):
@@ -475,7 +574,11 @@
 
 
 def count_every_gather(n_high):
-    return n_high - 1 + 9 * n_high
+    return 11 * n_high + 1
+
+
+def count_dp_gather(n_high):
+    return 3 * n_high + 1
 
 
 def weights_kernel(n_dp, down, o_t, q_up, kv_up, gains, cot, f_down, f_o, f_q, f_kv, f_g, f_cot, send, recv, local):
@@ -495,7 +598,7 @@
 
 def gather_weights(n_dp, n_tensor, down, o_t, q_up, kv_up, gains, cot):
     n_high = n_dp // 2
-    count = 2 * count_every_gather(n_high) + 4 * (2 * n_high - 1)
+    count = 2 * count_every_gather(n_high) + 4 * count_dp_gather(n_high)
 
     def over(block, *lead):
         return jax.ShapeDtypeStruct((*lead, *block.shape), block.dtype)
@@ -810,14 +913,16 @@
     return weights / jnp.sum(weights, axis=-1, keepdims=True)
 
 
-def attend_rows(
-    x, gain_attn, gain_q, gain_kv, down, q_up, kv_up, bias, cos_full, sin_full,
-    normed, latents, q_normed, kv_normed, q_rows, kv_rows, key_rot, mixed,
-):
-    rank_q = gain_q.shape[1]
+def latent_rows(x, gain_attn, down, normed, latents):
     stream = x[...].astype(F32)
     normed[...] = (stream * inverse_rms(stream) * gain_attn).astype(BF)
     latents[...] = dot(normed[...], down)
+
+
+def attend_rows(
+    gain_q, gain_kv, q_up, kv_up, bias, cos_full, sin_full, latents, q_normed, kv_normed, q_rows, kv_rows, key_rot, mixed,
+):
+    rank_q = gain_q.shape[1]
     q_latent = latents[:, :rank_q]
     q_normed[...] = (q_latent * inverse_rms(q_latent) * gain_q).astype(BF)
     kv_latent = latents[:, rank_q : rank_q + KR]
@@ -848,11 +953,12 @@
 
 def attend_kernel(
     x, gain_attn, gain_q, gain_kv, down, q_up, kv_up, seg_row, valid_row, cos_full, sin_full,
-    *outs,
+    normed, *outs,
 ):
+    latent_rows(x, gain_attn[...], down[...], normed, outs[0])
     attend_rows(
-        x, gain_attn[...], gain_q[...], gain_kv[...], down[...], q_up[...], kv_up[...],
-        attention_mask(seg_row, valid_row), cos_full, sin_full, *outs,
+        gain_q[...], gain_kv[...], q_up[...], kv_up[...], attention_mask(seg_row, valid_row),
+        cos_full, sin_full, *outs,
     )
 
 
@@ -978,40 +1084,63 @@
     own_rows = pl.ds(pl.multiple_of(rank * rows, 16), rows)
     cot[...] = cotangent[own_rows, :]
     links.meet(swap=True)
-    o_stream = dp_gather(links, copies, o_t, f_o)
-    take_turns(
-        every_gather(links, copies, down, f_down),
-        dp_gather(links, copies, gains, f_g),
-        dp_gather(links, copies, q_up, f_q),
-        dp_gather(links, copies, kv_up, f_kv),
-        pack_stream(w_gate, w_up, w_down_t, packed),
-        later(itertools.islice(o_stream, 1), 1),
-    )
+    downs = EveryGather(links, copies, down, f_down, down.shape[1])
+    small_gathers = [
+        DpGather(links, copies, source, target)
+        for source, target in ((gains, f_g), (q_up, f_q), (kv_up, f_kv))
+    ]
+    o = DpGather(links, copies, o_t, f_o)
+    cots = EveryGather(links, copies, cot, f_cot)
+    downs.start()
+    for work in small_gathers:
+        work.start()
+    n_high = links.n_high
+    downs.first(0)
+    for work in small_gathers:
+        work.own_low()
+    for i in range(1, n_high):
+        downs.first(i)
+        downs.second(i - 1)
+    for i in range(n_high - 1):
+        for work in small_gathers:
+            work.step(i)
+    o.start()
+    o.own_low()
+    downs.second(n_high - 1)
+    for _ in pack_stream(w_gate, w_up, w_down_t, packed):
+        pass
+    swap = Swap(links, copies, packed, f_w)
+    for i in range(n_high):
+        downs.third(i)
+    for i in range(n_high):
+        downs.fourth(i)
+    small_gathers[0].finish()
 
     def gain_of(row, count):
         return jnp.concatenate(
             [f_g[k].astype(F32)[row : row + 1, :count] for k in range(n_dp)], axis=1
         )
 
-    swap = Swap(links, copies, packed, f_w)
-    swap.send(range(2, n_dp, 2))
-    next(o_stream)
     width = o_t.shape[0]
     full_down = f_down[...].reshape(n_dp * width, down.shape[1])
+    latent_rows(x, gain_of(0, width), full_down, normed, latents)
+    for work in small_gathers[1:]:
+        work.finish()
     full_q = f_q[...].reshape(n_dp * q_up.shape[0], q_up.shape[1])
     full_kv = f_kv[...].reshape(n_dp * kv_up.shape[0], kv_up.shape[1])
+    o.step(0)
     attend_rows(
-        x, gain_of(0, width), gain_of(1, q_up.shape[0]), gain_of(2, kv_up.shape[0]),
-        full_down, full_q, full_kv, attention_mask(seg_row, valid_row), cos_full, sin_full,
-        normed, latents, q_normed, kv_normed, q_rows, kv_rows, key_rot, mixed,
+        gain_of(1, q_up.shape[0]), gain_of(2, kv_up.shape[0]), full_q, full_kv,
+        attention_mask(seg_row, valid_row), cos_full, sin_full,
+        latents, q_normed, kv_normed, q_rows, kv_rows, key_rot, mixed,
     )
-    for _ in range(links.n_high - 1):
-        next(o_stream)
-    cots = EveryGather(links, copies, cot, f_cot, cot.shape[-1])
+    for i in range(1, n_high - 1):
+        o.step(i)
     cots.start()
     cots.first(0)
+    swap.send(range(2, n_dp, 2))
     swap.send(range(1, n_dp, 2))
-    take_turns(o_stream)
+    o.finish()
     full_o = f_o[...].reshape(n_dp * width, o_t.shape[1])
     attn_part = dot_nt(mixed[...], full_o).astype(BF)
     for side in range(2):
@@ -1034,7 +1163,6 @@
     normeds = EveryGather(links, copies, block, f_normed)
     normeds.start()
     normeds.first(0)
-    n_high = links.n_high
     for i in range(n_high + 2):
         if 1 <= i < n_high:
             cots.first(i)
@@ -1096,13 +1224,13 @@
     for i in range(1, n_high):
         normeds.first(i)
         if i == 1:
-            feed_forward_of(links.behind(normeds.order[0]))
+            feed_forward_of(normeds.line.source(0))
         normeds.second(i)
         normeds.third(i)
         if i > 1:
-            feed_forward_of(links.behind(normeds.order[i - 1]))
+            feed_forward_of(normeds.line.source(i - 1))
         normeds.fourth(i)
-    feed_forward_of(links.behind(normeds.order[n_high - 1]))
+    feed_forward_of(normeds.line.source(n_high - 1))
     swap.sent()
     all_tokens = n_dp * x.shape[0]
     for k in range(n_dp):
@@ -1134,7 +1262,7 @@
     wide = -(-2 * slice_ff // 128) * 128
     cut = 2 * slice_ff // 128 * 128
     heads = q_up.shape[1] // (NOPE + ROPE)
-    count = 3 * count_every_gather(n_high) + 4 * (2 * n_high - 1) + n_dp + 1
+    count = 3 * count_every_gather(n_high) + 4 * count_dp_gather(n_high) + n_dp + 1
     block = (rows, columns)
 
     def over(block, *lead, kind=BF):

time: 514 us -> 494 us (0.961)
  Pallas kernels: 500 us -> 480 us
    pallas_call x1, Pallas kernels: 260 us -> 240 us  [forward(): pl.pallas_call(functools.partial(forward_kernel, n_dp), out_shape=(over(d...]
where the time goes in v6:
time: 494 us; the launch traced here: 487 us
  Pallas kernels  480 us (97%)
    pallas_call x1, Pallas kernels, forward(): pl.pallas_call(functools.partial(forward_kernel, n_dp), out_shape=(over(d...  240 us
    pallas_call x1, Pallas kernels, back(): pl.pallas_call(functools.partial(back_kernel, n_dp), out_shape=(out((4, r...  231 us

profile of v6, /device:TPU:1, one launch (start us, length us, event | category | flops | bytes accessed | tf_op | source)
XLA Modules:
  0.0 486.9 jit_solution(16406917774882873815)
XLA Ops:
  0.7 1.2 broadcast_in_dim.22.gain_attn
  1.9 1.2 broadcast_in_dim.25.gain_mlp
  3.1 0.4 fusion.1
  3.5 0.8 pad_maximum_fusion.turns
  4.3 239.6 %forward.1 = (bf16[8,4,80,1152]{3,2,1,0:T(8,128)(2,1)}, bf16[8,320,640]{2,1,0:T(8,128)(2,1)}, bf16[8,96,960]{2,1,0:T(8,128)(2,1)}, bf16[8,32,1280]{2,1,0:T(8,128...) custom-call(bf16[192,2560]{1,0:T(8,128)(2,1)} %x.3, ...), custom_call_target="tpu_custom_call" | custom-call | tf_op jit(solution)/shard_map/forward/pallas_call | solution.py:1271
  243.9 230.8 %back.1 = (f32[4,48,2560]{2,1,0:T(8,128)}, f32[192,2560]{1,0:T(8,128)}, bf16[4,80,1152]{2,1,0:T(8,128)(2,1)}, f32[320,640]{1,0:T(8,128)}, f32[96,960]{1,0:T(8,12...) custom-call(bf16[4,2,2,2,48,2560]{5,4,3,2,1,0:T(8,128)(2,1)} %bitcast.18, ...), custom_call_target="tpu_custom_call" | custom-call | tf_op jit(solution)/shard_map/back/pallas_call | solution.py:1776
  474.7 9.4 %unpack.1 = (f32[320,1600]{1,0:T(8,128)}, f32[320,1600]{1,0:T(8,128)}, f32[320,1600]{1,0:T(8,128)}, f32[320,640]{1,0:T(8,128)}, f32[320,768]{1,0:T(8,128)}, /*in...) custom-call(bf16[8,320,640]{2,1,0:T(8,128)(2,1)} %get-tuple-element., ...), custom_call_target="tpu_custom_call" | custom-call | tf_op jit(solution)/shard_map/unpack/pallas_call | solution.py:1864
  484.1 1.3 reduce
  485.4 1.3 reduce.1
  (1 shorter events, 0.0 us)

commit v7 on v6

--- a/solution.py
+++ b/solution.py
@@ -1059,9 +1059,9 @@
 def forward_kernel(
     n_dp, x, cotangent, q_down, kv_down_t, gain_attn, gain_q, gain_kv, gain_mlp, q_up, kv_up, o_t,
     w_gate, w_up, w_down_t, seg_row, valid_row, turns,
-    f_down, f_o, f_q, f_kv, f_g, m_part, g_part, w_grads,
+    d_out, o_out, q_out, kv_out, f_g, m_part, g_part, w_grads,
     normed, latents, q_normed, kv_normed, q_rows, kv_rows, key_rot, mixed, resid, branch, cot,
-    down, gains, packed, f_w, f_cot, f_normed, hidden_all, both_all, m_block, g_block,
+    f_down, f_o, f_q, f_kv, down, gains, packed, f_w, f_cot, f_normed, hidden_all, both_all, m_block, g_block,
     part, from_core, out_side, from_side, block, send, recv, local,
 ):
     links = Links(n_dp)
@@ -1128,6 +1128,10 @@
         work.finish()
     full_q = f_q[...].reshape(n_dp * q_up.shape[0], q_up.shape[1])
     full_kv = f_kv[...].reshape(n_dp * kv_up.shape[0], kv_up.shape[1])
+    keeps = [
+        copies.near(source, target)
+        for source, target in ((f_down, d_out), (f_q, q_out), (f_kv, kv_out))
+    ]
     o.step(0)
     attend_rows(
         gain_of(1, q_up.shape[0]), gain_of(2, kv_up.shape[0]), full_q, full_kv,
@@ -1141,6 +1145,7 @@
     swap.send(range(2, n_dp, 2))
     swap.send(range(1, n_dp, 2))
     o.finish()
+    keeps.append(copies.near(f_o, o_out))
     full_o = f_o[...].reshape(n_dp * width, o_t.shape[1])
     attn_part = dot_nt(mixed[...], full_o).astype(BF)
     for side in range(2):
@@ -1247,6 +1252,8 @@
         stores.append(copies.near(packed.at[k], w_grads.at[k]))
     while stores:
         stores.pop().wait()
+    for keep in keeps:
+        keep.wait()
     copies.finish()
 
 
@@ -1292,8 +1299,12 @@
             over(block),
         ),
         in_specs=[VMEM] * 17,
-        out_specs=[VMEM] * 5 + [ANY] * 3 + [VMEM] * 11,
+        out_specs=[ANY] * 4 + [VMEM] + [ANY] * 3 + [VMEM] * 11,
         scratch_shapes=[
+            pltpu.VMEM((n_dp, 4, *down_shape), BF),
+            pltpu.VMEM((n_dp, *o_t.shape), BF),
+            pltpu.VMEM((n_dp, *q_up.shape), BF),
+            pltpu.VMEM((n_dp, *kv_up.shape), BF),
             pltpu.VMEM(down_shape, BF),
             pltpu.VMEM((16, gain_lanes), BF),
             pltpu.VMEM((n_dp, w_gate.shape[0], lanes), BF),
@@ -1309,7 +1320,7 @@
             pltpu.VMEM(block, BF),
             pltpu.VMEM(block, BF),
             pltpu.VMEM(block, BF),
-            *semaphores(count, 8 + 2 * n_high + n_dp),
+            *semaphores(count, 12 + 2 * n_high + n_dp),
         ],
         compiler_params=params(7, 62),
         name="forward",
@@ -1542,10 +1553,10 @@
 
 def back_kernel(
     n_dp, g_part, m_part, w_part, resid, branch, cot, x, normed, latents, q_normed, kv_normed,
-    q_rows, kv_rows, key_rot, mixed, f_down, f_o, f_q, f_kv, f_g, seg_row, valid_row,
+    q_rows, kv_rows, key_rot, mixed, d_in, o_in, q_in, kv_in, f_g, seg_row, valid_row,
     turns,
     block_full, grad_input, d_full, o_sum, q_sum, kv_sum, small_full, w_full,
-    attn_full, grad_rows, g_rows, m_rows, grad_q, grad_kv, lat, lat_in, lat_half, lat_side,
+    f_down, f_o, f_q, f_kv, attn_full, grad_rows, g_rows, m_rows, grad_q, grad_kv, lat, lat_in, lat_half, lat_side,
     lat_full, d_block, small, small_in, stats, stats_in, stats_block, small_block, *rest,
 ):
     g_bufs, m_bufs = rest[:8], (rest[0], *rest[8:13])
@@ -1569,6 +1580,10 @@
     swap = Swap(links, copies, w_part, w_full)
     high = range(links.n_high)
     g.start()
+    loads = [
+        copies.near(source, target)
+        for source, target in ((d_in, f_down), (o_in, f_o), (q_in, f_q), (kv_in, f_kv))
+    ]
     swap.send(range(2, n_dp, 2))
     for i in range(links.n_high + 1):
         if i in high:
@@ -1598,6 +1613,8 @@
     for _ in t_stream:
         pass
 
+    for load in loads:
+        load.wait()
     grad_attn = attn_full[...].reshape(length, x.shape[1])
     for k in range(n_dp):
         o_bufs[0][k // 2, k % 2] = dot_tn(
@@ -1785,9 +1802,10 @@
             out((4, 2, *one)),
             out(w_part.shape, BF),
         ),
-        in_specs=[ANY] * 3 + [VMEM] * 4 + [ANY] + [VMEM] * 15,
+        in_specs=[ANY] * 3 + [VMEM] * 4 + [ANY] + [VMEM] * 7 + [ANY] * 4 + [VMEM] * 4,
         out_specs=[ANY] + [VMEM] * 6 + [ANY],
         scratch_shapes=[
+            *(pltpu.VMEM(full.shape, BF) for full in (f_down, f_o, f_q, f_kv)),
             pltpu.VMEM((4, rows, columns), BF),
             pltpu.VMEM((rows, columns), BF),
             pltpu.VMEM((rows, columns), F32),
@@ -1812,7 +1830,7 @@
             *scatter_into_scratch(n_high, o_shape),
             *scatter_into_scratch(n_high, q_shape),
             *scatter_into_scratch(n_high, kv_shape),
-            *semaphores(count, 2 * n_high + 6),
+            *semaphores(count, 2 * n_high + 10),
         ],
         compiler_params=params(8, 62),
         name="back",

time: 494 us -> 487 us (0.986)
  Pallas kernels: 480 us -> 473 us
where the time goes in v7:
time: 487 us; the launch traced here: 480 us
  Pallas kernels  473 us (97%)
    pallas_call x1, Pallas kernels, forward(): pl.pallas_call(functools.partial(forward_kernel, n_dp), out_shape=(over(d...  236 us
    pallas_call x1, Pallas kernels, back(): pl.pallas_call(functools.partial(back_kernel, n_dp), out_shape=(out((4, r...  227 us

profile of v7, /device:TPU:1, one launch (start us, length us, event | category | flops | bytes accessed | tf_op | source)
XLA Modules:
  0.0 480.2 jit_solution(5734642577237871676)
XLA Ops:
  0.7 1.2 broadcast_in_dim.22.gain_attn
  1.9 1.2 broadcast_in_dim.25.gain_mlp
  3.1 0.4 fusion.1
  3.5 0.8 pad_maximum_fusion.turns
  4.3 236.2 %forward.1 = (bf16[8,4,80,1152]{3,2,1,0:T(8,128)(2,1)}, bf16[8,320,640]{2,1,0:T(8,128)(2,1)}, bf16[8,96,960]{2,1,0:T(8,128)(2,1)}, bf16[8,32,1280]{2,1,0:T(8,128...) custom-call(bf16[192,2560]{1,0:T(8,128)(2,1)} %x.3, ...), custom_call_target="tpu_custom_call" | custom-call | tf_op jit(solution)/shard_map/forward/pallas_call | solution.py:1278
  240.6 227.4 %back.1 = (f32[4,48,2560]{2,1,0:T(8,128)}, f32[192,2560]{1,0:T(8,128)}, bf16[4,80,1152]{2,1,0:T(8,128)(2,1)}, f32[320,640]{1,0:T(8,128)}, f32[96,960]{1,0:T(8,12...) custom-call(bf16[4,2,2,2,48,2560]{5,4,3,2,1,0:T(8,128)(2,1)} %bitcast.18, ...), custom_call_target="tpu_custom_call" | custom-call | tf_op jit(solution)/shard_map/back/pallas_call | solution.py:1793
  468.0 9.4 %unpack.1 = (f32[320,1600]{1,0:T(8,128)}, f32[320,1600]{1,0:T(8,128)}, f32[320,1600]{1,0:T(8,128)}, f32[320,640]{1,0:T(8,128)}, f32[320,768]{1,0:T(8,128)}, /*in...) custom-call(bf16[8,320,640]{2,1,0:T(8,128)(2,1)} %get-tuple-element., ...), custom_call_target="tpu_custom_call" | custom-call | tf_op jit(solution)/shard_map/unpack/pallas_call | solution.py:1882
  477.4 1.3 reduce
  478.7 1.3 reduce.1
  (1 shorter events, 0.0 us)

commit v8 on v7

--- a/solution.py
+++ b/solution.py
@@ -1084,7 +1084,7 @@
     own_rows = pl.ds(pl.multiple_of(rank * rows, 16), rows)
     cot[...] = cotangent[own_rows, :]
     links.meet(swap=True)
-    downs = EveryGather(links, copies, down, f_down, down.shape[1])
+    downs = EveryGather(links, copies, down, f_down)
     small_gathers = [
         DpGather(links, copies, source, target)
         for source, target in ((gains, f_g), (q_up, f_q), (kv_up, f_kv))

time: 487 us -> 518 us (1.064)
  Pallas kernels: 473 us -> 504 us
    pallas_call x1, Pallas kernels: 236 us -> 267 us  [forward(): pl.pallas_call(functools.partial(forward_kernel, n_dp), out_shape=(over(d...]
where the time goes in v8:
time: 518 us; the launch traced here: 511 us
  Pallas kernels  504 us (97%)
    pallas_call x1, Pallas kernels, forward(): pl.pallas_call(functools.partial(forward_kernel, n_dp), out_shape=(over(d...  267 us
    pallas_call x1, Pallas kernels, back(): pl.pallas_call(functools.partial(back_kernel, n_dp), out_shape=(out((4, r...  227 us

profile of v8, /device:TPU:1, one launch (start us, length us, event | category | flops | bytes accessed | tf_op | source)
XLA Modules:
  0.0 510.8 jit_solution(18399170796194776402)
XLA Ops:
  0.7 1.2 broadcast_in_dim.22.gain_attn
  1.9 1.2 broadcast_in_dim.25.gain_mlp
  3.1 0.4 fusion.1
  3.5 0.8 pad_maximum_fusion.turns
  4.3 266.9 %forward.1 = (bf16[8,4,80,1152]{3,2,1,0:T(8,128)(2,1)}, bf16[8,320,640]{2,1,0:T(8,128)(2,1)}, bf16[8,96,960]{2,1,0:T(8,128)(2,1)}, bf16[8,32,1280]{2,1,0:T(8,128...) custom-call(bf16[192,2560]{1,0:T(8,128)(2,1)} %x.3, ...), custom_call_target="tpu_custom_call" | custom-call | tf_op jit(solution)/shard_map/forward/pallas_call | solution.py:1278
  271.3 227.4 %back.1 = (f32[4,48,2560]{2,1,0:T(8,128)}, f32[192,2560]{1,0:T(8,128)}, bf16[4,80,1152]{2,1,0:T(8,128)(2,1)}, f32[320,640]{1,0:T(8,128)}, f32[96,960]{1,0:T(8,12...) custom-call(bf16[4,2,2,2,48,2560]{5,4,3,2,1,0:T(8,128)(2,1)} %bitcast.18, ...), custom_call_target="tpu_custom_call" | custom-call | tf_op jit(solution)/shard_map/back/pallas_call | solution.py:1793
  498.7 9.4 %unpack.1 = (f32[320,1600]{1,0:T(8,128)}, f32[320,1600]{1,0:T(8,128)}, f32[320,1600]{1,0:T(8,128)}, f32[320,640]{1,0:T(8,128)}, f32[320,768]{1,0:T(8,128)}, /*in...) custom-call(bf16[8,320,640]{2,1,0:T(8,128)(2,1)} %get-tuple-element., ...), custom_call_target="tpu_custom_call" | custom-call | tf_op jit(solution)/shard_map/unpack/pallas_call | solution.py:1882
  508.1 1.3 reduce
  509.4 1.3 reduce.1
  (1 shorter events, 0.0 us)
